TPU v7x, 128 devices: a whole 4x4x4 slice. The times are simulated.
128 devices in a mesh: lat: 32 (over x, z, core), lon: 4 (over y).
Axes of the slice: x: 4, y: 4, z: 4, core: 2. Of those that a mesh axis runs over, the one named last changes fastest.
Arguments:
- spectra: bfloat16 [131072, 8448], P(('lat', 'lon')), may hold values from -6 to 6
- pc_basis: bfloat16 [8448, 256], replicated, may hold values from -0.0625 to 0.0625
- destination: int32 [131072, 1], P(('lat', 'lon')), may hold values from 0 to 127; in each aligned block of 1024 rows (0 to 1023, 1024 to 2047, ...) at most 16 rows name the same one
- corner_row: int32 [131072], P(('lat', 'lon')), may hold values from 0 to 64
- corner_col: int32 [131072], P(('lat', 'lon')), may hold values from 0 to 64
- corner_weight: bfloat16 [131072, 4], P(('lat', 'lon')), may hold values from 0 to 1
- state: bfloat16 [2048, 256, 128], P('lat', 'lon'), may hold values from -6 to 6
- inv_sigma: float32 [256], replicated, may hold values from 0.5 to 2
- w_in: bfloat16 [128, 512], replicated, may hold values from -0.5 to 0.5
- b_in: float32 [512], replicated, may hold values from -3 to 3
- w_out: bfloat16 [512, 256], replicated, may hold values from -0.25 to 0.25
- b_out: float32 [256], replicated, may hold values from -3 to 3
Outputs:
- departures: bfloat16 [131072, 256], P(('lat', 'lon'))
- state_gradient: float32 [2048, 256, 128], P('lat', 'lon')
Inputs may be any that keep to these rules, and one draw needn't show every extreme that they name: `destination`: in the rows of one device no tile is named by more than 16 spectra, a bound that some block reaches.
All inputs are finite; a program needn't handle non-finite values.
Results may differ from a plain program's by a relative error of at most 0.0075.
Values may be sent and summed in bfloat16 or wider, within the bound.
No kernel may reach another device: no remote copies, remote signals or barrier semaphores. Data moves between devices by JAX's collectives and lax.ppermute only.
A program may use at most 128 MiB of HBM per device.

v0:
```python
import jax
import jax.numpy as jnp
from jax import lax
from jax.experimental import pallas as pl
from jax.experimental.pallas import tpu as pltpu
from jax.sharding import PartitionSpec as P

CAP = 16
F32 = jnp.float32
BF16 = jnp.bfloat16
I32 = jnp.int32
NT = (((1,), (1,)), ((), ()))
AXES = ("lat", "lon")


def iota(shape, dim):
    return lax.broadcasted_iota(I32, shape, dim)


def mm(a, b):
    return jnp.dot(a, b, preferred_element_type=F32)


def ones_where(mask):
    return jnp.where(mask, 1.0, 0.0).astype(BF16)


def call(body, out_shape, name, *args, scratch=()):
    return pl.pallas_call(body, out_shape=out_shape, scratch_shapes=scratch, name=name)(*args)


def route_body(dest_ref, row_ref, col_ref, weight_ref, state_ref, send_ref, place_ref, first_ref, last_ref):
    first_ref[...] = state_ref[:, 0, :]
    last_ref[...] = state_ref[:, 63, :]
    dest = dest_ref[...]
    tiles = send_ref.shape[0]
    obs = dest.shape[1]
    onehot = jnp.where(iota((tiles, obs), 0) == dest, 1.0, 0.0)
    before = ones_where(iota((obs, obs), 0) < iota((obs, obs), 1))
    rank = mm(onehot.astype(BF16), before)
    slot = jnp.sum(onehot * rank, axis=0, keepdims=True).astype(I32)
    place_ref[...] = dest * CAP + slot
    here = iota((CAP, obs), 0) == slot
    weights = weight_ref[...].astype(F32)
    fields = [weights[k : k + 1] for k in range(4)]
    fields += [row_ref[...].astype(F32), col_ref[...].astype(F32)]
    parts = [jnp.where(here, field, 0.0) for field in fields]
    parts.append(jnp.zeros((128 - CAP * len(parts), obs), F32))
    table = jnp.concatenate(parts, 0).astype(BF16)
    send_ref[...] = lax.dot_general(onehot.astype(BF16), table, NT, preferred_element_type=F32)


def fields_by_row(recv, first, count):
    tiles = recv.shape[0]
    pick = ones_where((iota((count, tiles), 0) + first) // CAP == iota((count, tiles), 1))
    mine = mm(pick, recv)
    mine = jnp.where(iota((count, 128), 0) % CAP == iota((count, 128), 1) % CAP, mine, 0.0)
    spread = ones_where(iota((128, 768), 0) // CAP == iota((128, 768), 1) // 128)
    out = mm(mine.astype(BF16), spread)
    return [out[:, 128 * k : 128 * k + 128] for k in range(6)]


def fields_by_lane(recv, slots):
    tiles = recv.shape[0]
    pick = ones_where(iota((tiles, slots), 1) // CAP == iota((tiles, slots), 0))
    mine = mm(recv.astype(F32).T.astype(BF16), pick)
    mine = jnp.where(iota((128, slots), 1) % CAP == iota((128, slots), 0) % CAP, mine, 0.0)
    gather = ones_where(iota((8, 128), 1) // CAP == iota((8, 128), 0))
    out = mm(gather, mine.astype(BF16))
    return [out[k : k + 1] for k in range(6)]


def pair_of(hit0, value0, hit1, value1):
    return jnp.where(hit0, value0, jnp.where(hit1, value1, jnp.zeros((), value0.dtype)))


def gather_body(recv_ref, own_ref, top_ref, bottom_ref, left_ref, right_ref, out_ref, matrix_ref, rim_ref):
    slots = out_ref.shape[0]
    chunk = matrix_ref.shape[0]
    rim_ref[0:64, :] = top_ref[0:64, :]
    rim_ref[64:128, :] = bottom_ref[0:64, :]
    rim_ref[128:192, :] = left_ref[...]
    rim_ref[192:256, :] = right_ref[...]
    rim_ref[256:272, :] = top_ref[64:80, :]
    rim_ref[272:288, :] = bottom_ref[64:80, :]
    rim_ref[288:384, :] = jnp.zeros((96, rim_ref.shape[1]), BF16)
    recv = recv_ref[...].astype(BF16)
    shape = (chunk, 128)
    lane = iota(shape, 1).astype(F32)
    high = lane >= 64.0
    upper = jnp.where(high, 1.0, 0.0)
    in_row = lane - 64.0 * upper

    def step(i, carry):
        first = i * chunk
        w0, w1, w2, w3, row, col = fields_by_row(recv, first, chunk)
        at0, at1 = in_row == col - 1.0, in_row == col
        p0 = pair_of(at0, w0, at1, w2)
        p1 = pair_of(at0, w1, at1, w3)
        edge = 65.0 * upper
        matrix_ref[:, 4096:4224] = pair_of(edge == row, p0, edge == row + 1.0, p1).astype(BF16)
        side = pair_of(in_row == row - 1.0, jnp.where(high, w2, w0), in_row == row, jnp.where(high, w3, w1))
        matrix_ref[:, 4224:4352] = jnp.where(col == 64.0 * upper, side, 0.0).astype(BF16)
        corner = pair_of(lane == 0.0, w0, lane == 16.0, w1) + pair_of(lane == 1.0, w2, lane == 17.0, w3)
        at_row = jnp.where(lane < 16.0, 0.0, 64.0)
        at_col = jnp.where((lane == 1.0) | (lane == 17.0), 64.0, 0.0)
        matrix_ref[:, 4352:4480] = jnp.where((row == at_row) & (col == at_col), corner, 0.0).astype(BF16)
        p0, p1, offset = p0.astype(BF16), p1.astype(BF16), (row - upper).astype(BF16)
        for j in range(32):
            matrix_ref[:, 128 * j : 128 * j + 128] = pair_of(offset == 2.0 * j + 1.0, p0, offset == 2.0 * j, p1)
        out = mm(matrix_ref[:, :4096], own_ref[...]) + mm(matrix_ref[:, 4096:], rim_ref[...])
        out_ref[pl.ds(pl.multiple_of(first, chunk), chunk), :] = out.astype(BF16)
        return carry

    lax.fori_loop(0, slots // chunk, step, 0)


def components_body(spectra_ref, basis_ref, place_ref, send_ref, pcs_ref, pick_ref):
    i = pl.program_id(0)
    rows = spectra_ref.shape[0]
    slots = send_ref.shape[0]
    at = pl.ds(pl.multiple_of(i * rows, rows), rows)
    pcs_ref[at, :] = mm(spectra_ref[...], basis_ref[...]).astype(BF16)
    pick_ref[:, at] = ones_where(iota((slots, rows), 0) == place_ref[...])

    @pl.when(i == pl.num_programs(0) - 1)
    def _():
        send_ref[...] = mm(pick_ref[...], pcs_ref[...]).astype(BF16)


def network_body(column_ref, pcs_ref, inv_ref, w_in_ref, b_in_ref, w_out_ref, b_out_ref, dep_ref, g_ref):
    pre = mm(column_ref[...], w_in_ref[...]) + b_in_ref[...]
    sig = jax.nn.sigmoid(pre)
    hidden = (pre * sig).astype(BF16)
    sim = mm(hidden, w_out_ref[...]) + b_out_ref[...]
    inv = inv_ref[...]
    dep = (sim - pcs_ref[...].astype(F32)) * inv
    dep_ref[...] = dep.astype(BF16)
    g_sim = (dep * inv).astype(BF16)
    g_hidden = lax.dot_general(g_sim, w_out_ref[...], NT, preferred_element_type=F32)
    g_pre = (g_hidden * sig * (1.0 + pre * (1.0 - sig))).astype(BF16)
    g_ref[...] = lax.dot_general(g_pre, w_in_ref[...], NT, preferred_element_type=F32).astype(BF16)


def unpack_body(back_ref, place_ref, out_ref, pick_ref):
    slots = back_ref.shape[0]
    obs = out_ref.shape[0]
    rows = jnp.broadcast_to(place_ref[...].astype(F32), (128, obs)).T
    lane = iota((obs, 128), 1).astype(F32)
    for b in range(slots // 128):
        pick_ref[:, 128 * b : 128 * b + 128] = ones_where(rows - 128.0 * b == lane)
    out_ref[...] = mm(pick_ref[...], back_ref[...]).astype(BF16)


def scatter_rim_body(recv_ref, g_ref, up_ref, down_ref, left_ref, right_ref, matrix_ref):
    slots = g_ref.shape[0]
    w0, w1, w2, w3, row, col = fields_by_lane(recv_ref[...].astype(BF16), slots)
    sub = iota((64, slots), 0).astype(F32)
    at0, at1 = sub == col - 1.0, sub == col
    matrix_ref[0:64, :] = jnp.where(row == 0.0, pair_of(at0, w0, at1, w2), 0.0).astype(BF16)
    matrix_ref[80:144, :] = jnp.where(row == 64.0, pair_of(at0, w1, at1, w3), 0.0).astype(BF16)
    at0, at1 = sub == row - 1.0, sub == row
    matrix_ref[160:224, :] = jnp.where(col == 0.0, pair_of(at0, w0, at1, w1), 0.0).astype(BF16)
    matrix_ref[224:288, :] = jnp.where(col == 64.0, pair_of(at0, w2, at1, w3), 0.0).astype(BF16)
    sub = iota((16, slots), 0).astype(F32)
    at0, at1 = (sub == 0.0) & (col == 0.0), (sub == 1.0) & (col == 64.0)
    matrix_ref[64:80, :] = jnp.where(row == 0.0, pair_of(at0, w0, at1, w2), 0.0).astype(BF16)
    matrix_ref[144:160, :] = jnp.where(row == 64.0, pair_of(at0, w1, at1, w3), 0.0).astype(BF16)
    out = mm(matrix_ref[...], g_ref[...])
    up_ref[...] = out[0:80].astype(BF16)
    down_ref[...] = out[80:160].astype(BF16)
    left_ref[...] = out[160:224]
    right_ref[...] = out[224:288]


def scatter_body(recv_ref, g_ref, out_ref, matrix_ref):
    slots = g_ref.shape[0]
    rows = matrix_ref.shape[0] // 64
    w0, w1, w2, w3, row, col = fields_by_lane(recv_ref[...].astype(BF16), slots)
    sub = iota((64, slots), 0).astype(F32)
    at0, at1 = sub == col - 1.0, sub == col
    p0 = pair_of(at0, w0, at1, w2).astype(BF16)
    p1 = pair_of(at0, w1, at1, w3).astype(BF16)
    row = jnp.broadcast_to(row, (64, slots)).astype(BF16)

    def step(i, carry):
        base = (i * rows).astype(F32)
        for j in range(rows):
            at = base + j
            matrix_ref[64 * j : 64 * j + 64, :] = pair_of(row == (at + 1.0).astype(BF16), p0, row == at.astype(BF16), p1)
        out = mm(matrix_ref[...], g_ref[...])
        out_ref[pl.ds(i * rows, rows)] = out.reshape(rows, 64, out.shape[1])
        return carry

    lax.fori_loop(0, 64 // rows, step, 0)


def shift(x, axis, step, closed):
    count = lax.axis_size(axis)
    pairs = [(i, (i + step) % count) for i in range(count) if closed or 0 <= i + step < count]
    return lax.ppermute(x, axis, pairs)


def exchange(x):
    return lax.all_to_all(x, AXES, split_axis=0, concat_axis=0, tiled=True)


def per_device(
    spectra,
    pc_basis,
    destination,
    corner_row,
    corner_col,
    corner_weight,
    state,
    inv_sigma,
    w_in,
    b_in,
    w_out,
    b_out,
):
    tiles = lax.axis_size("lat") * lax.axis_size("lon")
    obs = spectra.shape[0]
    npc = pc_basis.shape[1]
    levels = state.shape[2]
    slots = tiles * CAP
    sds = jax.ShapeDtypeStruct

    send_meta, place, first, last = call(
        route_body,
        (sds((tiles, 128), F32), sds((1, obs), I32), sds((64, levels), BF16), sds((64, levels), BF16)),
        "route",
        destination.reshape(1, obs),
        corner_row.reshape(1, obs),
        corner_col.reshape(1, obs),
        corner_weight.T,
        state,
    )
    recv_meta = exchange(send_meta)

    left = shift(last, "lon", 1, True)
    right = shift(first, "lon", -1, True)
    fill = jnp.zeros((14, levels), BF16)
    top = shift(jnp.concatenate([state[63], left[63:], right[63:], fill], 0), "lat", 1, False)
    bottom = shift(jnp.concatenate([state[0], left[:1], right[:1], fill], 0), "lat", -1, False)

    rows = obs // 4
    send_pcs = pl.pallas_call(
        components_body,
        grid=(obs // rows,),
        in_specs=[
            pl.BlockSpec((rows, spectra.shape[1]), lambda i: (i, 0)),
            pl.BlockSpec(pc_basis.shape, lambda i: (0, 0)),
            pl.BlockSpec((1, rows), lambda i: (0, i)),
        ],
        out_specs=pl.BlockSpec((slots, npc), lambda i: (0, 0)),
        out_shape=sds((slots, npc), BF16),
        scratch_shapes=[pltpu.VMEM((obs, npc), BF16), pltpu.VMEM((slots, obs), BF16)],
        name="components",
    )(spectra, pc_basis, place)
    recv_pcs = exchange(send_pcs.reshape(tiles, CAP, npc)).reshape(slots, npc)

    columns = call(
        gather_body,
        sds((slots, levels), BF16),
        "interpolate",
        recv_meta,
        state.reshape(-1, levels),
        top,
        bottom,
        left,
        right,
        scratch=[pltpu.VMEM((512, 4480), BF16), pltpu.VMEM((384, levels), BF16)],
    )

    def whole(x):
        return pl.BlockSpec(x.shape, lambda i: (0,) * x.ndim)

    block = slots // 4
    constants = (inv_sigma[None], w_in, b_in[None], w_out, b_out[None])
    dep, g = pl.pallas_call(
        network_body,
        grid=(slots // block,),
        in_specs=[
            pl.BlockSpec((block, levels), lambda i: (i, 0)),
            pl.BlockSpec((block, npc), lambda i: (i, 0)),
            *map(whole, constants),
        ],
        out_specs=[
            pl.BlockSpec((block, npc), lambda i: (i, 0)),
            pl.BlockSpec((block, levels), lambda i: (i, 0)),
        ],
        out_shape=(sds((slots, npc), BF16), sds((slots, levels), BF16)),
        name="network",
    )(columns, recv_pcs, *constants)
    back = exchange(dep.reshape(tiles, CAP, npc)).reshape(slots, npc)

    up, down, g_left, g_right = call(
        scatter_rim_body,
        (sds((80, levels), BF16), sds((80, levels), BF16), sds((64, levels), F32), sds((64, levels), F32)),
        "adjoint_rim",
        recv_meta,
        g,
        scratch=[pltpu.VMEM((288, slots), BF16)],
    )
    from_below = shift(up, "lat", -1, False)
    from_above = shift(down, "lat", 1, False)
    gradient = call(
        scatter_body,
        sds((64, 64, levels), F32),
        "adjoint",
        recv_meta,
        g,
        scratch=[pltpu.VMEM((512, slots), BF16)],
    )
    above, below = from_above[64:66].astype(F32), from_below[64:66].astype(F32)
    g_left = g_left.at[0].add(above[0]).at[63].add(below[0])
    g_right = g_right.at[0].add(above[1]).at[63].add(below[1])
    from_right = shift(g_left.astype(BF16), "lon", -1, True)
    from_left = shift(g_right.astype(BF16), "lon", 1, True)
    gradient = call(
        edge_body,
        sds((64, 64, levels), F32),
        "edges",
        gradient,
        from_left,
        from_right,
        from_above,
        from_below,
    )
    departures = call(
        unpack_body,
        sds((obs, npc), BF16),
        "unpack",
        back,
        place,
        scratch=[pltpu.VMEM((obs, slots), BF16)],
    )
    return (departures, gradient)


def edge_body(grad_ref, left_ref, right_ref, above_ref, below_ref, out_ref):
    out_ref[...] = grad_ref[...]
    out_ref[0] += above_ref[0:64, :].astype(F32)
    out_ref[63] += below_ref[0:64, :].astype(F32)
    out_ref[:, 0, :] += left_ref[...].astype(F32)
    out_ref[:, 63, :] += right_ref[...].astype(F32)


def solution(mesh):
    return jax.shard_map(
        per_device,
        mesh=mesh,
        in_specs=(
            P(AXES, None),
            P(),
            P(AXES, None),
            P(AXES),
            P(AXES),
            P(AXES, None),
            P("lat", "lon", None),
            P(),
            P(),
            P(),
            P(),
            P(),
        ),
        out_specs=(P(AXES, None), P("lat", "lon", None)),
        check_vma=False,
    )
```

profile of v0, /device:TPU:6, one launch (start us, length us, event | category | flops | bytes accessed | tf_op | source)
XLA Modules:
  0.0 132.9 jit_solution(11758813078407830639)
XLA Ops:
  0.6 2.6 %route.1 = (f32[128,128]{1,0:T(8,128)}, s32[1,1024]{1,0:T(1,128)}, bf16[64,128]{1,0:T(8,128)(2,1)}, bf16[64,128]{1,0:T(8,128)(2,1)}) custom-call(s32[1,1024]{1,0:T(1,128)} %bitcast.30, s32[1,1024]{1,0:T(1,128)} %bitcast.31, s32[1,1024]{1,0:T(1,128)} %bitcast.32, bf16[4,1024]{1,0:T(4,128)(2,1)} %bitcast.29, bf16[64,64,128]{2,1,0:T(8,128)(2,1)} %state_ref.1), custom_call_target="tpu_custom_call" | custom-call | tf_op jit(solution)/shard_map/route/pallas_call | solution.py:29
  3.2 10.5 %all-to-all-start = ((f32[128,1,128]{2,1,0:T(1,128)}), f32[128,1,128]{2,1,0:T(1,128)S(1)}, u32[]{:S(2)}, u32[]{:S(2)}) async-start(f32[128,1,128]{2,1,0:T(1,128)} %bitcast.28), calls=%async_computation | async-start | bytes 131072 | tf_op jit(solution)/shard_map/all_to_all | solution.py:205
  13.7 0.0 copy-start.12
  13.7 0.0 copy-start.11
  13.7 13.2 %components.1 = bf16[2048,256]{1,0:T(8,128)(2,1)} custom-call(bf16[1024,8448]{1,0:T(8,128)(2,1)} %spectra_ref.1, bf16[8448,256]{1,0:T(8,128)(2,1)} %basis_ref.1, s32[1,1024]{1,0:T(1,128)} %get-tuple-element.63.place_ref), custom_call_target="tpu_custom_call" | custom-call | tf_op jit(solution)/shard_map/components/pallas_call | solution.py:248
  26.9 0.0 all-to-all-done
  26.9 0.0 copy-start.2
  26.9 9.8 %all-to-all-start.1 = ((bf16[128,16,256]{2,1,0:T(8,128)(2,1)}), bf16[128,16,256]{2,1,0:T(8,128)(2,1)S(1)}, u32[]{:S(2)}, u32[]{:S(2)}) async-start(bf16[128,16,256]{2,1,0:T(8,128)(2,1)} %bitcast.21), calls=%async_computation.1 | async-start | bytes 2097152 | tf_op jit(solution)/shard_map/all_to_all | solution.py:205
  36.7 0.0 copy-done.12
  36.7 1.5 %collective-permute-start = (bf16[64,128]{1,0:T(8,128)(2,1)S(1)}, bf16[64,128]{1,0:T(8,128)(2,1)S(1)}, u32[]{:S(2)}, u32[]{:S(2)}) collective-permute-start(bf16[64,128]{1,0:T(8,128)(2,1)S(1)} %copy-done.12), channel_id=1, source_target_pairs={{0,1},{1,2},{2,3},{3,0},{4,5},{5,6},{6,7},{7,4},{8,9},{9,10},{10,1... | collective-permute-start | bytes 49160 | tf_op jit(solution)/shard_map/ppermute | solution.py:201
  38.3 0.0 copy-done.11
  38.3 1.8 %collective-permute-start.1 = (bf16[64,128]{1,0:T(8,128)(2,1)S(1)}, bf16[64,128]{1,0:T(8,128)(2,1)S(1)}, u32[]{:S(2)}, u32[]{:S(2)}) collective-permute-start(bf16[64,128]{1,0:T(8,128)(2,1)S(1)} %copy-done.11), channel_id=1, source_target_pairs={{0,3},{1,0},{2,1},{3,2},{4,7},{5,4},{6,5},{7,6},{8,11},{9,8},{10,9... | collective-permute-start | bytes 49160 | tf_op jit(solution)/shard_map/ppermute | solution.py:201
  40.0 0.7 slice_bitcast_fusion
  40.8 0.1 pad.15.clone
  40.8 10.1 %collective-permute-done.left_ref = bf16[64,128]{1,0:T(8,128)(2,1)S(1)} collective-permute-done((bf16[64,128]{1,0:T(8,128)(2,1)S(1)}, bf16[64,128]{1,0:T(8,128)(2,1)S(1)}, u32[]{:S(2)}, u32[]{:S(2)}) %collective-permute-start) | collective-permute-done | bytes 16416 | tf_op jit(solution)/shard_map/ppermute | solution.py:201
  51.0 0.0 copy-start.7
  51.0 0.0 collective-permute-done.1.right_ref
  51.0 0.0 copy-start.8
  51.0 0.1 maximum_maximum_fusion.1
  51.1 5.5 %collective-permute-start.3 = (bf16[80,128]{1,0:T(8,128)(2,1)S(1)}, bf16[80,128]{1,0:T(8,128)(2,1)S(1)}, u32[]{:S(2)}, u32[]{:S(2)}) collective-permute-start(bf16[80,128]{1,0:T(8,128)(2,1)S(1)} %get-tuple-element.80), channel_id=1, source_target_pairs={{4,0},{8,4},{12,8},{16,12},{20,16},{24,20},{28,24},{32,28},{36,32}... | collective-permute-start | bytes 61448 | tf_op jit(solution)/shard_map/ppermute | solution.py:201
  56.6 1.9 %collective-permute-start.2 = (bf16[80,128]{1,0:T(8,128)(2,1)S(1)}, bf16[80,128]{1,0:T(8,128)(2,1)S(1)}, u32[]{:S(2)}, u32[]{:S(2)}) collective-permute-start(bf16[80,128]{1,0:T(8,128)(2,1)S(1)} %get-tuple-element.81), channel_id=1, source_target_pairs={{0,4},{4,8},{8,12},{12,16},{16,20},{20,24},{24,28},{28,32},{32,36}... | collective-permute-start | bytes 61448 | tf_op jit(solution)/shard_map/ppermute | solution.py:201
  58.5 0.0 collective-permute-done.3.bottom_ref
  58.5 0.0 copy-start.3
  58.5 5.3 %collective-permute-done.2.top_ref = bf16[80,128]{1,0:T(8,128)(2,1)S(1)} collective-permute-done((bf16[80,128]{1,0:T(8,128)(2,1)S(1)}, bf16[80,128]{1,0:T(8,128)(2,1)S(1)}, u32[]{:S(2)}, u32[]{:S(2)}) %collective-permute-start.2) | collective-permute-done | bytes 20512 | tf_op jit(solution)/shard_map/ppermute | solution.py:201
  63.8 0.0 copy-start.4
  63.8 0.0 copy-done.2
  63.8 0.0 copy-done.7
  63.8 0.0 copy-done.8
  63.8 0.0 copy-done.3
  63.8 0.6 copy-done.4
  64.4 12.0 %interpolate.1.column_ref = bf16[2048,128]{1,0:T(8,128)(2,1)} custom-call(f32[128,128]{1,0:T(8,128)} %bitcast.25, bf16[4096,128]{1,0:T(8,128)(2,1)} %bitcast.20, bf16[80,128]{1,0:T(8,128)(2,1)} %copy-done.4, bf16[80,128]{1,0:T(8,128)(2,1)} %copy-done.3, bf16[64,128]{1,0:T(8,128)(2,1)} %copy-done.7, bf16[64,128]{1,0:T(8,128)(2,1)} %copy-done.8), custom_call_target="tpu_custom_call" | custom-call | tf_op jit(solution)/shard_map/interpolate/pallas_call | solution.py:29
  76.3 0.0 all-to-all-done.1
  76.3 0.0 copy-start.1
  76.3 1.0 copy-done.1
  77.3 5.5 %network.1 = (bf16[2048,256]{1,0:T(8,128)(2,1)}, bf16[2048,128]{1,0:T(8,128)(2,1)}) custom-call(bf16[2048,128]{1,0:T(8,128)(2,1)} %interpolate.1.column_ref, bf16[2048,256]{1,0:T(8,128)(2,1)} %bitcast.23, f32[1,256]{1,0:T(1,128)} %bitcast.34, bf16[128,512]{1,0:T(8,128)(2,1)} %w_in_ref.1, f32[1,512]{1,0:T(1,128)} %bitcast.33, bf16[512,256]{1,0:T(8,128)(2,1)} %w_out_ref.1, ...), custom_call_target="tpu_custom_call" | custom-call | tf_op jit(solution)/shard_map/network/pallas_call | solution.py:281
  82.8 4.8 %all-to-all-start.2 = ((bf16[128,16,256]{2,1,0:T(8,128)(2,1)}), bf16[128,16,256]{2,1,0:T(8,128)(2,1)S(1)}, u32[]{:S(2)}, u32[]{:S(2)}) async-start(bf16[128,16,256]{2,1,0:T(8,128)(2,1)} %bitcast.24), calls=%async_computation.2 | async-start | bytes 2097152 | tf_op jit(solution)/shard_map/all_to_all | solution.py:205
  87.6 2.6 %adjoint_rim.1 = (bf16[80,128]{1,0:T(8,128)(2,1)}, bf16[80,128]{1,0:T(8,128)(2,1)}, f32[64,128]{1,0:T(8,128)}, f32[64,128]{1,0:T(8,128)}) custom-call(f32[128,128]{1,0:T(8,128)} %bitcast.26, bf16[2048,128]{1,0:T(8,128)(2,1)} %get-tuple-element.65.g_ref), custom_call_target="tpu_custom_call" | custom-call | tf_op jit(solution)/shard_map/adjoint_rim/pallas_call | solution.py:29
  90.3 2.0 %collective-permute-start.4 = (bf16[80,128]{1,0:T(8,128)(2,1)}, bf16[80,128]{1,0:T(8,128)(2,1)S(1)}, u32[]{:S(2)}, u32[]{:S(2)}) collective-permute-start(bf16[80,128]{1,0:T(8,128)(2,1)} %get-tuple-element.67), channel_id=1, source_target_pairs={{0,4},{4,8},{8,12},{12,16},{16,20},{20,24},{24,28},{28,32},{32,36}... | collective-permute-start | bytes 61448 | tf_op jit(solution)/shard_map/ppermute | solution.py:201
  92.3 5.6 %collective-permute-start.5 = (bf16[80,128]{1,0:T(8,128)(2,1)}, bf16[80,128]{1,0:T(8,128)(2,1)S(1)}, u32[]{:S(2)}, u32[]{:S(2)}) collective-permute-start(bf16[80,128]{1,0:T(8,128)(2,1)} %get-tuple-element.68), channel_id=1, source_target_pairs={{4,0},{8,4},{12,8},{16,12},{20,16},{24,20},{28,24},{32,28},{36,32}... | collective-permute-start | bytes 61448 | tf_op jit(solution)/shard_map/ppermute | solution.py:201
  97.9 5.6 %collective-permute-done.4.above_ref = bf16[80,128]{1,0:T(8,128)(2,1)S(1)} collective-permute-done((bf16[80,128]{1,0:T(8,128)(2,1)}, bf16[80,128]{1,0:T(8,128)(2,1)S(1)}, u32[]{:S(2)}, u32[]{:S(2)}) %collective-permute-start.4) | collective-permute-done | bytes 20512 | tf_op jit(solution)/shard_map/ppermute | solution.py:201
  103.6 0.7 slice_add_fusion.2
  104.3 1.3 scatter-add.16
  105.6 1.3 scatter-add.14
  106.9 0.0 collective-permute-done.5.below_ref
  106.9 0.0 copy-start.6
  106.9 0.7 slice_add_fusion
  107.6 1.3 scatter-add.19
  108.9 0.8 convert_element_type.15
  109.7 1.3 scatter-add.15
  110.9 0.8 convert_element_type.14
  111.7 1.4 %collective-permute-start.6 = (bf16[64,128]{1,0:T(8,128)(2,1)S(1)}, bf16[64,128]{1,0:T(8,128)(2,1)S(1)}, u32[]{:S(2)}, u32[]{:S(2)}) collective-permute-start(bf16[64,128]{1,0:T(8,128)(2,1)S(1)} %convert_element_type.14), channel_id=1, source_target_pairs={{0,1},{1,2},{2,3},{3,0},{4,5},{5,6},{6,7},{7,4},{8,9},{9,10},{10,1... | collective-permute-start | bytes 49160 | tf_op jit(solution)/shard_map/ppermute | solution.py:201
  113.1 1.8 %collective-permute-start.7 = (bf16[64,128]{1,0:T(8,128)(2,1)S(1)}, bf16[64,128]{1,0:T(8,128)(2,1)S(1)}, u32[]{:S(2)}, u32[]{:S(2)}) collective-permute-start(bf16[64,128]{1,0:T(8,128)(2,1)S(1)} %convert_element_type.15), channel_id=1, source_target_pairs={{0,3},{1,0},{2,1},{3,2},{4,7},{5,4},{6,5},{7,6},{8,11},{9,8},{10,9... | collective-permute-start | bytes 49160 | tf_op jit(solution)/shard_map/ppermute | solution.py:201
  114.9 8.6 %adjoint.1.grad_ref = f32[64,64,128]{2,1,0:T(8,128)} custom-call(f32[128,128]{1,0:T(8,128)} %bitcast.27, bf16[2048,128]{1,0:T(8,128)(2,1)} %get-tuple-element.65.g_ref), custom_call_target="tpu_custom_call" | custom-call | tf_op jit(solution)/shard_map/adjoint/pallas_call | solution.py:29
  123.6 0.0 collective-permute-done.6.left_ref
  123.6 0.0 copy-start.9
  123.6 0.0 collective-permute-done.7.right_ref
  123.6 0.0 copy-done.5
  123.6 0.0 copy-done.6
  123.6 0.6 copy-done.9
  124.2 0.6 copy-done.10
  124.8 3.2 %edges.1 = f32[64,64,128]{2,1,0:T(8,128)} custom-call(f32[64,64,128]{2,1,0:T(8,128)} %adjoint.1.grad_ref, bf16[64,128]{1,0:T(8,128)(2,1)} %copy-done.9, bf16[64,128]{1,0:T(8,128)(2,1)} %copy-done.10, bf16[80,128]{1,0:T(8,128)(2,1)} %copy-done.5, bf16[80,128]{1,0:T(8,128)(2,1)} %copy-done.6), custom_call_target="tpu_custom_call" | custom-call | tf_op jit(solution)/shard_map/edges/pallas_call | solution.py:29
  128.0 0.0 all-to-all-done.2
  128.0 1.0 copy-done
  129.0 3.9 %unpack.1 = bf16[1024,256]{1,0:T(8,128)(2,1)} custom-call(bf16[2048,256]{1,0:T(8,128)(2,1)} %bitcast.22, s32[1,1024]{1,0:T(1,128)} %get-tuple-element.63.place_ref), custom_call_target="tpu_custom_call" | custom-call | tf_op jit(solution)/shard_map/unpack/pallas_call | solution.py:29
  (8 shorter events, 0.0 us)
Async XLA Ops:
  3.2 23.7 %all-to-all-start = ((f32[128,1,128]{2,1,0:T(1,128)}), f32[128,1,128]{2,1,0:T(1,128)S(1)}, u32[]{:S(2)}, u32[]{:S(2)}) async-start(f32[128,1,128]{2,1,0:T(1,128)} %bitcast.28), calls=%async_computation | async-start | bytes 131072 | tf_op jit(solution)/shard_map/all_to_all | solution.py:205
  13.7 23.0 %copy-start.12 = (bf16[64,128]{1,0:T(8,128)(2,1)S(1)}, bf16[64,128]{1,0:T(8,128)(2,1)}, u32[]{:S(2)}) copy-start(bf16[64,128]{1,0:T(8,128)(2,1)} %get-tuple-element.61) | copy-start | bytes 49156
  13.7 24.6 %copy-start.11 = (bf16[64,128]{1,0:T(8,128)(2,1)S(1)}, bf16[64,128]{1,0:T(8,128)(2,1)}, u32[]{:S(2)}) copy-start(bf16[64,128]{1,0:T(8,128)(2,1)} %get-tuple-element.62) | copy-start | bytes 49156
  26.9 36.9 %copy-start.2 = (f32[128,1,128]{2,1,0:T(1,128)}, f32[128,1,128]{2,1,0:T(1,128)S(1)}, u32[]{:S(2)}) copy-start(f32[128,1,128]{2,1,0:T(1,128)S(1)} %all-to-all-done) | copy-start | bytes 196612
  26.9 49.4 %all-to-all-start.1 = ((bf16[128,16,256]{2,1,0:T(8,128)(2,1)}), bf16[128,16,256]{2,1,0:T(8,128)(2,1)S(1)}, u32[]{:S(2)}, u32[]{:S(2)}) async-start(bf16[128,16,256]{2,1,0:T(8,128)(2,1)} %bitcast.21), calls=%async_computation.1 | async-start | bytes 2097152 | tf_op jit(solution)/shard_map/all_to_all | solution.py:205
  36.7 14.3 %collective-permute-start = (bf16[64,128]{1,0:T(8,128)(2,1)S(1)}, bf16[64,128]{1,0:T(8,128)(2,1)S(1)}, u32[]{:S(2)}, u32[]{:S(2)}) collective-permute-start(bf16[64,128]{1,0:T(8,128)(2,1)S(1)} %copy-done.12), channel_id=1, source_target_pairs={{0,1},{1,2},{2,3},{3,0},{4,5},{5,6},{6,7},{7,4},{8,9},{9,10},{10,1... | collective-permute-start | bytes 49160 | tf_op jit(solution)/shard_map/ppermute | solution.py:201
  38.3 12.7 %collective-permute-start.1 = (bf16[64,128]{1,0:T(8,128)(2,1)S(1)}, bf16[64,128]{1,0:T(8,128)(2,1)S(1)}, u32[]{:S(2)}, u32[]{:S(2)}) collective-permute-start(bf16[64,128]{1,0:T(8,128)(2,1)S(1)} %copy-done.11), channel_id=1, source_target_pairs={{0,3},{1,0},{2,1},{3,2},{4,7},{5,4},{6,5},{7,6},{8,11},{9,8},{10,9... | collective-permute-start | bytes 49160 | tf_op jit(solution)/shard_map/ppermute | solution.py:201
  51.0 12.8 %copy-start.7 = (bf16[64,128]{1,0:T(8,128)(2,1)}, bf16[64,128]{1,0:T(8,128)(2,1)S(1)}, u32[]{:S(2)}) copy-start(bf16[64,128]{1,0:T(8,128)(2,1)S(1)} %collective-permute-done.left_ref) | copy-start | bytes 49156
  51.0 12.8 %copy-start.8 = (bf16[64,128]{1,0:T(8,128)(2,1)}, bf16[64,128]{1,0:T(8,128)(2,1)S(1)}, u32[]{:S(2)}) copy-start(bf16[64,128]{1,0:T(8,128)(2,1)S(1)} %collective-permute-done.1.right_ref) | copy-start | bytes 49156
  51.1 7.4 %collective-permute-start.3 = (bf16[80,128]{1,0:T(8,128)(2,1)S(1)}, bf16[80,128]{1,0:T(8,128)(2,1)S(1)}, u32[]{:S(2)}, u32[]{:S(2)}) collective-permute-start(bf16[80,128]{1,0:T(8,128)(2,1)S(1)} %get-tuple-element.80), channel_id=1, source_target_pairs={{4,0},{8,4},{12,8},{16,12},{20,16},{24,20},{28,24},{32,28},{36,32}... | collective-permute-start | bytes 61448 | tf_op jit(solution)/shard_map/ppermute | solution.py:201
  56.6 7.2 %collective-permute-start.2 = (bf16[80,128]{1,0:T(8,128)(2,1)S(1)}, bf16[80,128]{1,0:T(8,128)(2,1)S(1)}, u32[]{:S(2)}, u32[]{:S(2)}) collective-permute-start(bf16[80,128]{1,0:T(8,128)(2,1)S(1)} %get-tuple-element.81), channel_id=1, source_target_pairs={{0,4},{4,8},{8,12},{12,16},{16,20},{20,24},{24,28},{28,32},{32,36}... | collective-permute-start | bytes 61448 | tf_op jit(solution)/shard_map/ppermute | solution.py:201
  58.5 5.3 %copy-start.3 = (bf16[80,128]{1,0:T(8,128)(2,1)}, bf16[80,128]{1,0:T(8,128)(2,1)S(1)}, u32[]{:S(2)}) copy-start(bf16[80,128]{1,0:T(8,128)(2,1)S(1)} %collective-permute-done.3.bottom_ref) | copy-start | bytes 61444
  63.8 0.6 copy-start.4
  76.3 1.0 copy-start.1
  82.8 45.2 %all-to-all-start.2 = ((bf16[128,16,256]{2,1,0:T(8,128)(2,1)}), bf16[128,16,256]{2,1,0:T(8,128)(2,1)S(1)}, u32[]{:S(2)}, u32[]{:S(2)}) async-start(bf16[128,16,256]{2,1,0:T(8,128)(2,1)} %bitcast.24), calls=%async_computation.2 | async-start | bytes 2097152 | tf_op jit(solution)/shard_map/all_to_all | solution.py:205
  90.3 13.3 %collective-permute-start.4 = (bf16[80,128]{1,0:T(8,128)(2,1)}, bf16[80,128]{1,0:T(8,128)(2,1)S(1)}, u32[]{:S(2)}, u32[]{:S(2)}) collective-permute-start(bf16[80,128]{1,0:T(8,128)(2,1)} %get-tuple-element.67), channel_id=1, source_target_pairs={{0,4},{4,8},{8,12},{12,16},{16,20},{20,24},{24,28},{28,32},{32,36}... | collective-permute-start | bytes 61448 | tf_op jit(solution)/shard_map/ppermute | solution.py:201
  92.3 14.6 %collective-permute-start.5 = (bf16[80,128]{1,0:T(8,128)(2,1)}, bf16[80,128]{1,0:T(8,128)(2,1)S(1)}, u32[]{:S(2)}, u32[]{:S(2)}) collective-permute-start(bf16[80,128]{1,0:T(8,128)(2,1)} %get-tuple-element.68), channel_id=1, source_target_pairs={{4,0},{8,4},{12,8},{16,12},{20,16},{24,20},{28,24},{32,28},{36,32}... | collective-permute-start | bytes 61448 | tf_op jit(solution)/shard_map/ppermute | solution.py:201
  103.6 20.0 %copy-start.5 = (bf16[80,128]{1,0:T(8,128)(2,1)}, bf16[80,128]{1,0:T(8,128)(2,1)S(1)}, u32[]{:S(2)}) copy-start(bf16[80,128]{1,0:T(8,128)(2,1)S(1)} %collective-permute-done.4.above_ref) | copy-start | bytes 61444
  106.9 16.7 %copy-start.6 = (bf16[80,128]{1,0:T(8,128)(2,1)}, bf16[80,128]{1,0:T(8,128)(2,1)S(1)}, u32[]{:S(2)}) copy-start(bf16[80,128]{1,0:T(8,128)(2,1)S(1)} %collective-permute-done.5.below_ref) | copy-start | bytes 61444
  111.7 11.9 %collective-permute-start.6 = (bf16[64,128]{1,0:T(8,128)(2,1)S(1)}, bf16[64,128]{1,0:T(8,128)(2,1)S(1)}, u32[]{:S(2)}, u32[]{:S(2)}) collective-permute-start(bf16[64,128]{1,0:T(8,128)(2,1)S(1)} %convert_element_type.14), channel_id=1, source_target_pairs={{0,1},{1,2},{2,3},{3,0},{4,5},{5,6},{6,7},{7,4},{8,9},{9,10},{10,1... | collective-permute-start | bytes 49160 | tf_op jit(solution)/shard_map/ppermute | solution.py:201
  113.1 10.4 %collective-permute-start.7 = (bf16[64,128]{1,0:T(8,128)(2,1)S(1)}, bf16[64,128]{1,0:T(8,128)(2,1)S(1)}, u32[]{:S(2)}, u32[]{:S(2)}) collective-permute-start(bf16[64,128]{1,0:T(8,128)(2,1)S(1)} %convert_element_type.15), channel_id=1, source_target_pairs={{0,3},{1,0},{2,1},{3,2},{4,7},{5,4},{6,5},{7,6},{8,11},{9,8},{10,9... | collective-permute-start | bytes 49160 | tf_op jit(solution)/shard_map/ppermute | solution.py:201
  123.6 0.6 copy-start.9
  124.2 0.6 copy-start.10
  128.0 1.0 copy-start
where the time goes:
time: 134 us; the launch traced here: 133 us
  Pallas kernels  51.6 us (39%)
  starting transfers between devices  46.6 us (35%)
  waiting for transfers between devices  21 us (16%)
  local copies, waits for them, and re-layouts  9.72 us (7%)
  other arithmetic  3.04 us (2%)
    pallas_call x6, Pallas kernels, call(): pl.pallas_call(body, out_shape=out_shape, scratch_shapes=scratch, name=name)  32.9 us
    all_to_all x3, starting transfers between devices, exchange(): return lax.all_to_all(x, AXES, split_axis=0, concat_axis=0, tiled=True)  25.1 us
    ppermute x8, starting transfers between devices, shift(): return lax.ppermute(x, axis, pairs)  21.6 us
    ppermute x8, waiting for transfers between devices, shift(): return lax.ppermute(x, axis, pairs)  21 us
    pallas_call x1, Pallas kernels, per_device(): pl.pallas_call(components_body, grid=(obs // rows,), in_specs=[pl.BlockSp...  13.2 us
    pallas_call x1, Pallas kernels, per_device(): pl.pallas_call(network_body, grid=(slots // block,), in_specs=[pl.BlockSp...  5.51 us
    unnamed x26, local copies, waits for them, and re-layouts  3.73 us
  transfers between devices with their start and end apart: 11, of which 3 were waited for; matrix products, arithmetic and copies ran while one was open for 7% of the time, Pallas kernels for 30%

commit v1 on v0

v1 whole, which is shorter than its diff:
```python
import jax
import jax.numpy as jnp
from jax import lax
from jax.experimental import pallas as pl
from jax.experimental.pallas import tpu as pltpu
from jax.sharding import PartitionSpec as P

CAP = 16
F32 = jnp.float32
BF16 = jnp.bfloat16
I32 = jnp.int32
NT = (((1,), (1,)), ((), ()))
AXES = ("lat", "lon")


def iota(shape, dim):
    return lax.broadcasted_iota(I32, shape, dim)


def mm(a, b):
    return jnp.dot(a, b, preferred_element_type=F32)


def ones_where(mask):
    return jnp.where(mask, 1.0, 0.0).astype(BF16)


def call(body, out_shape, name, *args, scratch=(), specs=None, outs=None, grant=8, alias=None):
    vmem = pl.BlockSpec(memory_space=pltpu.VMEM)
    return pl.pallas_call(
        body,
        in_specs=specs or [vmem] * len(args),
        out_specs=outs or jax.tree.map(lambda s: vmem, out_shape),
        out_shape=out_shape,
        scratch_shapes=scratch,
        input_output_aliases=alias or {},
        compiler_params=pltpu.CompilerParams(vmem_limit_bytes=grant << 20) if grant else None,
        name=name,
    )(*args)


def route_body(dest_ref, row_ref, col_ref, weight_ref, state_ref, send_ref, place_ref, first_ref, last_ref):
    first_ref[...] = state_ref[:, 0, :]
    last_ref[...] = state_ref[:, 63, :]
    dest = dest_ref[...]
    tiles = send_ref.shape[0]
    obs = dest.shape[1]
    onehot = jnp.where(iota((tiles, obs), 0) == dest, 1.0, 0.0)
    before = ones_where(iota((obs, obs), 0) < iota((obs, obs), 1))
    rank = mm(onehot.astype(BF16), before)
    slot = jnp.sum(onehot * rank, axis=0, keepdims=True).astype(I32)
    place_ref[...] = dest * CAP + slot
    here = iota((CAP, obs), 0) == slot
    weights = weight_ref[...].astype(F32)
    fields = [weights[k : k + 1] for k in range(4)]
    fields += [row_ref[...].astype(F32), col_ref[...].astype(F32)]
    parts = [jnp.where(here, field, 0.0) for field in fields]
    parts.append(jnp.zeros((128 - CAP * len(parts), obs), F32))
    table = jnp.concatenate(parts, 0).astype(BF16)
    send_ref[...] = lax.dot_general(onehot.astype(BF16), table, NT, preferred_element_type=F32)


def fields_by_row(recv, first, count):
    tiles = recv.shape[0]
    pick = ones_where((iota((count, tiles), 0) + first) // CAP == iota((count, tiles), 1))
    mine = mm(pick, recv)
    mine = jnp.where(iota((count, 128), 0) % CAP == iota((count, 128), 1) % CAP, mine, 0.0)
    spread = ones_where(iota((128, 768), 0) // CAP == iota((128, 768), 1) // 128)
    out = mm(mine.astype(BF16), spread)
    return [out[:, 128 * k : 128 * k + 128] for k in range(6)]


def fields_by_lane(recv, slots):
    tiles = recv.shape[0]
    pick = ones_where(iota((tiles, slots), 1) // CAP == iota((tiles, slots), 0))
    mine = mm(recv.astype(F32).T.astype(BF16), pick)
    mine = jnp.where(iota((128, slots), 1) % CAP == iota((128, slots), 0) % CAP, mine, 0.0)
    gather = ones_where(iota((8, 128), 1) // CAP == iota((8, 128), 0))
    out = mm(gather, mine.astype(BF16))
    return [out[k : k + 1] for k in range(6)]


def pair_of(hit0, value0, hit1, value1):
    return jnp.where(hit0, value0, jnp.where(hit1, value1, jnp.zeros((), value0.dtype)))


def gather_body(recv_ref, own_ref, top_ref, bottom_ref, left_ref, right_ref, out_ref, rim_ref, *matrices):
    slots = out_ref.shape[0]
    chunk = matrices[0].shape[0]
    rim_ref[0:64, :] = top_ref[...]
    rim_ref[64:128, :] = bottom_ref[...]
    rim_ref[128:192, :] = left_ref[0:64, :]
    rim_ref[192:256, :] = right_ref[0:64, :]
    rim_ref[256:272, :] = left_ref[64:80, :]
    rim_ref[272:288, :] = right_ref[64:80, :]
    rim_ref[288:384, :] = jnp.zeros((96, rim_ref.shape[1]), BF16)
    recv = recv_ref[...].astype(BF16)
    lane = iota((chunk, 128), 1).astype(F32)
    upper = jnp.where(lane >= 64.0, 1.0, 0.0)
    in_row = (lane - 64.0 * upper).astype(BF16)
    upper = upper.astype(BF16)
    lane = lane.astype(BF16)

    def build(first, matrix_ref):
        w0, w1, w2, w3, row, col = [f.astype(BF16) for f in fields_by_row(recv, first, chunk)]
        at0, at1 = in_row == col - 1.0, in_row == col
        p0 = pair_of(at0, w0, at1, w2)
        p1 = pair_of(at0, w1, at1, w3)
        zero = jnp.zeros((), BF16)
        edge = 65.0 * upper
        matrix_ref[:, 4096:4224] = pair_of(edge == row, p0, edge == row + 1.0, p1)
        high = upper > 0.5
        side = pair_of(in_row == row - 1.0, jnp.where(high, w2, w0), in_row == row, jnp.where(high, w3, w1))
        matrix_ref[:, 4224:4352] = jnp.where(col == 64.0 * upper, side, zero)
        corner = pair_of(lane == 0.0, w0, lane == 1.0, w1) + pair_of(lane == 16.0, w2, lane == 17.0, w3)
        at_col = jnp.where(lane < 16.0, zero, zero + 64.0)
        odd = jnp.where(lane < 16.0, lane, lane - 16.0)
        matrix_ref[:, 4352:4480] = jnp.where(row == 64.0 * odd, jnp.where(col == at_col, corner, zero), zero)
        offset = row - upper
        for j in range(32):
            matrix_ref[:, 128 * j : 128 * j + 128] = pair_of(offset == 2.0 * j + 1.0, p0, offset == 2.0 * j, p1)

    def use(first, matrix_ref):
        out = mm(matrix_ref[:, :4096], own_ref[...]) + mm(matrix_ref[:, 4096:], rim_ref[...])
        out_ref[first : first + chunk, :] = out.astype(BF16)

    count = slots // chunk
    build(0, matrices[0])
    for i in range(count):
        if i + 1 < count:
            build((i + 1) * chunk, matrices[i + 1])
        use(i * chunk, matrices[i])


def components_body(spectra_ref, basis_ref, place_ref, send_ref, back_ref, buffer, pcs_ref, pick_ref, back_buffer, part_ref, out_buffer, sems, back_sem, out_sems, basis_buffer, basis_sem):
    obs = spectra_ref.shape[0]
    slots = send_ref.shape[0]
    blocks = buffer.shape[0]
    rows = obs // blocks
    copies = [
        pltpu.make_async_copy(spectra_ref.at[pl.ds(i * rows, rows), :], buffer.at[i], sems.at[i]) for i in range(blocks)
    ]
    basis = pltpu.make_async_copy(basis_ref, basis_buffer, basis_sem)
    basis.start()
    for copy in copies:
        copy.start()
    place = place_ref[...]
    wide = jnp.broadcast_to(place.astype(F32), (128, obs)).T
    lane = iota((obs, 128), 1).astype(F32)
    for b in range(slots // 128):
        back_buffer[:, 128 * b : 128 * b + 128] = ones_where(wide - 128.0 * b == lane)
    save = pltpu.make_async_copy(back_buffer, back_ref, back_sem)
    save.start()
    for b in range(slots // 256):
        pick_ref[256 * b : 256 * b + 256, :] = ones_where(iota((256, obs), 0) + 256 * b == place)
    for i, copy in enumerate(copies):
        if i == blocks - 1:
            part_ref[...] = mm(pick_ref[:, : i * rows], pcs_ref[: i * rows, :])
        if i == 0:
            basis.wait()
        copy.wait()
        pcs_ref[i * rows : i * rows + rows, :] = mm(buffer[i], basis_buffer[...]).astype(BF16)
    last = obs - rows
    outs = []
    for i in range(4):
        at = slice(i * slots // 4, (i + 1) * slots // 4)
        out_buffer[at, :] = (part_ref[at, :] + mm(pick_ref[at, last:], pcs_ref[last:, :])).astype(BF16)
        outs.append(pltpu.make_async_copy(out_buffer.at[at, :], send_ref.at[at, :], out_sems.at[i]))
        outs[i].start()
    for copy in outs:
        copy.wait()
    save.wait()


def network_body(column_ref, pcs_ref, inv_ref, w_in_ref, b_in_ref, w_out_ref, b_out_ref, dep_ref, g_ref, buffer, sems):
    slots = column_ref.shape[0]
    block = slots // 4
    inv = inv_ref[...]
    copies = []
    for i in range(4):
        at = slice(i * block, (i + 1) * block)
        pre = mm(column_ref[at, :], w_in_ref[...]) + b_in_ref[...]
        sig = jax.nn.sigmoid(pre)
        hidden = (pre * sig).astype(BF16)
        sim = mm(hidden, w_out_ref[...]) + b_out_ref[...]
        dep = (sim - pcs_ref[at, :].astype(F32)) * inv
        buffer[at, :] = dep.astype(BF16)
        copies.append(pltpu.make_async_copy(buffer.at[at, :], dep_ref.at[at, :], sems.at[i]))
        copies[i].start()
        g_sim = (dep * inv).astype(BF16)
        g_hidden = lax.dot_general(g_sim, w_out_ref[...], NT, preferred_element_type=F32)
        g_pre = (g_hidden * sig * (1.0 + pre * (1.0 - sig))).astype(BF16)
        g_ref[at, :] = lax.dot_general(g_pre, w_in_ref[...], NT, preferred_element_type=F32).astype(BF16)
    for copy in copies:
        copy.wait()


def finish_body(back_ref, pick_ref, left_ref, right_ref, above_ref, below_ref, grad_ref, dep_ref, out_ref, picks, sides, rows, sems, in_sems, out_sems):
    edges = [
        (out_ref.at[:, pl.ds(0, 8), :], sides.at[0]),
        (out_ref.at[:, pl.ds(56, 8), :], sides.at[1]),
        (out_ref.at[0, pl.ds(8, 48), :], rows.at[0]),
        (out_ref.at[63, pl.ds(8, 48), :], rows.at[1]),
    ]
    loads = [pltpu.make_async_copy(a, b, in_sems.at[i]) for i, (a, b) in enumerate(edges)]
    stores = [pltpu.make_async_copy(b, a, out_sems.at[i]) for i, (a, b) in enumerate(edges)]
    for copy in loads:
        copy.start()
    obs = dep_ref.shape[0]
    block = obs // 4
    copies = [pltpu.make_async_copy(pick_ref.at[pl.ds(i * block, block), :], picks.at[i], sems.at[i]) for i in range(4)]
    for copy in copies:
        copy.start()
    for copy in loads:
        copy.wait()
    above, below = above_ref[...].astype(F32), below_ref[...].astype(F32)
    sides[0, :, 0, :] += left_ref[0:64, :].astype(F32)
    sides[1, :, 7, :] += right_ref[0:64, :].astype(F32)
    sides[0, 0] += above[0:8]
    sides[1, 0] += above[56:64]
    sides[0, 63] += below[0:8]
    sides[1, 63] += below[56:64]
    rows[0] += above[8:56]
    rows[1] += below[8:56]
    for copy in stores:
        copy.start()
    for i, copy in enumerate(copies):
        copy.wait()
        dep_ref[i * block : i * block + block, :] = mm(picks[i], back_ref[...]).astype(BF16)
    for copy in stores:
        copy.wait()


def scatter_rim_body(recv_ref, g_ref, up_ref, down_ref, left_ref, right_ref, matrix_ref):
    slots = g_ref.shape[0]
    w0, w1, w2, w3, row, col = fields_by_lane(recv_ref[...].astype(BF16), slots)
    sub = iota((64, slots), 0).astype(F32)
    at0, at1 = sub == col - 1.0, sub == col
    matrix_ref[0:64, :] = jnp.where(row == 0.0, pair_of(at0, w0, at1, w2), 0.0).astype(BF16)
    matrix_ref[64:128, :] = jnp.where(row == 64.0, pair_of(at0, w1, at1, w3), 0.0).astype(BF16)
    at0, at1 = sub == row - 1.0, sub == row
    matrix_ref[128:192, :] = jnp.where(col == 0.0, pair_of(at0, w0, at1, w1), 0.0).astype(BF16)
    matrix_ref[208:272, :] = jnp.where(col == 64.0, pair_of(at0, w2, at1, w3), 0.0).astype(BF16)
    sub = iota((16, slots), 0).astype(F32)
    at0, at1 = (sub == 0.0) & (row == 0.0), (sub == 1.0) & (row == 64.0)
    matrix_ref[192:208, :] = jnp.where(col == 0.0, pair_of(at0, w0, at1, w1), 0.0).astype(BF16)
    matrix_ref[272:288, :] = jnp.where(col == 64.0, pair_of(at0, w2, at1, w3), 0.0).astype(BF16)
    out = mm(matrix_ref[...], g_ref[...])
    up_ref[...] = out[0:64]
    down_ref[...] = out[64:128]
    left_ref[...] = out[128:208].astype(BF16)
    right_ref[...] = out[208:288].astype(BF16)


def corner_body(up_ref, down_ref, left_ref, right_ref, up_out, down_out):
    at = iota((64, 128), 0)
    left = left_ref[64:80, :].astype(F32)
    right = right_ref[64:80, :].astype(F32)
    for k, (ref, out) in enumerate(((up_ref, up_out), (down_ref, down_out))):
        extra = jnp.where(at == 0, left[k : k + 1], jnp.where(at == 63, right[k : k + 1], 0.0))
        out[...] = (ref[...] + extra).astype(BF16)


def scatter_body(recv_ref, g_ref, out_ref, buffer, sems, *matrices):
    slots = g_ref.shape[0]
    rows = matrices[0].shape[0] // 64
    w0, w1, w2, w3, row, col = [f.astype(BF16) for f in fields_by_lane(recv_ref[...].astype(BF16), slots)]
    sub = iota((64, slots), 0).astype(F32).astype(BF16)
    at0, at1 = sub == col - 1.0, sub == col
    p0 = pair_of(at0, w0, at1, w2)
    p1 = pair_of(at0, w1, at1, w3)
    row = jnp.broadcast_to(row, (64, slots))

    def build(base, matrix_ref):
        for j in range(rows):
            at = float(base + j)
            matrix_ref[64 * j : 64 * j + 64, :] = pair_of(row == at + 1.0, p0, row == at, p1)

    count = 64 // rows
    copies = []
    build(0, matrices[0])
    for i in range(count):
        if i + 1 < count:
            build((i + 1) * rows, matrices[i + 1])
        out = mm(matrices[i][...], g_ref[...])
        buffer[i * rows : i * rows + rows] = out.reshape(rows, 64, out.shape[1])
        at = pl.ds(i * rows, rows)
        copies.append(pltpu.make_async_copy(buffer.at[at], out_ref.at[at], sems.at[i]))
        copies[i].start()
    for copy in copies:
        copy.wait()


def in_hbm(x):
    return pltpu.with_memory_space_constraint(x, pltpu.HBM)


def shift(x, axis, step, closed):
    count = lax.axis_size(axis)
    pairs = [(i, (i + step) % count) for i in range(count) if closed or 0 <= i + step < count]
    return lax.ppermute(x, axis, pairs)


def exchange(x):
    return lax.all_to_all(x, AXES, split_axis=0, concat_axis=0, tiled=True)


def per_device(
    spectra,
    pc_basis,
    destination,
    corner_row,
    corner_col,
    corner_weight,
    state,
    inv_sigma,
    w_in,
    b_in,
    w_out,
    b_out,
):
    tiles = lax.axis_size("lat") * lax.axis_size("lon")
    obs = spectra.shape[0]
    npc = pc_basis.shape[1]
    levels = state.shape[2]
    slots = tiles * CAP
    sds = jax.ShapeDtypeStruct

    top = shift(state[63], "lat", 1, False)
    bottom = shift(state[0], "lat", -1, False)
    send_meta, place, first, last = call(
        route_body,
        (sds((tiles, 128), F32), sds((1, obs), I32), sds((64, levels), BF16), sds((64, levels), BF16)),
        "route",
        destination.reshape(1, obs),
        corner_row.reshape(1, obs),
        corner_col.reshape(1, obs),
        corner_weight.T,
        state,
        grant=None,
    )
    recv_meta = exchange(send_meta)

    fill = jnp.zeros((14, levels), BF16)
    left = shift(jnp.concatenate([last, top[63:], bottom[63:], fill], 0), "lon", 1, True)
    right = shift(jnp.concatenate([first, top[:1], bottom[:1], fill], 0), "lon", -1, True)

    vmem = pl.BlockSpec(memory_space=pltpu.VMEM)
    hbm = pl.BlockSpec(memory_space=pltpu.HBM)
    send_pcs, pick = call(
        components_body,
        (pltpu.HBM((slots, npc), BF16), pltpu.HBM((obs, slots), BF16)),
        "components",
        in_hbm(spectra),
        in_hbm(pc_basis),
        place,
        specs=[hbm, hbm, vmem],
        outs=(hbm, hbm),
        scratch=[
            pltpu.VMEM((4, obs // 4, spectra.shape[1]), BF16),
            pltpu.VMEM((obs, npc), BF16),
            pltpu.VMEM((slots, obs), BF16),
            pltpu.VMEM((obs, slots), BF16),
            pltpu.VMEM((slots, npc), F32),
            pltpu.VMEM((slots, npc), BF16),
            pltpu.SemaphoreType.DMA((4,)),
            pltpu.SemaphoreType.DMA,
            pltpu.SemaphoreType.DMA((4,)),
            pltpu.VMEM(pc_basis.shape, BF16),
            pltpu.SemaphoreType.DMA,
        ],
        grant=42,
    )
    send_pcs, top, bottom, left, right = lax.optimization_barrier((send_pcs, top, bottom, left, right))
    recv_pcs = exchange(send_pcs.reshape(tiles, CAP, npc)).reshape(slots, npc)

    columns = call(
        gather_body,
        sds((slots, levels), BF16),
        "interpolate",
        recv_meta,
        state.reshape(-1, levels),
        top,
        bottom,
        left,
        right,
        scratch=[pltpu.VMEM((384, levels), BF16)] + [pltpu.VMEM((slots // 4, 4480), BF16)] * 4,
        grant=26,
    )
    dep, g = call(
        network_body,
        (pltpu.HBM((slots, npc), BF16), sds((slots, levels), BF16)),
        "network",
        columns,
        recv_pcs,
        inv_sigma[None],
        w_in,
        b_in[None],
        w_out,
        b_out[None],
        outs=(hbm, vmem),
        scratch=[pltpu.VMEM((slots, npc), BF16), pltpu.SemaphoreType.DMA((4,))],
        grant=16,
    )
    up, down, g_left, g_right = call(
        scatter_rim_body,
        (sds((64, levels), F32), sds((64, levels), F32), sds((80, levels), BF16), sds((80, levels), BF16)),
        "adjoint_rim",
        recv_meta,
        g,
        scratch=[pltpu.VMEM((288, slots), BF16)],
        grant=16,
    )
    from_right = shift(g_left, "lon", -1, True)
    from_left = shift(g_right, "lon", 1, True)
    back = exchange(dep.reshape(tiles, CAP, npc)).reshape(slots, npc)
    up, down = call(
        corner_body,
        (sds((64, levels), BF16), sds((64, levels), BF16)),
        "corners",
        up,
        down,
        from_left,
        from_right,
    )
    from_below = shift(up, "lat", -1, False)
    from_above = shift(down, "lat", 1, False)
    gradient = call(
        scatter_body,
        pltpu.HBM((64, 64, levels), F32),
        "adjoint",
        recv_meta,
        g,
        outs=hbm,
        scratch=[pltpu.VMEM((64, 64, levels), F32), pltpu.SemaphoreType.DMA((4,))]
        + [pltpu.VMEM((1024, slots), BF16)] * 4,
        grant=28,
    )
    departures, gradient = call(
        finish_body,
        (sds((obs, npc), BF16), pltpu.HBM((64, 64, levels), F32)),
        "finish",
        back,
        in_hbm(pick),
        from_left,
        from_right,
        from_above,
        from_below,
        in_hbm(gradient),
        specs=[vmem, hbm, vmem, vmem, vmem, vmem, hbm],
        outs=(vmem, hbm),
        scratch=[
            pltpu.VMEM((4, obs // 4, slots), BF16),
            pltpu.VMEM((2, 64, 8, levels), F32),
            pltpu.VMEM((2, 48, levels), F32),
            pltpu.SemaphoreType.DMA((4,)),
            pltpu.SemaphoreType.DMA((4,)),
            pltpu.SemaphoreType.DMA((4,)),
        ],
        alias={6: 1},
    )
    return (departures, gradient)


def solution(mesh):
    return jax.shard_map(
        per_device,
        mesh=mesh,
        in_specs=(
            P(AXES, None),
            P(),
            P(AXES, None),
            P(AXES),
            P(AXES),
            P(AXES, None),
            P("lat", "lon", None),
            P(),
            P(),
            P(),
            P(),
            P(),
        ),
        out_specs=(P(AXES, None), P("lat", "lon", None)),
        check_vma=False,
    )
```

time: 134 us -> 116 us (0.87)
  Pallas kernels: 51.6 us -> 42.9 us
  local copies, waits for them, and re-layouts: 9.72 us -> 2.43 us
  other arithmetic: 3.04 us -> 0.82 us
    ppermute x8, waiting for transfers between devices: 21 us -> 10.1 us  [shift(): return lax.ppermute(x, axis, pairs)]
    all_to_all x3, waiting for transfers between devices: 0.01 us -> 10.5 us  [exchange(): return lax.all_to_all(x, AXES, split_axis=0, concat_axis=0, tiled=True)]
    pallas_call x8, Pallas kernels: 51.6 us -> 42.9 us  [call(): pl.pallas_call(body, in_specs=specs or [vmem] * len(args), out_specs=outs...]
    scatter-add x4 -> x0, local copies, waits for them, and re-layouts: 5.16 us -> none  [the longest x2 2.58 us: per_device(): g_left = g_left.at[0].add(above[0]).at[63].add(below[0])]
    unnamed x26 -> x14, local copies, waits for them, and re-layouts: 3.73 us -> 1.6 us
    convert_element_type x4 -> x0, other arithmetic: 1.53 us -> none  [the longest x1 0.76 us: per_device(): from_right = shift(g_left.astype(BF16), 'lon', -1, True)]
    add x2 -> x0, other arithmetic: 1.43 us -> none  [per_device(): g_left = g_left.at[0].add(above[0]).at[63].add(below[0])]
  transfers between devices with their start and end apart: 11 -> 11, of which waited for: 3 -> 2; matrix products, arithmetic and copies ran while one was open for 7% -> 1% of each run, Pallas kernels for 30% -> 30%
where the time goes in v1:
time: 116 us; the launch traced here: 115 us
  starting transfers between devices  47.1 us (41%)
  Pallas kernels  42.9 us (37%)
  waiting for transfers between devices  20.6 us (18%)
  local copies, waits for them, and re-layouts  2.43 us (2%)
    pallas_call x8, Pallas kernels, call(): pl.pallas_call(body, in_specs=specs or [vmem] * len(args), out_specs=outs...  42.9 us
    all_to_all x3, starting transfers between devices, exchange(): return lax.all_to_all(x, AXES, split_axis=0, concat_axis=0, tiled=True)  25.5 us
    ppermute x8, starting transfers between devices, shift(): return lax.ppermute(x, axis, pairs)  21.6 us
    all_to_all x3, waiting for transfers between devices, exchange(): return lax.all_to_all(x, AXES, split_axis=0, concat_axis=0, tiled=True)  10.5 us
    ppermute x8, waiting for transfers between devices, shift(): return lax.ppermute(x, axis, pairs)  10.1 us
  transfers between devices with their start and end apart: 11, of which 2 were waited for; matrix products, arithmetic and copies ran while one was open for 1% of the time, Pallas kernels for 30%

profile of v1, /device:TPU:6, one launch (start us, length us, event | category | flops | bytes accessed | tf_op | source)
XLA Modules:
  0.0 114.8 jit_solution(11221289130170564000)
XLA Ops:
  0.6 0.7 slice_bitcast_fusion
  1.4 5.6 %collective-permute-start.1 = (bf16[64,128]{1,0:T(8,128)(2,1)S(1)}, bf16[64,128]{1,0:T(8,128)(2,1)S(1)}, u32[]{:S(2)}, u32[]{:S(2)}) collective-permute-start(bf16[64,128]{1,0:T(8,128)(2,1)S(1)} %get-tuple-element.40), channel_id=1, source_target_pairs={{4,0},{8,4},{12,8},{16,12},{20,16},{24,20},{28,24},{32,28},{36,32}... | collective-permute-start | bytes 49160 | tf_op jit(solution)/shard_map/ppermute | solution.py:301
  7.0 1.9 %collective-permute-start = (bf16[64,128]{1,0:T(8,128)(2,1)S(1)}, bf16[64,128]{1,0:T(8,128)(2,1)S(1)}, u32[]{:S(2)}, u32[]{:S(2)}) collective-permute-start(bf16[64,128]{1,0:T(8,128)(2,1)S(1)} %get-tuple-element.41), channel_id=1, source_target_pairs={{0,4},{4,8},{8,12},{12,16},{16,20},{20,24},{24,28},{28,32},{32,36}... | collective-permute-start | bytes 49160 | tf_op jit(solution)/shard_map/ppermute | solution.py:301
  8.9 2.6 %route.1 = (f32[128,128]{1,0:T(8,128)}, s32[1,1024]{1,0:T(1,128)}, bf16[64,128]{1,0:T(8,128)(2,1)}, bf16[64,128]{1,0:T(8,128)(2,1)}) custom-call(s32[1,1024]{1,0:T(1,128)} %bitcast.33, s32[1,1024]{1,0:T(1,128)} %bitcast.34, s32[1,1024]{1,0:T(1,128)} %bitcast.35, bf16[4,1024]{1,0:T(4,128)(2,1)} %bitcast.32, bf16[64,64,128]{2,1,0:T(8,128)(2,1)} %state_ref.1), custom_call_target="tpu_custom_call" | custom-call | tf_op jit(solution)/shard_map/route/pallas_call | solution.py:30
  11.5 10.0 %all-to-all-start = ((f32[128,1,128]{2,1,0:T(1,128)}), f32[128,1,128]{2,1,0:T(1,128)S(1)}, u32[]{:S(2)}, u32[]{:S(2)}) async-start(f32[128,1,128]{2,1,0:T(1,128)} %bitcast.31), calls=%async_computation | async-start | bytes 131072 | tf_op jit(solution)/shard_map/all_to_all | solution.py:305
  21.5 0.1 pad.7.clone
  21.6 0.0 collective-permute-done.1.bottom_ref
  21.6 0.0 collective-permute-done.top_ref
  21.7 0.8 maximum_maximum_fusion.1
  22.5 2.8 %collective-permute-start.3 = (bf16[80,128]{1,0:T(8,128)(2,1)S(1)}, bf16[80,128]{1,0:T(8,128)(2,1)S(1)}, u32[]{:S(2)}, u32[]{:S(2)}) collective-permute-start(bf16[80,128]{1,0:T(8,128)(2,1)S(1)} %get-tuple-element.46), channel_id=1, source_target_pairs={{0,3},{1,0},{2,1},{3,2},{4,7},{5,4},{6,5},{7,6},{8,11},{9,8},{10,9... | collective-permute-start | bytes 61448 | tf_op jit(solution)/shard_map/ppermute | solution.py:301
  25.3 0.0 collective-permute-start.2
  25.3 0.0 copy-start.3
  25.3 0.7 copy-done.3
  26.0 0.0 copy-start
  26.0 0.0 copy-start.1
  26.0 0.0 copy-start.4
  26.0 0.0 copy-start.5
  26.0 0.0 copy-start.6
  26.0 17.2 %components.1 = (bf16[2048,256]{1,0:T(8,128)(2,1)}, bf16[1024,2048]{1,0:T(8,128)(2,1)}) custom-call(bf16[1024,8448]{1,0:T(8,128)(2,1)} %spectra_ref.1, bf16[8448,256]{1,0:T(8,128)(2,1)} %basis_ref.1, s32[1,1024]{1,0:T(1,128)S(1)} %copy-done.3), custom_call_target="tpu_custom_call" | custom-call | tf_op jit(solution)/shard_map/components/pallas_call | solution.py:30
  43.3 0.0 collective-permute-done.3.right_ref
  43.3 0.0 collective-permute-done.2.left_ref
  43.3 0.0 all-to-all-done
  43.3 10.0 %all-to-all-start.1 = ((bf16[128,16,256]{2,1,0:T(8,128)(2,1)}), bf16[128,16,256]{2,1,0:T(8,128)(2,1)S(1)}, u32[]{:S(2)}, u32[]{:S(2)}) async-start(bf16[128,16,256]{2,1,0:T(8,128)(2,1)} %bitcast.30), calls=%async_computation.1 | async-start | bytes 2097152 | tf_op jit(solution)/shard_map/all_to_all | solution.py:305
  53.3 0.0 copy-done
  53.3 7.4 %interpolate.1.column_ref = bf16[2048,128]{1,0:T(8,128)(2,1)S(1)} custom-call(f32[128,128]{1,0:T(8,128)S(1)} %bitcast.23, bf16[4096,128]{1,0:T(8,128)(2,1)S(1)} %bitcast.20, bf16[64,128]{1,0:T(8,128)(2,1)S(1)} %collective-permute-done.top_ref, bf16[64,128]{1,0:T(8,128)(2,1)S(1)} %collective-permute-done.1.bottom_ref, ...), custom_call_target="tpu_custom_call" | custom-call | tf_op jit(solution)/shard_map/interpolate/pallas_call | solution.py:30
  60.7 10.5 %all-to-all-done.1 = bf16[128,16,256]{2,1,0:T(8,128)(2,1)S(1)} async-done(((bf16[128,16,256]{2,1,0:T(8,128)(2,1)}), bf16[128,16,256]{2,1,0:T(8,128)(2,1)S(1)}, u32[]{:S(2)}, u32[]{:S(2)}) %all-to-all-start.1) | async-done | bytes 1048608 | tf_op jit(solution)/shard_map/all_to_all | solution.py:305
  71.2 0.0 copy-done.1
  71.2 0.0 copy-done.4
  71.2 0.0 copy-done.5
  71.2 0.0 copy-done.6
  71.2 0.0 copy-start.2
  71.2 0.9 copy-done.2
  72.1 3.2 %network.1 = (bf16[2048,256]{1,0:T(8,128)(2,1)}, bf16[2048,128]{1,0:T(8,128)(2,1)S(1)}) custom-call(bf16[2048,128]{1,0:T(8,128)(2,1)S(1)} %interpolate.1.column_ref, bf16[2048,256]{1,0:T(8,128)(2,1)S(1)} %bitcast.21, f32[1,256]{1,0:T(1,128)S(1)} %bitcast.27, bf16[128,512]{1,0:T(8,128)(2,1)S(1)} %copy-done.2, f32[1,512]{1,0:T(1,128)S(1)} %bitcast.26, ...), custom_call_target="tpu_custom_call" | custom-call | tf_op jit(solution)/shard_map/network/pallas_call | solution.py:30
  75.4 5.5 %all-to-all-start.2 = ((bf16[128,16,256]{2,1,0:T(8,128)(2,1)}), bf16[128,16,256]{2,1,0:T(8,128)(2,1)S(1)}, u32[]{:S(2)}, u32[]{:S(2)}) async-start(bf16[128,16,256]{2,1,0:T(8,128)(2,1)} %bitcast.29), calls=%async_computation.2 | async-start | bytes 2097152 | tf_op jit(solution)/shard_map/all_to_all | solution.py:305
  80.8 0.9 adjoint_rim.1
  81.8 1.8 %collective-permute-start.4 = (bf16[80,128]{1,0:T(8,128)(2,1)S(1)}, bf16[80,128]{1,0:T(8,128)(2,1)S(1)}, u32[]{:S(2)}, u32[]{:S(2)}) collective-permute-start(bf16[80,128]{1,0:T(8,128)(2,1)S(1)} %get-tuple-element.34), channel_id=1, source_target_pairs={{0,1},{1,2},{2,3},{3,0},{4,5},{5,6},{6,7},{7,4},{8,9},{9,10},{10,1... | collective-permute-start | bytes 61448 | tf_op jit(solution)/shard_map/ppermute | solution.py:301
  83.6 1.7 %collective-permute-start.5 = (bf16[80,128]{1,0:T(8,128)(2,1)S(1)}, bf16[80,128]{1,0:T(8,128)(2,1)S(1)}, u32[]{:S(2)}, u32[]{:S(2)}) collective-permute-start(bf16[80,128]{1,0:T(8,128)(2,1)S(1)} %get-tuple-element.35), channel_id=1, source_target_pairs={{0,3},{1,0},{2,1},{3,2},{4,7},{5,4},{6,5},{7,6},{8,11},{9,8},{10,9... | collective-permute-start | bytes 61448 | tf_op jit(solution)/shard_map/ppermute | solution.py:301
  85.3 10.1 %collective-permute-done.4.left_ref = bf16[80,128]{1,0:T(8,128)(2,1)S(1)} collective-permute-done((bf16[80,128]{1,0:T(8,128)(2,1)S(1)}, bf16[80,128]{1,0:T(8,128)(2,1)S(1)}, u32[]{:S(2)}, u32[]{:S(2)}) %collective-permute-start.4) | collective-permute-done | bytes 20512 | tf_op jit(solution)/shard_map/ppermute | solution.py:301
  95.4 0.0 collective-permute-done.5.right_ref
  95.4 1.9 %collective-permute-start.6 = (bf16[64,128]{1,0:T(8,128)(2,1)S(1)}, bf16[64,128]{1,0:T(8,128)(2,1)S(1)}, u32[]{:S(2)}, u32[]{:S(2)}) collective-permute-start(bf16[64,128]{1,0:T(8,128)(2,1)S(1)} %get-tuple-element.38), channel_id=1, source_target_pairs={{0,4},{4,8},{8,12},{12,16},{16,20},{20,24},{24,28},{28,32},{32,36}... | collective-permute-start | bytes 49160 | tf_op jit(solution)/shard_map/ppermute | solution.py:301
  97.3 5.8 %collective-permute-start.7 = (bf16[64,128]{1,0:T(8,128)(2,1)S(1)}, bf16[64,128]{1,0:T(8,128)(2,1)S(1)}, u32[]{:S(2)}, u32[]{:S(2)}) collective-permute-start(bf16[64,128]{1,0:T(8,128)(2,1)S(1)} %get-tuple-element.39), channel_id=1, source_target_pairs={{4,0},{8,4},{12,8},{16,12},{20,16},{24,20},{28,24},{32,28},{36,32}... | collective-permute-start | bytes 49160 | tf_op jit(solution)/shard_map/ppermute | solution.py:301
  103.1 5.9 %adjoint.1.grad_ref = f32[64,64,128]{2,1,0:T(8,128)} custom-call(f32[128,128]{1,0:T(8,128)S(1)} %bitcast.25, bf16[2048,128]{1,0:T(8,128)(2,1)S(1)} %get-tuple-element.33.g_ref), custom_call_target="tpu_custom_call" | custom-call | tf_op jit(solution)/shard_map/adjoint/pallas_call | solution.py:30
  109.0 0.0 collective-permute-done.6.above_ref
  109.0 0.0 collective-permute-done.7.below_ref
  109.0 0.0 all-to-all-done.2
  109.0 5.6 %finish.1 = (bf16[1024,256]{1,0:T(8,128)(2,1)}, f32[64,64,128]{2,1,0:T(8,128)}) custom-call(bf16[2048,256]{1,0:T(8,128)(2,1)S(1)} %bitcast.22, bf16[1024,2048]{1,0:T(8,128)(2,1)} %get-tuple-element.32.pick_ref, bf16[80,128]{1,0:T(8,128)(2,1)S(1)} %collective-permute-done.4.left_ref, ...), custom_call_target="tpu_custom_call", output_to_operand_aliasing={{1}: (6, {})} | custom-call | tf_op jit(solution)/shard_map/finish/pallas_call | solution.py:30
  (4 shorter events, 0.0 us)
Async XLA Ops:
  1.4 20.3 %collective-permute-start.1 = (bf16[64,128]{1,0:T(8,128)(2,1)S(1)}, bf16[64,128]{1,0:T(8,128)(2,1)S(1)}, u32[]{:S(2)}, u32[]{:S(2)}) collective-permute-start(bf16[64,128]{1,0:T(8,128)(2,1)S(1)} %get-tuple-element.40), channel_id=1, source_target_pairs={{4,0},{8,4},{12,8},{16,12},{20,16},{24,20},{28,24},{32,28},{36,32}... | collective-permute-start | bytes 49160 | tf_op jit(solution)/shard_map/ppermute | solution.py:301
  7.0 14.6 %collective-permute-start = (bf16[64,128]{1,0:T(8,128)(2,1)S(1)}, bf16[64,128]{1,0:T(8,128)(2,1)S(1)}, u32[]{:S(2)}, u32[]{:S(2)}) collective-permute-start(bf16[64,128]{1,0:T(8,128)(2,1)S(1)} %get-tuple-element.41), channel_id=1, source_target_pairs={{0,4},{4,8},{8,12},{12,16},{16,20},{20,24},{24,28},{28,32},{32,36}... | collective-permute-start | bytes 49160 | tf_op jit(solution)/shard_map/ppermute | solution.py:301
  11.5 31.8 %all-to-all-start = ((f32[128,1,128]{2,1,0:T(1,128)}), f32[128,1,128]{2,1,0:T(1,128)S(1)}, u32[]{:S(2)}, u32[]{:S(2)}) async-start(f32[128,1,128]{2,1,0:T(1,128)} %bitcast.31), calls=%async_computation | async-start | bytes 131072 | tf_op jit(solution)/shard_map/all_to_all | solution.py:305
  22.5 20.8 %collective-permute-start.3 = (bf16[80,128]{1,0:T(8,128)(2,1)S(1)}, bf16[80,128]{1,0:T(8,128)(2,1)S(1)}, u32[]{:S(2)}, u32[]{:S(2)}) collective-permute-start(bf16[80,128]{1,0:T(8,128)(2,1)S(1)} %get-tuple-element.46), channel_id=1, source_target_pairs={{0,3},{1,0},{2,1},{3,2},{4,7},{5,4},{6,5},{7,6},{8,11},{9,8},{10,9... | collective-permute-start | bytes 61448 | tf_op jit(solution)/shard_map/ppermute | solution.py:301
  25.3 18.0 %collective-permute-start.2 = (bf16[80,128]{1,0:T(8,128)(2,1)S(1)}, bf16[80,128]{1,0:T(8,128)(2,1)S(1)}, u32[]{:S(2)}, u32[]{:S(2)}) collective-permute-start(bf16[80,128]{1,0:T(8,128)(2,1)S(1)} %get-tuple-element.47), channel_id=1, source_target_pairs={{0,1},{1,2},{2,3},{3,0},{4,5},{5,6},{6,7},{7,4},{8,9},{9,10},{10,1... | collective-permute-start | bytes 61448 | tf_op jit(solution)/shard_map/ppermute | solution.py:301
  25.3 0.7 copy-start.3
  26.0 27.3 %copy-start = (bf16[64,64,128]{2,1,0:T(8,128)(2,1)S(1)}, bf16[64,64,128]{2,1,0:T(8,128)(2,1)}, u32[]{:S(2)}) copy-start(bf16[64,64,128]{2,1,0:T(8,128)(2,1)} %state_ref.1) | copy-start | bytes 3145732
  26.0 45.2 %copy-start.1 = (bf16[512,256]{1,0:T(8,128)(2,1)S(1)}, bf16[512,256]{1,0:T(8,128)(2,1)}, u32[]{:S(2)}) copy-start(bf16[512,256]{1,0:T(8,128)(2,1)} %w_out_ref.1) | copy-start | bytes 786436
  26.0 45.2 %copy-start.4 = (f32[512]{0:T(512)S(1)}, f32[512]{0:T(512)}, u32[]{:S(2)}) copy-start(f32[512]{0:T(512)} %param.21) | copy-start | bytes 6148
  26.0 45.2 %copy-start.5 = (f32[256]{0:T(256)S(1)}, f32[256]{0:T(256)}, u32[]{:S(2)}) copy-start(f32[256]{0:T(256)} %param.19) | copy-start | bytes 3076
  26.0 45.2 %copy-start.6 = (f32[256]{0:T(256)S(1)}, f32[256]{0:T(256)}, u32[]{:S(2)}) copy-start(f32[256]{0:T(256)} %param.23) | copy-start | bytes 3076
  43.3 27.9 %all-to-all-start.1 = ((bf16[128,16,256]{2,1,0:T(8,128)(2,1)}), bf16[128,16,256]{2,1,0:T(8,128)(2,1)S(1)}, u32[]{:S(2)}, u32[]{:S(2)}) async-start(bf16[128,16,256]{2,1,0:T(8,128)(2,1)} %bitcast.30), calls=%async_computation.1 | async-start | bytes 2097152 | tf_op jit(solution)/shard_map/all_to_all | solution.py:305
  71.2 0.9 copy-start.2
  75.4 33.6 %all-to-all-start.2 = ((bf16[128,16,256]{2,1,0:T(8,128)(2,1)}), bf16[128,16,256]{2,1,0:T(8,128)(2,1)S(1)}, u32[]{:S(2)}, u32[]{:S(2)}) async-start(bf16[128,16,256]{2,1,0:T(8,128)(2,1)} %bitcast.29), calls=%async_computation.2 | async-start | bytes 2097152 | tf_op jit(solution)/shard_map/all_to_all | solution.py:305
  81.8 13.6 %collective-permute-start.4 = (bf16[80,128]{1,0:T(8,128)(2,1)S(1)}, bf16[80,128]{1,0:T(8,128)(2,1)S(1)}, u32[]{:S(2)}, u32[]{:S(2)}) collective-permute-start(bf16[80,128]{1,0:T(8,128)(2,1)S(1)} %get-tuple-element.34), channel_id=1, source_target_pairs={{0,1},{1,2},{2,3},{3,0},{4,5},{5,6},{6,7},{7,4},{8,9},{9,10},{10,1... | collective-permute-start | bytes 61448 | tf_op jit(solution)/shard_map/ppermute | solution.py:301
  83.6 11.8 %collective-permute-start.5 = (bf16[80,128]{1,0:T(8,128)(2,1)S(1)}, bf16[80,128]{1,0:T(8,128)(2,1)S(1)}, u32[]{:S(2)}, u32[]{:S(2)}) collective-permute-start(bf16[80,128]{1,0:T(8,128)(2,1)S(1)} %get-tuple-element.35), channel_id=1, source_target_pairs={{0,3},{1,0},{2,1},{3,2},{4,7},{5,4},{6,5},{7,6},{8,11},{9,8},{10,9... | collective-permute-start | bytes 61448 | tf_op jit(solution)/shard_map/ppermute | solution.py:301
  95.4 13.6 %collective-permute-start.6 = (bf16[64,128]{1,0:T(8,128)(2,1)S(1)}, bf16[64,128]{1,0:T(8,128)(2,1)S(1)}, u32[]{:S(2)}, u32[]{:S(2)}) collective-permute-start(bf16[64,128]{1,0:T(8,128)(2,1)S(1)} %get-tuple-element.38), channel_id=1, source_target_pairs={{0,4},{4,8},{8,12},{12,16},{16,20},{20,24},{24,28},{28,32},{32,36}... | collective-permute-start | bytes 49160 | tf_op jit(solution)/shard_map/ppermute | solution.py:301
  97.3 11.7 %collective-permute-start.7 = (bf16[64,128]{1,0:T(8,128)(2,1)S(1)}, bf16[64,128]{1,0:T(8,128)(2,1)S(1)}, u32[]{:S(2)}, u32[]{:S(2)}) collective-permute-start(bf16[64,128]{1,0:T(8,128)(2,1)S(1)} %get-tuple-element.39), channel_id=1, source_target_pairs={{4,0},{8,4},{12,8},{16,12},{20,16},{24,20},{28,24},{32,28},{36,32}... | collective-permute-start | bytes 49160 | tf_op jit(solution)/shard_map/ppermute | solution.py:301

commit v2 on v1

v2 whole, which is shorter than its diff:
```python
import functools

import jax
import jax.numpy as jnp
from jax import lax
from jax.experimental import pallas as pl
from jax.experimental.pallas import tpu as pltpu
from jax.sharding import PartitionSpec as P

CAP = 16
F32 = jnp.float32
BF16 = jnp.bfloat16
I32 = jnp.int32
NT = (((1,), (1,)), ((), ()))
AXES = ("lat", "lon")


def iota(shape, dim):
    return lax.broadcasted_iota(I32, shape, dim)


def mm(a, b):
    return jnp.dot(a, b, preferred_element_type=F32)


def ones_where(mask):
    return jnp.where(mask, 1.0, 0.0).astype(BF16)


def call(body, out_shape, name, *args, scratch=(), specs=None, outs=None, grant=8, alias=None):
    vmem = pl.BlockSpec(memory_space=pltpu.VMEM)
    return pl.pallas_call(
        body,
        in_specs=specs or [vmem] * len(args),
        out_specs=outs or jax.tree.map(lambda s: vmem, out_shape),
        out_shape=out_shape,
        scratch_shapes=scratch,
        input_output_aliases=alias or {},
        compiler_params=pltpu.CompilerParams(vmem_limit_bytes=grant << 20) if grant else None,
        name=name,
    )(*args)


def route_body(dest_ref, row_ref, col_ref, weight_ref, state_ref, send_ref, place_ref, first_ref, last_ref):
    first_ref[...] = state_ref[:, 0, :]
    last_ref[...] = state_ref[:, 63, :]
    dest = dest_ref[...]
    tiles = send_ref.shape[0]
    obs = dest.shape[1]
    onehot = jnp.where(iota((tiles, obs), 0) == dest, 1.0, 0.0)
    before = ones_where(iota((obs, obs), 0) < iota((obs, obs), 1))
    rank = mm(onehot.astype(BF16), before)
    slot = jnp.sum(onehot * rank, axis=0, keepdims=True).astype(I32)
    place_ref[...] = dest * CAP + slot
    here = iota((CAP, obs), 0) == slot
    weights = weight_ref[...].astype(F32)
    fields = [weights[k : k + 1] for k in range(4)]
    fields += [row_ref[...].astype(F32), col_ref[...].astype(F32)]
    parts = [jnp.where(here, field, 0.0) for field in fields]
    parts.append(jnp.zeros((128 - CAP * len(parts), obs), F32))
    table = jnp.concatenate(parts, 0).astype(BF16)
    send_ref[...] = lax.dot_general(onehot.astype(BF16), table, NT, preferred_element_type=F32)


def fields_by_row(recv, first, count):
    tiles = recv.shape[0]
    pick = ones_where((iota((count, tiles), 0) + first) // CAP == iota((count, tiles), 1))
    mine = mm(pick, recv)
    mine = jnp.where(iota((count, 128), 0) % CAP == iota((count, 128), 1) % CAP, mine, 0.0)
    spread = ones_where(iota((128, 768), 0) // CAP == iota((128, 768), 1) // 128)
    out = mm(mine.astype(BF16), spread)
    return [out[:, 128 * k : 128 * k + 128] for k in range(6)]


def fields_by_lane(recv, slots):
    tiles = recv.shape[0]
    pick = ones_where(iota((tiles, slots), 1) // CAP == iota((tiles, slots), 0))
    mine = mm(recv.astype(F32).T.astype(BF16), pick)
    mine = jnp.where(iota((128, slots), 1) % CAP == iota((128, slots), 0) % CAP, mine, 0.0)
    gather = ones_where(iota((8, 128), 1) // CAP == iota((8, 128), 0))
    out = mm(gather, mine.astype(BF16))
    return [out[k : k + 1] for k in range(6)]


def pair_of(hit0, value0, hit1, value1):
    return jnp.where(hit0, value0, jnp.where(hit1, value1, jnp.zeros((), value0.dtype)))


def gather_body(recv_ref, own_ref, top_ref, bottom_ref, left_ref, right_ref, out_ref, rim_ref, *matrices):
    slots = out_ref.shape[0]
    chunk = matrices[0].shape[0]
    rim_ref[0:64, :] = top_ref[...]
    rim_ref[64:128, :] = bottom_ref[...]
    rim_ref[128:192, :] = left_ref[0:64, :]
    rim_ref[192:256, :] = right_ref[0:64, :]
    rim_ref[256:272, :] = left_ref[64:80, :]
    rim_ref[272:288, :] = right_ref[64:80, :]
    rim_ref[288:384, :] = jnp.zeros((96, rim_ref.shape[1]), BF16)
    recv = recv_ref[...].astype(BF16)
    lane = iota((chunk, 128), 1).astype(F32)
    upper = jnp.where(lane >= 64.0, 1.0, 0.0)
    in_row = (lane - 64.0 * upper).astype(BF16)
    upper = upper.astype(BF16)
    lane = lane.astype(BF16)

    def build(first, matrix_ref):
        w0, w1, w2, w3, row, col = [f.astype(BF16) for f in fields_by_row(recv, first, chunk)]
        at0, at1 = in_row == col - 1.0, in_row == col
        p0 = pair_of(at0, w0, at1, w2)
        p1 = pair_of(at0, w1, at1, w3)
        zero = jnp.zeros((), BF16)
        edge = 65.0 * upper
        matrix_ref[:, 4096:4224] = pair_of(edge == row, p0, edge == row + 1.0, p1)
        high = upper > 0.5
        side = pair_of(in_row == row - 1.0, jnp.where(high, w2, w0), in_row == row, jnp.where(high, w3, w1))
        matrix_ref[:, 4224:4352] = jnp.where(col == 64.0 * upper, side, zero)
        corner = pair_of(lane == 0.0, w0, lane == 1.0, w1) + pair_of(lane == 16.0, w2, lane == 17.0, w3)
        at_col = jnp.where(lane < 16.0, zero, zero + 64.0)
        odd = jnp.where(lane < 16.0, lane, lane - 16.0)
        matrix_ref[:, 4352:4480] = jnp.where(row == 64.0 * odd, jnp.where(col == at_col, corner, zero), zero)
        offset = row - upper
        for j in range(32):
            matrix_ref[:, 128 * j : 128 * j + 128] = pair_of(offset == 2.0 * j + 1.0, p0, offset == 2.0 * j, p1)

    def use(first, matrix_ref):
        out = mm(matrix_ref[:, :4096], own_ref[...]) + mm(matrix_ref[:, 4096:], rim_ref[...])
        out_ref[first : first + chunk, :] = out.astype(BF16)

    count = slots // chunk
    build(0, matrices[0])
    for i in range(count):
        if i + 1 < count:
            build((i + 1) * chunk, matrices[i + 1])
        use(i * chunk, matrices[i])


def components_body(spectra_ref, basis_ref, place_ref, pcs_ref, buffer, basis_buffer, sems, basis_sem):
    obs = spectra_ref.shape[0]
    blocks = buffer.shape[0]
    rows = obs // blocks
    basis = pltpu.make_async_copy(basis_ref, basis_buffer, basis_sem)
    basis.start()
    copies = [
        pltpu.make_async_copy(spectra_ref.at[pl.ds(i * rows, rows), :], buffer.at[i], sems.at[i]) for i in range(blocks)
    ]
    for copy in copies:
        copy.start()
    basis.wait()
    for i, copy in enumerate(copies):
        copy.wait()
        pcs_ref[i * rows : i * rows + rows, :] = mm(buffer[i], basis_buffer[...]).astype(BF16)


def network_body(recv_ref, place_ref, pcs_ref, inv_ref, w_in_hbm, b_in_ref, w_out_hbm, b_out_ref, dep_ref, send_ref, pack_ref, unpack_ref, w_in_ref, w_out_ref, g_ref, dep_buffer, send_buffer, w_sems, dep_sems, send_sems):
    slots = recv_ref.shape[0]
    obs = pcs_ref.shape[0]
    loads = [pltpu.make_async_copy(w_in_hbm, w_in_ref, w_sems.at[0]), pltpu.make_async_copy(w_out_hbm, w_out_ref, w_sems.at[1])]
    for copy in loads:
        copy.start()
    inv = inv_ref[...]
    copies = []
    block = obs // 4
    place = place_ref[...]
    wide = jnp.broadcast_to(place.astype(F32), (128, obs)).T
    lane = iota((block, 128), 1).astype(F32)
    for i in range(4):
        at = slice(i * block, (i + 1) * block)
        for b in range(slots // 128):
            unpack_ref[at, 128 * b : 128 * b + 128] = ones_where(wide[at] - 128.0 * b == lane)
        half = slots // 4
        pack_ref[i * half : (i + 1) * half, :] = ones_where(iota((half, obs), 0) + i * half == place)
        column = mm(unpack_ref[at, :], recv_ref[...]).astype(BF16)
        if i == 0:
            for copy in loads:
                copy.wait()
        pre = mm(column, w_in_ref[...]) + b_in_ref[...]
        sig = jax.nn.sigmoid(pre)
        hidden = (pre * sig).astype(BF16)
        sim = mm(hidden, w_out_ref[...]) + b_out_ref[...]
        dep = (sim - pcs_ref[at, :].astype(F32)) * inv
        dep_buffer[at, :] = dep.astype(BF16)
        copies.append(pltpu.make_async_copy(dep_buffer.at[at, :], dep_ref.at[at, :], dep_sems.at[i]))
        copies[-1].start()
        g_sim = (dep * inv).astype(BF16)
        g_hidden = lax.dot_general(g_sim, w_out_ref[...], NT, preferred_element_type=F32)
        g_pre = (g_hidden * sig * (1.0 + pre * (1.0 - sig))).astype(BF16)
        g_ref[at, :] = lax.dot_general(g_pre, w_in_ref[...], NT, preferred_element_type=F32).astype(BF16)
    block = slots // 4
    for i in range(4):
        at = slice(i * block, (i + 1) * block)
        send_buffer[at, :] = mm(pack_ref[at, :], g_ref[...]).astype(BF16)
        copies.append(pltpu.make_async_copy(send_buffer.at[at, :], send_ref.at[at, :], send_sems.at[i]))
        copies[-1].start()
    for copy in copies:
        copy.wait()


def prepare_body(recv_ref, fields_ref):
    fields = fields_by_lane(recv_ref[...].astype(BF16), fields_ref.shape[1])
    fields_ref[...] = jnp.concatenate(fields + [fields[5], fields[5]], 0)


def scatter_rim_body(fields_ref, g_ref, up_ref, down_ref, left_ref, right_ref, rim_ref):
    slots = g_ref.shape[0]
    w0, w1, w2, w3, row, col = [fields_ref[k : k + 1, :].astype(BF16) for k in range(6)]
    zero = jnp.zeros((), BF16)
    sub = iota((64, slots), 0).astype(F32).astype(BF16)
    at0, at1 = sub == row - 1.0, sub == row
    rim_ref[128:192, :] = jnp.where(col == 0.0, pair_of(at0, w0, at1, w1), zero)
    rim_ref[208:272, :] = jnp.where(col == 64.0, pair_of(at0, w2, at1, w3), zero)
    low = iota((16, slots), 0).astype(F32).astype(BF16)
    first, last = jnp.where(row == 0.0, zero, zero - 1.0), jnp.where(row == 64.0, zero + 1.0, zero - 1.0)
    rim_ref[192:208, :] = jnp.where(col == 0.0, pair_of(low == first, w0, low == last, w1), zero)
    rim_ref[272:288, :] = jnp.where(col == 64.0, pair_of(low == first, w2, low == last, w3), zero)
    at0, at1 = sub == col - 1.0, sub == col
    rim_ref[0:64, :] = jnp.where(row == 0.0, pair_of(at0, w0, at1, w2), zero)
    rim_ref[64:128, :] = jnp.where(row == 64.0, pair_of(at0, w1, at1, w3), zero)
    out = mm(rim_ref[...], g_ref[...])
    up_ref[...] = out[0:64]
    down_ref[...] = out[64:128]
    left_ref[...] = out[128:208].astype(BF16)
    right_ref[...] = out[208:288].astype(BF16)


def corner_body(up_ref, down_ref, left_ref, right_ref, up_out, down_out):
    at = iota((64, 128), 0)
    left = left_ref[64:80, :].astype(F32)
    right = right_ref[64:80, :].astype(F32)
    for k, (ref, out) in enumerate(((up_ref, up_out), (down_ref, down_out))):
        extra = jnp.where(at == 0, left[k : k + 1], jnp.where(at == 63, right[k : k + 1], 0.0))
        out[...] = (ref[...] + extra).astype(BF16)


def scatter_body(half, fields_ref, g_ref, *refs):
    out_ref, buffer, sems = refs[-5:-2]
    matrices = refs[-2:]
    slots = g_ref.shape[0]
    rows = 16
    w0, w1, w2, w3, row, col = [fields_ref[k : k + 1, :].astype(BF16) for k in range(6)]
    sub = iota((64, slots), 0).astype(F32).astype(BF16)
    at0, at1 = sub == col - 1.0, sub == col
    p0 = pair_of(at0, w0, at1, w2)
    p1 = pair_of(at0, w1, at1, w3)
    row = jnp.broadcast_to(row, (64, slots))

    def build(first, matrix_ref):
        for j in range(rows):
            at = float(first + j)
            matrix_ref[64 * j : 64 * j + 64, :] = pair_of(row == at + 1.0, p0, row == at, p1)

    copies = []
    build(32 * half, matrices[0])
    for i in range(2):
        first = 32 * half + rows * i
        if i == 0:
            build(first + rows, matrices[1])
        out = mm(matrices[i][...], g_ref[...])
        buffer[i] = out.reshape(rows, 64, out.shape[1])
        copies.append(pltpu.make_async_copy(buffer.at[i], out_ref.at[pl.ds(first, rows)], sems.at[i]))
        copies[i].start()
    for copy in copies:
        copy.wait()


def edge_body(left_ref, right_ref, above_ref, below_ref, grad_ref, out_ref, sides, rows, in_sems, out_sems):
    edges = [
        (out_ref.at[:, pl.ds(0, 8), :], sides.at[0]),
        (out_ref.at[:, pl.ds(56, 8), :], sides.at[1]),
        (out_ref.at[0, pl.ds(8, 48), :], rows.at[0]),
        (out_ref.at[63, pl.ds(8, 48), :], rows.at[1]),
    ]
    loads = [pltpu.make_async_copy(a, b, in_sems.at[i]) for i, (a, b) in enumerate(edges)]
    stores = [pltpu.make_async_copy(b, a, out_sems.at[i]) for i, (a, b) in enumerate(edges)]
    for copy in loads:
        copy.start()
    for copy in loads:
        copy.wait()
    above, below = above_ref[...].astype(F32), below_ref[...].astype(F32)
    sides[0, :, 0, :] += left_ref[0:64, :].astype(F32)
    sides[1, :, 7, :] += right_ref[0:64, :].astype(F32)
    sides[0, 0] += above[0:8]
    sides[1, 0] += above[56:64]
    sides[0, 63] += below[0:8]
    sides[1, 63] += below[56:64]
    rows[0] += above[8:56]
    rows[1] += below[8:56]
    for copy in stores:
        copy.start()
    for copy in stores:
        copy.wait()


def in_hbm(x):
    return pltpu.with_memory_space_constraint(x, pltpu.HBM)


def shift(x, axis, step, closed):
    count = lax.axis_size(axis)
    pairs = [(i, (i + step) % count) for i in range(count) if closed or 0 <= i + step < count]
    return lax.ppermute(x, axis, pairs)


def exchange(x):
    return lax.all_to_all(x, AXES, split_axis=0, concat_axis=0, tiled=True)


def per_device(
    spectra,
    pc_basis,
    destination,
    corner_row,
    corner_col,
    corner_weight,
    state,
    inv_sigma,
    w_in,
    b_in,
    w_out,
    b_out,
):
    tiles = lax.axis_size("lat") * lax.axis_size("lon")
    obs = spectra.shape[0]
    npc = pc_basis.shape[1]
    levels = state.shape[2]
    slots = tiles * CAP
    sds = jax.ShapeDtypeStruct

    top = shift(state[63], "lat", 1, False)
    bottom = shift(state[0], "lat", -1, False)
    send_meta, place, first, last = call(
        route_body,
        (sds((tiles, 128), F32), sds((1, obs), I32), sds((64, levels), BF16), sds((64, levels), BF16)),
        "route",
        destination.reshape(1, obs),
        corner_row.reshape(1, obs),
        corner_col.reshape(1, obs),
        corner_weight.T,
        state,
        grant=None,
    )
    recv_meta = exchange(send_meta)

    fill = jnp.zeros((14, levels), BF16)
    left = shift(jnp.concatenate([last, top[63:], bottom[63:], fill], 0), "lon", 1, True)
    right = shift(jnp.concatenate([first, top[:1], bottom[:1], fill], 0), "lon", -1, True)

    vmem = pl.BlockSpec(memory_space=pltpu.VMEM)
    hbm = pl.BlockSpec(memory_space=pltpu.HBM)
    columns = call(
        gather_body,
        pltpu.HBM((slots, levels), BF16),
        "interpolate",
        recv_meta,
        state.reshape(-1, levels),
        top,
        bottom,
        left,
        right,
        scratch=[pltpu.VMEM((384, levels), BF16)] + [pltpu.VMEM((slots // 4, 4480), BF16)] * 4,
        grant=26,
    )
    columns, place = lax.optimization_barrier((columns, place))
    recv_columns = exchange(columns.reshape(tiles, CAP, levels)).reshape(slots, levels)
    pcs = call(
        components_body,
        sds((obs, npc), BF16),
        "components",
        in_hbm(spectra),
        in_hbm(pc_basis),
        place,
        specs=[hbm, hbm, vmem],
        scratch=[
            pltpu.VMEM((4, obs // 4, spectra.shape[1]), BF16),
            pltpu.VMEM(pc_basis.shape, BF16),
            pltpu.SemaphoreType.DMA((4,)),
            pltpu.SemaphoreType.DMA,
        ],
        grant=26,
    )
    departures, send_g = call(
        network_body,
        (pltpu.HBM((obs, npc), BF16), pltpu.HBM((slots, levels), BF16)),
        "network",
        recv_columns,
        place,
        pcs,
        inv_sigma[None],
        in_hbm(w_in),
        b_in[None],
        in_hbm(w_out),
        b_out[None],
        specs=[vmem] * 4 + [hbm, vmem, hbm, vmem],
        outs=(hbm, hbm),
        scratch=[
            pltpu.VMEM((slots, obs), BF16),
            pltpu.VMEM((obs, slots), BF16),
            pltpu.VMEM(w_in.shape, BF16),
            pltpu.VMEM(w_out.shape, BF16),
            pltpu.VMEM((obs, levels), BF16),
            pltpu.VMEM((obs, npc), BF16),
            pltpu.VMEM((slots, levels), BF16),
            pltpu.SemaphoreType.DMA((2,)),
            pltpu.SemaphoreType.DMA((4,)),
            pltpu.SemaphoreType.DMA((4,)),
        ],
        grant=24,
    )
    send_g, recv_meta = lax.optimization_barrier((send_g, recv_meta))
    g = exchange(send_g.reshape(tiles, CAP, levels)).reshape(slots, levels)
    fields = call(prepare_body, sds((8, slots), F32), "prepare", recv_meta)
    up, down, g_left, g_right = call(
        scatter_rim_body,
        (sds((64, levels), F32), sds((64, levels), F32), sds((80, levels), BF16), sds((80, levels), BF16)),
        "adjoint_rim",
        fields,
        g,
        scratch=[pltpu.VMEM((288, slots), BF16)],
    )
    from_right = shift(g_left, "lon", -1, True)
    from_left = shift(g_right, "lon", 1, True)
    half = [pltpu.VMEM((2, 16, 64, levels), F32), pltpu.SemaphoreType.DMA((2,))]
    half += [pltpu.VMEM((1024, slots), BF16)] * 2
    gradient = call(
        functools.partial(scatter_body, 0),
        pltpu.HBM((64, 64, levels), F32),
        "adjoint_a",
        fields,
        g,
        outs=hbm,
        scratch=half,
        grant=14,
    )
    up, down = call(
        corner_body,
        (sds((64, levels), BF16), sds((64, levels), BF16)),
        "corners",
        up,
        down,
        from_left,
        from_right,
    )
    up, down, g = lax.optimization_barrier((up, down, g))
    from_below = shift(up, "lat", -1, False)
    from_above = shift(down, "lat", 1, False)
    gradient = call(
        functools.partial(scatter_body, 1),
        pltpu.HBM((64, 64, levels), F32),
        "adjoint_b",
        fields,
        g,
        in_hbm(gradient),
        specs=[vmem, vmem, hbm],
        outs=hbm,
        scratch=half,
        grant=14,
        alias={2: 0},
    )
    gradient = call(
        edge_body,
        pltpu.HBM((64, 64, levels), F32),
        "edges",
        from_left,
        from_right,
        from_above,
        from_below,
        in_hbm(gradient),
        specs=[vmem, vmem, vmem, vmem, hbm],
        outs=hbm,
        scratch=[
            pltpu.VMEM((2, 64, 8, levels), F32),
            pltpu.VMEM((2, 48, levels), F32),
            pltpu.SemaphoreType.DMA((4,)),
            pltpu.SemaphoreType.DMA((4,)),
        ],
        alias={4: 0},
    )
    return (departures, gradient)


def solution(mesh):
    return jax.shard_map(
        per_device,
        mesh=mesh,
        in_specs=(
            P(AXES, None),
            P(),
            P(AXES, None),
            P(AXES),
            P(AXES),
            P(AXES, None),
            P("lat", "lon", None),
            P(),
            P(),
            P(),
            P(),
            P(),
        ),
        out_specs=(P(AXES, None), P("lat", "lon", None)),
        check_vma=False,
    )
```

time: 116 us -> 114 us (0.983)
  waiting for transfers between devices: 20.6 us -> 18.6 us
  starting transfers between devices: 47.1 us -> 48.7 us
  local copies, waits for them, and re-layouts: 2.43 us -> 0.95 us
    ppermute x8, waiting for transfers between devices: 10.1 us -> 6.76 us  [shift(): return lax.ppermute(x, axis, pairs)]
    all_to_all x3, starting transfers between devices: 25.5 us -> 27.1 us  [exchange(): return lax.all_to_all(x, AXES, split_axis=0, concat_axis=0, tiled=True)]
    unnamed x14 -> x10, local copies, waits for them, and re-layouts: 1.6 us -> 0.03 us
    all_to_all x3, waiting for transfers between devices: 10.5 us -> 11.8 us  [exchange(): return lax.all_to_all(x, AXES, split_axis=0, concat_axis=0, tiled=True)]
    pallas_call x8 -> x10, Pallas kernels: 42.9 us -> 42.4 us  [call(): pl.pallas_call(body, in_specs=specs or [vmem] * len(args), out_specs=outs...]
  transfers between devices with their start and end apart: 11 -> 11, of which waited for: 2 -> 4; matrix products, arithmetic and copies ran while one was open for 1% -> 1% of each run, Pallas kernels for 30% -> 22%
where the time goes in v2:
time: 114 us; the launch traced here: 112 us
  starting transfers between devices  48.7 us (43%)
  Pallas kernels  42.4 us (37%)
  waiting for transfers between devices  18.6 us (16%)
    pallas_call x10, Pallas kernels, call(): pl.pallas_call(body, in_specs=specs or [vmem] * len(args), out_specs=outs...  42.4 us
    all_to_all x3, starting transfers between devices, exchange(): return lax.all_to_all(x, AXES, split_axis=0, concat_axis=0, tiled=True)  27.1 us
    ppermute x8, starting transfers between devices, shift(): return lax.ppermute(x, axis, pairs)  21.6 us
    all_to_all x3, waiting for transfers between devices, exchange(): return lax.all_to_all(x, AXES, split_axis=0, concat_axis=0, tiled=True)  11.8 us
    ppermute x8, waiting for transfers between devices, shift(): return lax.ppermute(x, axis, pairs)  6.76 us
  transfers between devices with their start and end apart: 11, of which 4 were waited for; matrix products, arithmetic and copies ran while one was open for 1% of the time, Pallas kernels for 22%

profile of v2, /device:TPU:6, one launch (start us, length us, event | category | flops | bytes accessed | tf_op | source)
XLA Modules:
  0.0 112.5 jit_solution(7040919864376224697)
XLA Ops:
  0.6 0.0 copy-start
  0.6 0.8 slice_bitcast_fusion
  1.5 5.6 %collective-permute-start.1 = (bf16[64,128]{1,0:T(8,128)(2,1)S(1)}, bf16[64,128]{1,0:T(8,128)(2,1)S(1)}, u32[]{:S(2)}, u32[]{:S(2)}) collective-permute-start(bf16[64,128]{1,0:T(8,128)(2,1)S(1)} %get-tuple-element.40), channel_id=1, source_target_pairs={{4,0},{8,4},{12,8},{16,12},{20,16},{24,20},{28,24},{32,28},{36,32}... | collective-permute-start | bytes 49160 | tf_op jit(solution)/shard_map/ppermute | solution.py:300
  7.1 1.9 %collective-permute-start = (bf16[64,128]{1,0:T(8,128)(2,1)S(1)}, bf16[64,128]{1,0:T(8,128)(2,1)S(1)}, u32[]{:S(2)}, u32[]{:S(2)}) collective-permute-start(bf16[64,128]{1,0:T(8,128)(2,1)S(1)} %get-tuple-element.41), channel_id=1, source_target_pairs={{0,4},{4,8},{8,12},{12,16},{16,20},{20,24},{24,28},{28,32},{32,36}... | collective-permute-start | bytes 49160 | tf_op jit(solution)/shard_map/ppermute | solution.py:300
  9.0 2.6 %route.1 = (f32[128,128]{1,0:T(8,128)}, s32[1,1024]{1,0:T(1,128)}, bf16[64,128]{1,0:T(8,128)(2,1)}, bf16[64,128]{1,0:T(8,128)(2,1)}) custom-call(s32[1,1024]{1,0:T(1,128)} %bitcast.34, s32[1,1024]{1,0:T(1,128)} %bitcast.35, s32[1,1024]{1,0:T(1,128)} %bitcast.36, bf16[4,1024]{1,0:T(4,128)(2,1)} %bitcast.33, bf16[64,64,128]{2,1,0:T(8,128)(2,1)} %state_ref.1), custom_call_target="tpu_custom_call" | custom-call | tf_op jit(solution)/shard_map/route/pallas_call | solution.py:32
  11.6 0.0 copy-start.1
  11.6 10.0 %all-to-all-start = ((f32[128,1,128]{2,1,0:T(1,128)}), f32[128,1,128]{2,1,0:T(1,128)S(1)}, u32[]{:S(2)}, u32[]{:S(2)}) async-start(f32[128,1,128]{2,1,0:T(1,128)} %bitcast.32), calls=%async_computation | async-start | bytes 131072 | tf_op jit(solution)/shard_map/all_to_all | solution.py:304
  21.6 0.1 pad.7.clone
  21.7 0.0 collective-permute-done.1.bottom_ref
  21.7 0.0 collective-permute-done.top_ref
  21.8 0.8 maximum_maximum_fusion.1
  22.6 2.8 %collective-permute-start.3 = (bf16[80,128]{1,0:T(8,128)(2,1)S(1)}, bf16[80,128]{1,0:T(8,128)(2,1)S(1)}, u32[]{:S(2)}, u32[]{:S(2)}) collective-permute-start(bf16[80,128]{1,0:T(8,128)(2,1)S(1)} %get-tuple-element.46), channel_id=1, source_target_pairs={{0,3},{1,0},{2,1},{3,2},{4,7},{5,4},{6,5},{7,6},{8,11},{9,8},{10,9... | collective-permute-start | bytes 61448 | tf_op jit(solution)/shard_map/ppermute | solution.py:300
  25.4 0.0 collective-permute-start.2
  25.4 1.5 %collective-permute-done.3.right_ref = bf16[80,128]{1,0:T(8,128)(2,1)S(1)} collective-permute-done((bf16[80,128]{1,0:T(8,128)(2,1)S(1)}, bf16[80,128]{1,0:T(8,128)(2,1)S(1)}, u32[]{:S(2)}, u32[]{:S(2)}) %collective-permute-start.3) | collective-permute-done | bytes 20512 | tf_op jit(solution)/shard_map/ppermute | solution.py:300
  26.9 3.5 %collective-permute-done.2.left_ref = bf16[80,128]{1,0:T(8,128)(2,1)S(1)} collective-permute-done((bf16[80,128]{1,0:T(8,128)(2,1)S(1)}, bf16[80,128]{1,0:T(8,128)(2,1)S(1)}, u32[]{:S(2)}, u32[]{:S(2)}) %collective-permute-start.2) | collective-permute-done | bytes 20512 | tf_op jit(solution)/shard_map/ppermute | solution.py:300
  30.4 0.0 all-to-all-done
  30.4 0.0 copy-done
  30.4 8.0 %interpolate.1 = bf16[2048,128]{1,0:T(8,128)(2,1)} custom-call(f32[128,128]{1,0:T(8,128)S(1)} %bitcast.25, bf16[4096,128]{1,0:T(8,128)(2,1)S(1)} %bitcast.23, bf16[64,128]{1,0:T(8,128)(2,1)S(1)} %collective-permute-done.top_ref, bf16[64,128]{1,0:T(8,128)(2,1)S(1)} %collective-permute-done.1.bottom_ref, bf16[80,128]{1,0:T(8,128)(2,1)S(1)} %collective-permute-done.2.left_ref, ...), custom_call_target="tpu_custom_call" | custom-call | tf_op jit(solution)/shard_map/interpolate/pallas_call | solution.py:32
  38.4 7.3 %all-to-all-start.1 = ((bf16[128,16,128]{2,1,0:T(8,128)(2,1)}), bf16[128,16,128]{2,1,0:T(8,128)(2,1)S(1)}, u32[]{:S(2)}, u32[]{:S(2)}) async-start(bf16[128,16,128]{2,1,0:T(8,128)(2,1)} %bitcast.30), calls=%async_computation.1 | async-start | bytes 1048576 | tf_op jit(solution)/shard_map/all_to_all | solution.py:304
  45.8 0.0 copy-done.1
  45.8 0.0 copy-start.2
  45.8 0.0 copy-start.3
  45.8 0.0 copy-start.4
  45.8 15.6 %components.1.pcs_ref = bf16[1024,256]{1,0:T(8,128)(2,1)S(1)} custom-call(bf16[1024,8448]{1,0:T(8,128)(2,1)} %spectra_ref.1, bf16[8448,256]{1,0:T(8,128)(2,1)} %basis_ref.1, s32[1,1024]{1,0:T(1,128)S(1)} %copy-done.1), custom_call_target="tpu_custom_call" | custom-call | tf_op jit(solution)/shard_map/components/pallas_call | solution.py:32
  61.4 0.0 all-to-all-done.1
  61.4 0.0 copy-done.2
  61.4 0.0 copy-done.3
  61.4 0.0 copy-done.4
  61.4 6.7 %network.1 = (bf16[1024,256]{1,0:T(8,128)(2,1)}, bf16[2048,128]{1,0:T(8,128)(2,1)}) custom-call(bf16[2048,128]{1,0:T(8,128)(2,1)S(1)} %bitcast.24, s32[1,1024]{1,0:T(1,128)S(1)} %copy-done.1, bf16[1024,256]{1,0:T(8,128)(2,1)S(1)} %components.1.pcs_ref, f32[1,256]{1,0:T(1,128)S(1)} %bitcast.28, bf16[128,512]{1,0:T(8,128)(2,1)} %w_in_hbm.1, ...), custom_call_target="tpu_custom_call" | custom-call | tf_op jit(solution)/shard_map/network/pallas_call | solution.py:32
  68.2 9.8 %all-to-all-start.2 = ((bf16[128,16,128]{2,1,0:T(8,128)(2,1)}), bf16[128,16,128]{2,1,0:T(8,128)(2,1)S(1)}, u32[]{:S(2)}, u32[]{:S(2)}) async-start(bf16[128,16,128]{2,1,0:T(8,128)(2,1)} %bitcast.31), calls=%async_computation.2 | async-start | bytes 1048576 | tf_op jit(solution)/shard_map/all_to_all | solution.py:304
  77.9 0.5 prepare.1.fields_ref
  78.4 11.8 %all-to-all-done.2 = bf16[128,16,128]{2,1,0:T(8,128)(2,1)S(1)} async-done(((bf16[128,16,128]{2,1,0:T(8,128)(2,1)}), bf16[128,16,128]{2,1,0:T(8,128)(2,1)S(1)}, u32[]{:S(2)}, u32[]{:S(2)}) %all-to-all-start.2) | async-done | bytes 524320 | tf_op jit(solution)/shard_map/all_to_all | solution.py:304
  90.2 0.5 adjoint_rim.1
  90.7 0.6 collective-permute-start.4
  91.3 2.7 %collective-permute-start.5 = (bf16[80,128]{1,0:T(8,128)(2,1)S(1)}, bf16[80,128]{1,0:T(8,128)(2,1)S(1)}, u32[]{:S(2)}, u32[]{:S(2)}) collective-permute-start(bf16[80,128]{1,0:T(8,128)(2,1)S(1)} %get-tuple-element.32), channel_id=1, source_target_pairs={{0,3},{1,0},{2,1},{3,2},{4,7},{5,4},{6,5},{7,6},{8,11},{9,8},{10,9... | collective-permute-start | bytes 61448 | tf_op jit(solution)/shard_map/ppermute | solution.py:300
  94.0 1.8 %collective-permute-done.4.left_ref = bf16[80,128]{1,0:T(8,128)(2,1)S(1)} collective-permute-done((bf16[80,128]{1,0:T(8,128)(2,1)S(1)}, bf16[80,128]{1,0:T(8,128)(2,1)S(1)}, u32[]{:S(2)}, u32[]{:S(2)}) %collective-permute-start.4) | collective-permute-done | bytes 20512 | tf_op jit(solution)/shard_map/ppermute | solution.py:300
  95.7 0.0 collective-permute-done.5.right_ref
  95.8 1.9 %collective-permute-start.6 = (bf16[64,128]{1,0:T(8,128)(2,1)S(1)}, bf16[64,128]{1,0:T(8,128)(2,1)S(1)}, u32[]{:S(2)}, u32[]{:S(2)}) collective-permute-start(bf16[64,128]{1,0:T(8,128)(2,1)S(1)} %get-tuple-element.37), channel_id=1, source_target_pairs={{0,4},{4,8},{8,12},{12,16},{16,20},{20,24},{24,28},{28,32},{32,36}... | collective-permute-start | bytes 49160 | tf_op jit(solution)/shard_map/ppermute | solution.py:300
  97.7 6.0 %collective-permute-start.7 = (bf16[64,128]{1,0:T(8,128)(2,1)S(1)}, bf16[64,128]{1,0:T(8,128)(2,1)S(1)}, u32[]{:S(2)}, u32[]{:S(2)}) collective-permute-start(bf16[64,128]{1,0:T(8,128)(2,1)S(1)} %get-tuple-element.38), channel_id=1, source_target_pairs={{4,0},{8,4},{12,8},{16,12},{20,16},{24,20},{28,24},{32,28},{36,32}... | collective-permute-start | bytes 49160 | tf_op jit(solution)/shard_map/ppermute | solution.py:300
  103.7 3.3 %adjoint_a.1.refs_0_ = f32[64,64,128]{2,1,0:T(8,128)} custom-call(f32[8,2048]{1,0:T(8,128)S(1)} %prepare.1.fields_ref, bf16[2048,128]{1,0:T(8,128)(2,1)S(1)} %bitcast.21), custom_call_target="tpu_custom_call" | custom-call | tf_op jit(solution)/shard_map/adjoint_a/pallas_call | solution.py:32
  107.0 3.3 %adjoint_b.1.grad_ref = f32[64,64,128]{2,1,0:T(8,128)} custom-call(f32[8,2048]{1,0:T(8,128)S(1)} %prepare.1.fields_ref, bf16[2048,128]{1,0:T(8,128)(2,1)S(1)} %bitcast.22, f32[64,64,128]{2,1,0:T(8,128)} %adjoint_a.1.refs_0_), custom_call_target="tpu_custom_call", output_to_operand_aliasing={{}: (2, {})} | custom-call | tf_op jit(solution)/shard_map/adjoint_b/pallas_call | solution.py:32
  110.3 0.0 collective-permute-done.6.above_ref
  110.3 0.0 collective-permute-done.7.below_ref
  110.3 2.0 %edges.1 = f32[64,64,128]{2,1,0:T(8,128)} custom-call(bf16[80,128]{1,0:T(8,128)(2,1)S(1)} %collective-permute-done.4.left_ref, bf16[80,128]{1,0:T(8,128)(2,1)S(1)} %collective-permute-done.5.right_ref, bf16[64,128]{1,0:T(8,128)(2,1)S(1)} %collective-permute-done.6.above_ref, ...), custom_call_target="tpu_custom_call", output_to_operand_aliasing={{}: (4, {})} | custom-call | tf_op jit(solution)/shard_map/edges/pallas_call | solution.py:32
  (4 shorter events, 0.0 us)
Async XLA Ops:
  0.6 29.8 %copy-start = (bf16[64,64,128]{2,1,0:T(8,128)(2,1)S(1)}, bf16[64,64,128]{2,1,0:T(8,128)(2,1)}, u32[]{:S(2)}) copy-start(bf16[64,64,128]{2,1,0:T(8,128)(2,1)} %state_ref.1) | copy-start | bytes 3145732
  1.5 20.3 %collective-permute-start.1 = (bf16[64,128]{1,0:T(8,128)(2,1)S(1)}, bf16[64,128]{1,0:T(8,128)(2,1)S(1)}, u32[]{:S(2)}, u32[]{:S(2)}) collective-permute-start(bf16[64,128]{1,0:T(8,128)(2,1)S(1)} %get-tuple-element.40), channel_id=1, source_target_pairs={{4,0},{8,4},{12,8},{16,12},{20,16},{24,20},{28,24},{32,28},{36,32}... | collective-permute-start | bytes 49160 | tf_op jit(solution)/shard_map/ppermute | solution.py:300
  7.1 14.6 %collective-permute-start = (bf16[64,128]{1,0:T(8,128)(2,1)S(1)}, bf16[64,128]{1,0:T(8,128)(2,1)S(1)}, u32[]{:S(2)}, u32[]{:S(2)}) collective-permute-start(bf16[64,128]{1,0:T(8,128)(2,1)S(1)} %get-tuple-element.41), channel_id=1, source_target_pairs={{0,4},{4,8},{8,12},{12,16},{16,20},{20,24},{24,28},{28,32},{32,36}... | collective-permute-start | bytes 49160 | tf_op jit(solution)/shard_map/ppermute | solution.py:300
  11.6 34.1 %copy-start.1 = (s32[1,1024]{1,0:T(1,128)S(1)}, s32[1,1024]{1,0:T(1,128)}, u32[]{:S(2)}) copy-start(s32[1,1024]{1,0:T(1,128)} %get-tuple-element.26.place_ref) | copy-start | bytes 12292
  11.6 18.8 %all-to-all-start = ((f32[128,1,128]{2,1,0:T(1,128)}), f32[128,1,128]{2,1,0:T(1,128)S(1)}, u32[]{:S(2)}, u32[]{:S(2)}) async-start(f32[128,1,128]{2,1,0:T(1,128)} %bitcast.32), calls=%async_computation | async-start | bytes 131072 | tf_op jit(solution)/shard_map/all_to_all | solution.py:304
  22.6 4.3 %collective-permute-start.3 = (bf16[80,128]{1,0:T(8,128)(2,1)S(1)}, bf16[80,128]{1,0:T(8,128)(2,1)S(1)}, u32[]{:S(2)}, u32[]{:S(2)}) collective-permute-start(bf16[80,128]{1,0:T(8,128)(2,1)S(1)} %get-tuple-element.46), channel_id=1, source_target_pairs={{0,3},{1,0},{2,1},{3,2},{4,7},{5,4},{6,5},{7,6},{8,11},{9,8},{10,9... | collective-permute-start | bytes 61448 | tf_op jit(solution)/shard_map/ppermute | solution.py:300
  25.4 5.0 %collective-permute-start.2 = (bf16[80,128]{1,0:T(8,128)(2,1)S(1)}, bf16[80,128]{1,0:T(8,128)(2,1)S(1)}, u32[]{:S(2)}, u32[]{:S(2)}) collective-permute-start(bf16[80,128]{1,0:T(8,128)(2,1)S(1)} %get-tuple-element.47), channel_id=1, source_target_pairs={{0,1},{1,2},{2,3},{3,0},{4,5},{5,6},{6,7},{7,4},{8,9},{9,10},{10,1... | collective-permute-start | bytes 61448 | tf_op jit(solution)/shard_map/ppermute | solution.py:300
  38.4 23.0 %all-to-all-start.1 = ((bf16[128,16,128]{2,1,0:T(8,128)(2,1)}), bf16[128,16,128]{2,1,0:T(8,128)(2,1)S(1)}, u32[]{:S(2)}, u32[]{:S(2)}) async-start(bf16[128,16,128]{2,1,0:T(8,128)(2,1)} %bitcast.30), calls=%async_computation.1 | async-start | bytes 1048576 | tf_op jit(solution)/shard_map/all_to_all | solution.py:304
  45.8 15.6 %copy-start.2 = (f32[512]{0:T(512)S(1)}, f32[512]{0:T(512)}, u32[]{:S(2)}) copy-start(f32[512]{0:T(512)} %param.21) | copy-start | bytes 6148
  45.8 15.6 %copy-start.3 = (f32[256]{0:T(256)S(1)}, f32[256]{0:T(256)}, u32[]{:S(2)}) copy-start(f32[256]{0:T(256)} %param.19) | copy-start | bytes 3076
  45.8 15.6 %copy-start.4 = (f32[256]{0:T(256)S(1)}, f32[256]{0:T(256)}, u32[]{:S(2)}) copy-start(f32[256]{0:T(256)} %param.23) | copy-start | bytes 3076
  68.2 22.0 %all-to-all-start.2 = ((bf16[128,16,128]{2,1,0:T(8,128)(2,1)}), bf16[128,16,128]{2,1,0:T(8,128)(2,1)S(1)}, u32[]{:S(2)}, u32[]{:S(2)}) async-start(bf16[128,16,128]{2,1,0:T(8,128)(2,1)} %bitcast.31), calls=%async_computation.2 | async-start | bytes 1048576 | tf_op jit(solution)/shard_map/all_to_all | solution.py:304
  90.7 5.1 %collective-permute-start.4 = (bf16[80,128]{1,0:T(8,128)(2,1)S(1)}, bf16[80,128]{1,0:T(8,128)(2,1)S(1)}, u32[]{:S(2)}, u32[]{:S(2)}) collective-permute-start(bf16[80,128]{1,0:T(8,128)(2,1)S(1)} %get-tuple-element.31), channel_id=1, source_target_pairs={{0,1},{1,2},{2,3},{3,0},{4,5},{5,6},{6,7},{7,4},{8,9},{9,10},{10,1... | collective-permute-start | bytes 61448 | tf_op jit(solution)/shard_map/ppermute | solution.py:300
  91.3 4.4 %collective-permute-start.5 = (bf16[80,128]{1,0:T(8,128)(2,1)S(1)}, bf16[80,128]{1,0:T(8,128)(2,1)S(1)}, u32[]{:S(2)}, u32[]{:S(2)}) collective-permute-start(bf16[80,128]{1,0:T(8,128)(2,1)S(1)} %get-tuple-element.32), channel_id=1, source_target_pairs={{0,3},{1,0},{2,1},{3,2},{4,7},{5,4},{6,5},{7,6},{8,11},{9,8},{10,9... | collective-permute-start | bytes 61448 | tf_op jit(solution)/shard_map/ppermute | solution.py:300
  95.8 14.5 %collective-permute-start.6 = (bf16[64,128]{1,0:T(8,128)(2,1)S(1)}, bf16[64,128]{1,0:T(8,128)(2,1)S(1)}, u32[]{:S(2)}, u32[]{:S(2)}) collective-permute-start(bf16[64,128]{1,0:T(8,128)(2,1)S(1)} %get-tuple-element.37), channel_id=1, source_target_pairs={{0,4},{4,8},{8,12},{12,16},{16,20},{20,24},{24,28},{28,32},{32,36}... | collective-permute-start | bytes 49160 | tf_op jit(solution)/shard_map/ppermute | solution.py:300
  97.7 12.6 %collective-permute-start.7 = (bf16[64,128]{1,0:T(8,128)(2,1)S(1)}, bf16[64,128]{1,0:T(8,128)(2,1)S(1)}, u32[]{:S(2)}, u32[]{:S(2)}) collective-permute-start(bf16[64,128]{1,0:T(8,128)(2,1)S(1)} %get-tuple-element.38), channel_id=1, source_target_pairs={{4,0},{8,4},{12,8},{16,12},{20,16},{24,20},{28,24},{32,28},{36,32}... | collective-permute-start | bytes 49160 | tf_op jit(solution)/shard_map/ppermute | solution.py:300

commit v3 on v2

--- a/solution.py
+++ b/solution.py
@@ -41,9 +41,11 @@
     )(*args)
 
 
-def route_body(dest_ref, row_ref, col_ref, weight_ref, state_ref, send_ref, place_ref, first_ref, last_ref):
+def route_body(dest_ref, row_ref, col_ref, weight_ref, state_ref, send_ref, place_ref, first_ref, last_ref, head_ref, tail_ref):
     first_ref[...] = state_ref[:, 0, :]
     last_ref[...] = state_ref[:, 63, :]
+    head_ref[...] = state_ref[0]
+    tail_ref[...] = state_ref[63]
     dest = dest_ref[...]
     tiles = send_ref.shape[0]
     obs = dest.shape[1]
@@ -138,17 +140,29 @@
     obs = spectra_ref.shape[0]
     blocks = buffer.shape[0]
     rows = obs // blocks
+
+    def load(i):
+        at = pl.ds(pl.multiple_of(i * rows, rows), rows)
+        return pltpu.make_async_copy(spectra_ref.at[at, :], buffer.at[i], sems.at[i])
+
     basis = pltpu.make_async_copy(basis_ref, basis_buffer, basis_sem)
     basis.start()
-    copies = [
-        pltpu.make_async_copy(spectra_ref.at[pl.ds(i * rows, rows), :], buffer.at[i], sems.at[i]) for i in range(blocks)
-    ]
-    for copy in copies:
-        copy.start()
+    load(0).start()
+    load(1).start()
     basis.wait()
-    for i, copy in enumerate(copies):
-        copy.wait()
-        pcs_ref[i * rows : i * rows + rows, :] = mm(buffer[i], basis_buffer[...]).astype(BF16)
+
+    def step(i, carry):
+        load(i).wait()
+
+        @pl.when(i + 2 < blocks)
+        def _():
+            load(i + 2).start()
+
+        at = pl.ds(pl.multiple_of(i * rows, rows), rows)
+        pcs_ref[at, :] = mm(buffer[i], basis_buffer[...]).astype(BF16)
+        return carry
+
+    lax.fori_loop(0, blocks, step, 0)
 
 
 def network_body(recv_ref, place_ref, pcs_ref, inv_ref, w_in_hbm, b_in_ref, w_out_hbm, b_out_ref, dep_ref, send_ref, pack_ref, unpack_ref, w_in_ref, w_out_ref, g_ref, dep_buffer, send_buffer, w_sems, dep_sems, send_sems):
@@ -325,11 +339,9 @@
     slots = tiles * CAP
     sds = jax.ShapeDtypeStruct
 
-    top = shift(state[63], "lat", 1, False)
-    bottom = shift(state[0], "lat", -1, False)
-    send_meta, place, first, last = call(
+    send_meta, place, first, last, head, tail = call(
         route_body,
-        (sds((tiles, 128), F32), sds((1, obs), I32), sds((64, levels), BF16), sds((64, levels), BF16)),
+        (pltpu.HBM((tiles, 128), F32), sds((1, obs), I32)) + (sds((64, levels), BF16),) * 4,
         "route",
         destination.reshape(1, obs),
         corner_row.reshape(1, obs),
@@ -339,7 +351,8 @@
         grant=None,
     )
     recv_meta = exchange(send_meta)
-
+    top = shift(tail, "lat", 1, False)
+    bottom = shift(head, "lat", -1, False)
     fill = jnp.zeros((14, levels), BF16)
     left = shift(jnp.concatenate([last, top[63:], bottom[63:], fill], 0), "lon", 1, True)
     right = shift(jnp.concatenate([first, top[:1], bottom[:1], fill], 0), "lon", -1, True)
@@ -430,6 +443,7 @@
         scratch=half,
         grant=14,
     )
+    from_left, from_right, gradient = lax.optimization_barrier((from_left, from_right, gradient))
     up, down = call(
         corner_body,
         (sds((64, levels), BF16), sds((64, levels), BF16)),

time: 114 us -> 105 us (0.921)
  Pallas kernels: 42.4 us -> 35.8 us
  starting transfers between devices: 48.7 us -> 42.8 us
  waiting for transfers between devices: 18.6 us -> 22.4 us
    pallas_call x10, Pallas kernels: 42.4 us -> 35.8 us  [call(): pl.pallas_call(body, in_specs=specs or [vmem] * len(args), out_specs=outs...]
    all_to_all x3, starting transfers between devices: 27.1 us -> 20.9 us  [exchange(): return lax.all_to_all(x, AXES, split_axis=0, concat_axis=0, tiled=True)]
    all_to_all x3, waiting for transfers between devices: 11.8 us -> 15.1 us  [exchange(): return lax.all_to_all(x, AXES, split_axis=0, concat_axis=0, tiled=True)]
    unnamed x10, local copies, waits for them, and re-layouts: 0.03 us -> 1.25 us
  transfers between devices with their start and end apart: 11 -> 11, of which waited for: 4 -> 5; matrix products, arithmetic and copies ran while one was open for 1% -> 1% of each run, Pallas kernels for 22% -> 15%
where the time goes in v3:
time: 105 us; the launch traced here: 104 us
  starting transfers between devices  42.8 us (41%)
  Pallas kernels  35.8 us (34%)
  waiting for transfers between devices  22.4 us (21%)
  local copies, waits for them, and re-layouts  1.34 us (1%)
    pallas_call x10, Pallas kernels, call(): pl.pallas_call(body, in_specs=specs or [vmem] * len(args), out_specs=outs...  35.8 us
    ppermute x8, starting transfers between devices, shift(): return lax.ppermute(x, axis, pairs)  22 us
    all_to_all x3, starting transfers between devices, exchange(): return lax.all_to_all(x, AXES, split_axis=0, concat_axis=0, tiled=True)  20.9 us
    all_to_all x3, waiting for transfers between devices, exchange(): return lax.all_to_all(x, AXES, split_axis=0, concat_axis=0, tiled=True)  15.1 us
    ppermute x8, waiting for transfers between devices, shift(): return lax.ppermute(x, axis, pairs)  7.28 us
  transfers between devices with their start and end apart: 11, of which 5 were waited for; matrix products, arithmetic and copies ran while one was open for 1% of the time, Pallas kernels for 15%

profile of v3, /device:TPU:6, one launch (start us, length us, event | category | flops | bytes accessed | tf_op | source)
XLA Modules:
  0.0 104.1 jit_solution(17784322337209456611)
XLA Ops:
  0.6 2.6 %route.1 = (f32[128,128]{1,0:T(8,128)}, s32[1,1024]{1,0:T(1,128)}, bf16[64,128]{1,0:T(8,128)(2,1)}, bf16[64,128]{1,0:T(8,128)(2,1)}, bf16[64,128]{1,0:T(8,128)(2,1)}, /*index=5*/bf16[64,128]{1,0:T(8,128)(2,1)}) custom-call(s32[1,1024]{1,0:T(1,128)} %bitcast.30, s32[1,1024]{1,0:T(1,128)} %bitcast.31, s32[1,1024]{1,0:T(1,128)} %bitcast.32, ...), custom_call_target="tpu_custom_call" | custom-call | tf_op jit(solution)/shard_map/route/pallas_call | solution.py:32
  3.2 0.0 copy-start.1
  3.2 5.7 %collective-permute-start.1 = (bf16[64,128]{1,0:T(8,128)(2,1)}, bf16[64,128]{1,0:T(8,128)(2,1)S(1)}, u32[]{:S(2)}, u32[]{:S(2)}) collective-permute-start(bf16[64,128]{1,0:T(8,128)(2,1)} %get-tuple-element.28), channel_id=1, source_target_pairs={{4,0},{8,4},{12,8},{16,12},{20,16},{24,20},{28,24},{32,28},{36,32}... | collective-permute-start | bytes 49160 | tf_op jit(solution)/shard_map/ppermute | solution.py:314
  8.9 6.9 %all-to-all-start = ((f32[128,1,128]{2,1,0:T(1,128)}), f32[128,1,128]{2,1,0:T(1,128)S(1)}, u32[]{:S(2)}, u32[]{:S(2)}) async-start(f32[128,1,128]{2,1,0:T(1,128)} %bitcast.28), calls=%async_computation | async-start | bytes 131072 | tf_op jit(solution)/shard_map/all_to_all | solution.py:318
  15.7 2.0 %collective-permute-start = (bf16[64,128]{1,0:T(8,128)(2,1)}, bf16[64,128]{1,0:T(8,128)(2,1)S(1)}, u32[]{:S(2)}, u32[]{:S(2)}) collective-permute-start(bf16[64,128]{1,0:T(8,128)(2,1)} %get-tuple-element.27), channel_id=1, source_target_pairs={{0,4},{4,8},{8,12},{12,16},{16,20},{20,24},{24,28},{28,32},{32,36}... | collective-permute-start | bytes 49160 | tf_op jit(solution)/shard_map/ppermute | solution.py:314
  17.8 0.1 pad.7.clone
  17.8 0.0 collective-permute-done.1.bottom_ref
  17.9 5.3 %collective-permute-done.top_ref = bf16[64,128]{1,0:T(8,128)(2,1)S(1)} collective-permute-done((bf16[64,128]{1,0:T(8,128)(2,1)}, bf16[64,128]{1,0:T(8,128)(2,1)S(1)}, u32[]{:S(2)}, u32[]{:S(2)}) %collective-permute-start) | collective-permute-done | bytes 16416 | tf_op jit(solution)/shard_map/ppermute | solution.py:314
  23.2 0.8 maximum_maximum_fusion.1
  24.0 1.5 %collective-permute-start.2 = (bf16[80,128]{1,0:T(8,128)(2,1)S(1)}, bf16[80,128]{1,0:T(8,128)(2,1)S(1)}, u32[]{:S(2)}, u32[]{:S(2)}) collective-permute-start(bf16[80,128]{1,0:T(8,128)(2,1)S(1)} %get-tuple-element.55), channel_id=1, source_target_pairs={{0,1},{1,2},{2,3},{3,0},{4,5},{5,6},{6,7},{7,4},{8,9},{9,10},{10,1... | collective-permute-start | bytes 61448 | tf_op jit(solution)/shard_map/ppermute | solution.py:314
  25.5 1.8 %collective-permute-start.3 = (bf16[80,128]{1,0:T(8,128)(2,1)S(1)}, bf16[80,128]{1,0:T(8,128)(2,1)S(1)}, u32[]{:S(2)}, u32[]{:S(2)}) collective-permute-start(bf16[80,128]{1,0:T(8,128)(2,1)S(1)} %get-tuple-element.54), channel_id=1, source_target_pairs={{0,3},{1,0},{2,1},{3,2},{4,7},{5,4},{6,5},{7,6},{8,11},{9,8},{10,9... | collective-permute-start | bytes 61448 | tf_op jit(solution)/shard_map/ppermute | solution.py:314
  27.3 1.8 %collective-permute-done.2.left_ref = bf16[80,128]{1,0:T(8,128)(2,1)S(1)} collective-permute-done((bf16[80,128]{1,0:T(8,128)(2,1)S(1)}, bf16[80,128]{1,0:T(8,128)(2,1)S(1)}, u32[]{:S(2)}, u32[]{:S(2)}) %collective-permute-start.2) | collective-permute-done | bytes 20512 | tf_op jit(solution)/shard_map/ppermute | solution.py:314
  29.0 0.2 collective-permute-done.3.right_ref
  29.3 0.0 all-to-all-done
  29.3 0.0 copy-start
  29.3 1.2 %copy-done = bf16[64,64,128]{2,1,0:T(8,128)(2,1)S(1)} copy-done((bf16[64,64,128]{2,1,0:T(8,128)(2,1)S(1)}, bf16[64,64,128]{2,1,0:T(8,128)(2,1)}, u32[]{:S(2)}) %copy-start) | copy-done | bytes 1048600
  30.5 8.0 %interpolate.1 = bf16[2048,128]{1,0:T(8,128)(2,1)} custom-call(f32[128,128]{1,0:T(8,128)S(1)} %bitcast.21, bf16[4096,128]{1,0:T(8,128)(2,1)S(1)} %bitcast.19, bf16[64,128]{1,0:T(8,128)(2,1)S(1)} %collective-permute-done.top_ref, bf16[64,128]{1,0:T(8,128)(2,1)S(1)} %collective-permute-done.1.bottom_ref, bf16[80,128]{1,0:T(8,128)(2,1)S(1)} %collective-permute-done.2.left_ref, ...), custom_call_target="tpu_custom_call" | custom-call | tf_op jit(solution)/shard_map/interpolate/pallas_call | solution.py:32
  38.5 7.5 %all-to-all-start.1 = ((bf16[128,16,128]{2,1,0:T(8,128)(2,1)}), bf16[128,16,128]{2,1,0:T(8,128)(2,1)S(1)}, u32[]{:S(2)}, u32[]{:S(2)}) async-start(bf16[128,16,128]{2,1,0:T(8,128)(2,1)} %bitcast.26), calls=%async_computation.1 | async-start | bytes 1048576 | tf_op jit(solution)/shard_map/all_to_all | solution.py:318
  46.0 0.0 copy-done.1
  46.0 0.0 copy-start.2
  46.0 0.0 copy-start.3
  46.1 0.0 copy-start.4
  46.1 8.9 %components.1.pcs_ref = bf16[1024,256]{1,0:T(8,128)(2,1)S(1)} custom-call(bf16[1024,8448]{1,0:T(8,128)(2,1)} %spectra_ref.1, bf16[8448,256]{1,0:T(8,128)(2,1)} %basis_ref.1, s32[1,1024]{1,0:T(1,128)S(1)} %copy-done.1), custom_call_target="tpu_custom_call" | custom-call | tf_op jit(solution)/shard_map/components/pallas_call | solution.py:32
  54.9 3.3 %all-to-all-done.1 = bf16[128,16,128]{2,1,0:T(8,128)(2,1)S(1)} async-done(((bf16[128,16,128]{2,1,0:T(8,128)(2,1)}), bf16[128,16,128]{2,1,0:T(8,128)(2,1)S(1)}, u32[]{:S(2)}, u32[]{:S(2)}) %all-to-all-start.1) | async-done | bytes 524320 | tf_op jit(solution)/shard_map/all_to_all | solution.py:318
  58.3 0.0 copy-done.2
  58.3 0.0 copy-done.3
  58.3 0.0 copy-done.4
  58.3 6.8 %network.1 = (bf16[1024,256]{1,0:T(8,128)(2,1)}, bf16[2048,128]{1,0:T(8,128)(2,1)}) custom-call(bf16[2048,128]{1,0:T(8,128)(2,1)S(1)} %bitcast.20, s32[1,1024]{1,0:T(1,128)S(1)} %copy-done.1, bf16[1024,256]{1,0:T(8,128)(2,1)S(1)} %components.1.pcs_ref, f32[1,256]{1,0:T(1,128)S(1)} %bitcast.24, bf16[128,512]{1,0:T(8,128)(2,1)} %w_in_hbm.1, ...), custom_call_target="tpu_custom_call" | custom-call | tf_op jit(solution)/shard_map/network/pallas_call | solution.py:32
  65.1 6.5 %all-to-all-start.2 = ((bf16[128,16,128]{2,1,0:T(8,128)(2,1)}), bf16[128,16,128]{2,1,0:T(8,128)(2,1)S(1)}, u32[]{:S(2)}, u32[]{:S(2)}) async-start(bf16[128,16,128]{2,1,0:T(8,128)(2,1)} %bitcast.27), calls=%async_computation.2 | async-start | bytes 1048576 | tf_op jit(solution)/shard_map/all_to_all | solution.py:318
  71.5 0.5 prepare.1.fields_ref
  72.0 11.8 %all-to-all-done.2 = bf16[128,16,128]{2,1,0:T(8,128)(2,1)S(1)} async-done(((bf16[128,16,128]{2,1,0:T(8,128)(2,1)}), bf16[128,16,128]{2,1,0:T(8,128)(2,1)S(1)}, u32[]{:S(2)}, u32[]{:S(2)}) %all-to-all-start.2) | async-done | bytes 524320 | tf_op jit(solution)/shard_map/all_to_all | solution.py:318
  83.8 0.5 adjoint_rim.1
  84.3 0.6 collective-permute-start.4
  84.9 2.7 %collective-permute-start.5 = (bf16[80,128]{1,0:T(8,128)(2,1)S(1)}, bf16[80,128]{1,0:T(8,128)(2,1)S(1)}, u32[]{:S(2)}, u32[]{:S(2)}) collective-permute-start(bf16[80,128]{1,0:T(8,128)(2,1)S(1)} %get-tuple-element.39), channel_id=1, source_target_pairs={{0,3},{1,0},{2,1},{3,2},{4,7},{5,4},{6,5},{7,6},{8,11},{9,8},{10,9... | collective-permute-start | bytes 61448 | tf_op jit(solution)/shard_map/ppermute | solution.py:314
  87.6 3.3 %adjoint_a.1.refs_0_ = f32[64,64,128]{2,1,0:T(8,128)} custom-call(f32[8,2048]{1,0:T(8,128)S(1)} %prepare.1.fields_ref, bf16[2048,128]{1,0:T(8,128)(2,1)S(1)} %bitcast.17), custom_call_target="tpu_custom_call" | custom-call | tf_op jit(solution)/shard_map/adjoint_a/pallas_call | solution.py:32
  90.9 0.0 collective-permute-done.4.left_ref
  90.9 0.0 collective-permute-done.5.right_ref
  90.9 1.9 %collective-permute-start.6 = (bf16[64,128]{1,0:T(8,128)(2,1)S(1)}, bf16[64,128]{1,0:T(8,128)(2,1)S(1)}, u32[]{:S(2)}, u32[]{:S(2)}) collective-permute-start(bf16[64,128]{1,0:T(8,128)(2,1)S(1)} %get-tuple-element.46), channel_id=1, source_target_pairs={{0,4},{4,8},{8,12},{12,16},{16,20},{20,24},{24,28},{28,32},{32,36}... | collective-permute-start | bytes 49160 | tf_op jit(solution)/shard_map/ppermute | solution.py:314
  92.9 5.8 %collective-permute-start.7 = (bf16[64,128]{1,0:T(8,128)(2,1)S(1)}, bf16[64,128]{1,0:T(8,128)(2,1)S(1)}, u32[]{:S(2)}, u32[]{:S(2)}) collective-permute-start(bf16[64,128]{1,0:T(8,128)(2,1)S(1)} %get-tuple-element.47), channel_id=1, source_target_pairs={{4,0},{8,4},{12,8},{16,12},{20,16},{24,20},{28,24},{32,28},{36,32}... | collective-permute-start | bytes 49160 | tf_op jit(solution)/shard_map/ppermute | solution.py:314
  98.6 3.3 %adjoint_b.1.grad_ref = f32[64,64,128]{2,1,0:T(8,128)} custom-call(f32[8,2048]{1,0:T(8,128)S(1)} %prepare.1.fields_ref, bf16[2048,128]{1,0:T(8,128)(2,1)S(1)} %bitcast.18, f32[64,64,128]{2,1,0:T(8,128)} %adjoint_a.1.refs_0_), custom_call_target="tpu_custom_call", output_to_operand_aliasing={{}: (2, {})} | custom-call | tf_op jit(solution)/shard_map/adjoint_b/pallas_call | solution.py:32
  101.9 0.0 collective-permute-done.6.above_ref
  102.0 0.0 collective-permute-done.7.below_ref
  102.0 2.0 %edges.1 = f32[64,64,128]{2,1,0:T(8,128)} custom-call(bf16[80,128]{1,0:T(8,128)(2,1)S(1)} %collective-permute-done.4.left_ref, bf16[80,128]{1,0:T(8,128)(2,1)S(1)} %collective-permute-done.5.right_ref, bf16[64,128]{1,0:T(8,128)(2,1)S(1)} %collective-permute-done.6.above_ref, ...), custom_call_target="tpu_custom_call", output_to_operand_aliasing={{}: (4, {})} | custom-call | tf_op jit(solution)/shard_map/edges/pallas_call | solution.py:32
  (4 shorter events, 0.0 us)
Async XLA Ops:
  3.2 42.8 %copy-start.1 = (s32[1,1024]{1,0:T(1,128)S(1)}, s32[1,1024]{1,0:T(1,128)}, u32[]{:S(2)}) copy-start(s32[1,1024]{1,0:T(1,128)} %get-tuple-element.33.place_ref) | copy-start | bytes 12292
  3.2 14.6 %collective-permute-start.1 = (bf16[64,128]{1,0:T(8,128)(2,1)}, bf16[64,128]{1,0:T(8,128)(2,1)S(1)}, u32[]{:S(2)}, u32[]{:S(2)}) collective-permute-start(bf16[64,128]{1,0:T(8,128)(2,1)} %get-tuple-element.28), channel_id=1, source_target_pairs={{4,0},{8,4},{12,8},{16,12},{20,16},{24,20},{28,24},{32,28},{36,32}... | collective-permute-start | bytes 49160 | tf_op jit(solution)/shard_map/ppermute | solution.py:314
  8.9 20.4 %all-to-all-start = ((f32[128,1,128]{2,1,0:T(1,128)}), f32[128,1,128]{2,1,0:T(1,128)S(1)}, u32[]{:S(2)}, u32[]{:S(2)}) async-start(f32[128,1,128]{2,1,0:T(1,128)} %bitcast.28), calls=%async_computation | async-start | bytes 131072 | tf_op jit(solution)/shard_map/all_to_all | solution.py:318
  15.7 7.4 %collective-permute-start = (bf16[64,128]{1,0:T(8,128)(2,1)}, bf16[64,128]{1,0:T(8,128)(2,1)S(1)}, u32[]{:S(2)}, u32[]{:S(2)}) collective-permute-start(bf16[64,128]{1,0:T(8,128)(2,1)} %get-tuple-element.27), channel_id=1, source_target_pairs={{0,4},{4,8},{8,12},{12,16},{16,20},{20,24},{24,28},{28,32},{32,36}... | collective-permute-start | bytes 49160 | tf_op jit(solution)/shard_map/ppermute | solution.py:314
  24.0 5.1 %collective-permute-start.2 = (bf16[80,128]{1,0:T(8,128)(2,1)S(1)}, bf16[80,128]{1,0:T(8,128)(2,1)S(1)}, u32[]{:S(2)}, u32[]{:S(2)}) collective-permute-start(bf16[80,128]{1,0:T(8,128)(2,1)S(1)} %get-tuple-element.55), channel_id=1, source_target_pairs={{0,1},{1,2},{2,3},{3,0},{4,5},{5,6},{6,7},{7,4},{8,9},{9,10},{10,1... | collective-permute-start | bytes 61448 | tf_op jit(solution)/shard_map/ppermute | solution.py:314
  25.5 3.8 %collective-permute-start.3 = (bf16[80,128]{1,0:T(8,128)(2,1)S(1)}, bf16[80,128]{1,0:T(8,128)(2,1)S(1)}, u32[]{:S(2)}, u32[]{:S(2)}) collective-permute-start(bf16[80,128]{1,0:T(8,128)(2,1)S(1)} %get-tuple-element.54), channel_id=1, source_target_pairs={{0,3},{1,0},{2,1},{3,2},{4,7},{5,4},{6,5},{7,6},{8,11},{9,8},{10,9... | collective-permute-start | bytes 61448 | tf_op jit(solution)/shard_map/ppermute | solution.py:314
  29.3 1.2 %copy-start = (bf16[64,64,128]{2,1,0:T(8,128)(2,1)S(1)}, bf16[64,64,128]{2,1,0:T(8,128)(2,1)}, u32[]{:S(2)}) copy-start(bf16[64,64,128]{2,1,0:T(8,128)(2,1)} %state_ref.1) | copy-start | bytes 3145732
  38.5 19.8 %all-to-all-start.1 = ((bf16[128,16,128]{2,1,0:T(8,128)(2,1)}), bf16[128,16,128]{2,1,0:T(8,128)(2,1)S(1)}, u32[]{:S(2)}, u32[]{:S(2)}) async-start(bf16[128,16,128]{2,1,0:T(8,128)(2,1)} %bitcast.26), calls=%async_computation.1 | async-start | bytes 1048576 | tf_op jit(solution)/shard_map/all_to_all | solution.py:318
  46.0 12.2 %copy-start.2 = (f32[512]{0:T(512)S(1)}, f32[512]{0:T(512)}, u32[]{:S(2)}) copy-start(f32[512]{0:T(512)} %param.21) | copy-start | bytes 6148
  46.0 12.2 %copy-start.3 = (f32[256]{0:T(256)S(1)}, f32[256]{0:T(256)}, u32[]{:S(2)}) copy-start(f32[256]{0:T(256)} %param.19) | copy-start | bytes 3076
  46.1 12.2 %copy-start.4 = (f32[256]{0:T(256)S(1)}, f32[256]{0:T(256)}, u32[]{:S(2)}) copy-start(f32[256]{0:T(256)} %param.23) | copy-start | bytes 3076
  65.1 18.7 %all-to-all-start.2 = ((bf16[128,16,128]{2,1,0:T(8,128)(2,1)}), bf16[128,16,128]{2,1,0:T(8,128)(2,1)S(1)}, u32[]{:S(2)}, u32[]{:S(2)}) async-start(bf16[128,16,128]{2,1,0:T(8,128)(2,1)} %bitcast.27), calls=%async_computation.2 | async-start | bytes 1048576 | tf_op jit(solution)/shard_map/all_to_all | solution.py:318
  84.3 6.6 %collective-permute-start.4 = (bf16[80,128]{1,0:T(8,128)(2,1)S(1)}, bf16[80,128]{1,0:T(8,128)(2,1)S(1)}, u32[]{:S(2)}, u32[]{:S(2)}) collective-permute-start(bf16[80,128]{1,0:T(8,128)(2,1)S(1)} %get-tuple-element.38), channel_id=1, source_target_pairs={{0,1},{1,2},{2,3},{3,0},{4,5},{5,6},{6,7},{7,4},{8,9},{9,10},{10,1... | collective-permute-start | bytes 61448 | tf_op jit(solution)/shard_map/ppermute | solution.py:314
  84.9 6.0 %collective-permute-start.5 = (bf16[80,128]{1,0:T(8,128)(2,1)S(1)}, bf16[80,128]{1,0:T(8,128)(2,1)S(1)}, u32[]{:S(2)}, u32[]{:S(2)}) collective-permute-start(bf16[80,128]{1,0:T(8,128)(2,1)S(1)} %get-tuple-element.39), channel_id=1, source_target_pairs={{0,3},{1,0},{2,1},{3,2},{4,7},{5,4},{6,5},{7,6},{8,11},{9,8},{10,9... | collective-permute-start | bytes 61448 | tf_op jit(solution)/shard_map/ppermute | solution.py:314
  90.9 11.0 %collective-permute-start.6 = (bf16[64,128]{1,0:T(8,128)(2,1)S(1)}, bf16[64,128]{1,0:T(8,128)(2,1)S(1)}, u32[]{:S(2)}, u32[]{:S(2)}) collective-permute-start(bf16[64,128]{1,0:T(8,128)(2,1)S(1)} %get-tuple-element.46), channel_id=1, source_target_pairs={{0,4},{4,8},{8,12},{12,16},{16,20},{20,24},{24,28},{28,32},{32,36}... | collective-permute-start | bytes 49160 | tf_op jit(solution)/shard_map/ppermute | solution.py:314
  92.9 9.1 %collective-permute-start.7 = (bf16[64,128]{1,0:T(8,128)(2,1)S(1)}, bf16[64,128]{1,0:T(8,128)(2,1)S(1)}, u32[]{:S(2)}, u32[]{:S(2)}) collective-permute-start(bf16[64,128]{1,0:T(8,128)(2,1)S(1)} %get-tuple-element.47), channel_id=1, source_target_pairs={{4,0},{8,4},{12,8},{16,12},{20,16},{24,20},{28,24},{32,28},{36,32}... | collective-permute-start | bytes 49160 | tf_op jit(solution)/shard_map/ppermute | solution.py:314

commit v4 on v3

--- a/solution.py
+++ b/solution.py
@@ -27,7 +27,7 @@
     return jnp.where(mask, 1.0, 0.0).astype(BF16)
 
 
-def call(body, out_shape, name, *args, scratch=(), specs=None, outs=None, grant=8, alias=None):
+def call(body, out_shape, *args, scratch=(), specs=None, outs=None, grant=8, alias=None):
     vmem = pl.BlockSpec(memory_space=pltpu.VMEM)
     return pl.pallas_call(
         body,
@@ -37,15 +37,10 @@
         scratch_shapes=scratch,
         input_output_aliases=alias or {},
         compiler_params=pltpu.CompilerParams(vmem_limit_bytes=grant << 20) if grant else None,
-        name=name,
     )(*args)
 
 
-def route_body(dest_ref, row_ref, col_ref, weight_ref, state_ref, send_ref, place_ref, first_ref, last_ref, head_ref, tail_ref):
-    first_ref[...] = state_ref[:, 0, :]
-    last_ref[...] = state_ref[:, 63, :]
-    head_ref[...] = state_ref[0]
-    tail_ref[...] = state_ref[63]
+def route_body(dest_ref, row_ref, col_ref, weight_ref, send_ref, place_ref):
     dest = dest_ref[...]
     tiles = send_ref.shape[0]
     obs = dest.shape[1]
@@ -64,6 +59,24 @@
     send_ref[...] = lax.dot_general(onehot.astype(BF16), table, NT, preferred_element_type=F32)
 
 
+def border_body(state_ref, first_ref, last_ref, head_ref, tail_ref, sides, rows, sems):
+    edges = [
+        (state_ref.at[:, pl.ds(0, 8), :], sides.at[0]),
+        (state_ref.at[:, pl.ds(56, 8), :], sides.at[1]),
+        (state_ref.at[0], rows.at[0]),
+        (state_ref.at[63], rows.at[1]),
+    ]
+    copies = [pltpu.make_async_copy(a, b, sems.at[i]) for i, (a, b) in enumerate(edges)]
+    for copy in copies:
+        copy.start()
+    for copy in copies:
+        copy.wait()
+    first_ref[...] = sides[0, :, 0, :]
+    last_ref[...] = sides[1, :, 7, :]
+    head_ref[...] = rows[0]
+    tail_ref[...] = rows[1]
+
+
 def fields_by_row(recv, first, count):
     tiles = recv.shape[0]
     pick = ones_where((iota((count, tiles), 0) + first) // CAP == iota((count, tiles), 1))
@@ -88,9 +101,11 @@
     return jnp.where(hit0, value0, jnp.where(hit1, value1, jnp.zeros((), value0.dtype)))
 
 
-def gather_body(recv_ref, own_ref, top_ref, bottom_ref, left_ref, right_ref, out_ref, rim_ref, *matrices):
+def gather_body(recv_ref, own_hbm, top_ref, bottom_ref, left_ref, right_ref, out_ref, own_ref, buffer, own_sem, out_sems, rim_ref, *matrices):
     slots = out_ref.shape[0]
     chunk = matrices[0].shape[0]
+    load = pltpu.make_async_copy(own_hbm, own_ref, own_sem)
+    load.start()
     rim_ref[0:64, :] = top_ref[...]
     rim_ref[64:128, :] = bottom_ref[...]
     rim_ref[128:192, :] = left_ref[0:64, :]
@@ -126,14 +141,21 @@
 
     def use(first, matrix_ref):
         out = mm(matrix_ref[:, :4096], own_ref[...]) + mm(matrix_ref[:, 4096:], rim_ref[...])
-        out_ref[first : first + chunk, :] = out.astype(BF16)
-
+        at = slice(first, first + chunk)
+        buffer[at, :] = out.astype(BF16)
+        copies.append(pltpu.make_async_copy(buffer.at[at, :], out_ref.at[at, :], out_sems.at[len(copies)]))
+        copies[-1].start()
+
+    copies = []
     count = slots // chunk
     build(0, matrices[0])
+    load.wait()
     for i in range(count):
         if i + 1 < count:
             build((i + 1) * chunk, matrices[i + 1])
         use(i * chunk, matrices[i])
+    for copy in copies:
+        copy.wait()
 
 
 def components_body(spectra_ref, basis_ref, place_ref, pcs_ref, buffer, basis_buffer, sems, basis_sem):
@@ -339,45 +361,61 @@
     slots = tiles * CAP
     sds = jax.ShapeDtypeStruct
 
-    send_meta, place, first, last, head, tail = call(
+    vmem = pl.BlockSpec(memory_space=pltpu.VMEM)
+    hbm = pl.BlockSpec(memory_space=pltpu.HBM)
+    send_meta, place = call(
         route_body,
-        (pltpu.HBM((tiles, 128), F32), sds((1, obs), I32)) + (sds((64, levels), BF16),) * 4,
-        "route",
+        (pltpu.HBM((tiles, 128), F32), sds((1, obs), I32)),
         destination.reshape(1, obs),
         corner_row.reshape(1, obs),
         corner_col.reshape(1, obs),
         corner_weight.T,
-        state,
         grant=None,
     )
     recv_meta = exchange(send_meta)
+    first, last, head, tail = call(
+        border_body,
+        (sds((64, levels), BF16),) * 4,
+        in_hbm(state),
+        specs=[hbm],
+        scratch=[
+            pltpu.VMEM((2, 64, 8, levels), BF16),
+            pltpu.VMEM((2, 64, levels), BF16),
+            pltpu.SemaphoreType.DMA((4,)),
+        ],
+    )
     top = shift(tail, "lat", 1, False)
     bottom = shift(head, "lat", -1, False)
     fill = jnp.zeros((14, levels), BF16)
     left = shift(jnp.concatenate([last, top[63:], bottom[63:], fill], 0), "lon", 1, True)
     right = shift(jnp.concatenate([first, top[:1], bottom[:1], fill], 0), "lon", -1, True)
 
-    vmem = pl.BlockSpec(memory_space=pltpu.VMEM)
-    hbm = pl.BlockSpec(memory_space=pltpu.HBM)
     columns = call(
         gather_body,
         pltpu.HBM((slots, levels), BF16),
-        "interpolate",
         recv_meta,
-        state.reshape(-1, levels),
+        in_hbm(state.reshape(-1, levels)),
         top,
         bottom,
         left,
         right,
-        scratch=[pltpu.VMEM((384, levels), BF16)] + [pltpu.VMEM((slots // 4, 4480), BF16)] * 4,
-        grant=26,
+        specs=[vmem, hbm, vmem, vmem, vmem, vmem],
+        outs=hbm,
+        scratch=[
+            pltpu.VMEM((4096, levels), BF16),
+            pltpu.VMEM((slots, levels), BF16),
+            pltpu.SemaphoreType.DMA,
+            pltpu.SemaphoreType.DMA((4,)),
+            pltpu.VMEM((384, levels), BF16),
+        ]
+        + [pltpu.VMEM((slots // 4, 4480), BF16)] * 4,
+        grant=28,
     )
     columns, place = lax.optimization_barrier((columns, place))
     recv_columns = exchange(columns.reshape(tiles, CAP, levels)).reshape(slots, levels)
     pcs = call(
         components_body,
         sds((obs, npc), BF16),
-        "components",
         in_hbm(spectra),
         in_hbm(pc_basis),
         place,
@@ -393,7 +431,6 @@
     departures, send_g = call(
         network_body,
         (pltpu.HBM((obs, npc), BF16), pltpu.HBM((slots, levels), BF16)),
-        "network",
         recv_columns,
         place,
         pcs,
@@ -420,11 +457,10 @@
     )
     send_g, recv_meta = lax.optimization_barrier((send_g, recv_meta))
     g = exchange(send_g.reshape(tiles, CAP, levels)).reshape(slots, levels)
-    fields = call(prepare_body, sds((8, slots), F32), "prepare", recv_meta)
+    fields = call(prepare_body, sds((8, slots), F32), recv_meta)
     up, down, g_left, g_right = call(
         scatter_rim_body,
         (sds((64, levels), F32), sds((64, levels), F32), sds((80, levels), BF16), sds((80, levels), BF16)),
-        "adjoint_rim",
         fields,
         g,
         scratch=[pltpu.VMEM((288, slots), BF16)],
@@ -436,7 +472,6 @@
     gradient = call(
         functools.partial(scatter_body, 0),
         pltpu.HBM((64, 64, levels), F32),
-        "adjoint_a",
         fields,
         g,
         outs=hbm,
@@ -444,22 +479,13 @@
         grant=14,
     )
     from_left, from_right, gradient = lax.optimization_barrier((from_left, from_right, gradient))
-    up, down = call(
-        corner_body,
-        (sds((64, levels), BF16), sds((64, levels), BF16)),
-        "corners",
-        up,
-        down,
-        from_left,
-        from_right,
-    )
+    up, down = call(corner_body, (sds((64, levels), BF16), sds((64, levels), BF16)), up, down, from_left, from_right)
     up, down, g = lax.optimization_barrier((up, down, g))
     from_below = shift(up, "lat", -1, False)
     from_above = shift(down, "lat", 1, False)
     gradient = call(
         functools.partial(scatter_body, 1),
         pltpu.HBM((64, 64, levels), F32),
-        "adjoint_b",
         fields,
         g,
         in_hbm(gradient),
@@ -472,7 +498,6 @@
     gradient = call(
         edge_body,
         pltpu.HBM((64, 64, levels), F32),
-        "edges",
         from_left,
         from_right,
         from_above,

time: 105 us -> 104 us (level)
  local copies, waits for them, and re-layouts: 1.34 us -> 0.11 us
  Pallas kernels: 35.8 us -> 37 us
    unnamed x10 -> x8, local copies, waits for them, and re-layouts: 1.25 us -> 0.02 us
    pallas_call x10 -> x11, Pallas kernels: 35.8 us -> 37 us  [call(): pl.pallas_call(body, in_specs=specs or [vmem] * len(args), out_specs=outs...]
  transfers between devices with their start and end apart: 11 -> 11, of which waited for: 5 -> 5; matrix products, arithmetic and copies ran while one was open for 1% -> 0% of each run, Pallas kernels for 15% -> 17%
where the time goes in v4:
time: 104 us; the launch traced here: 103 us
  starting transfers between devices  42.8 us (41%)
  Pallas kernels  37 us (36%)
  waiting for transfers between devices  22.2 us (21%)
    pallas_call x11, Pallas kernels, call(): pl.pallas_call(body, in_specs=specs or [vmem] * len(args), out_specs=outs...  37 us
    ppermute x8, starting transfers between devices, shift(): return lax.ppermute(x, axis, pairs)  22 us
    all_to_all x3, starting transfers between devices, exchange(): return lax.all_to_all(x, AXES, split_axis=0, concat_axis=0, tiled=True)  20.9 us
    all_to_all x3, waiting for transfers between devices, exchange(): return lax.all_to_all(x, AXES, split_axis=0, concat_axis=0, tiled=True)  15.1 us
    ppermute x8, waiting for transfers between devices, shift(): return lax.ppermute(x, axis, pairs)  7.07 us
  transfers between devices with their start and end apart: 11, of which 5 were waited for; matrix products, arithmetic and copies ran while one was open for 0% of the time, Pallas kernels for 17%

profile of v4, /device:TPU:6, one launch (start us, length us, event | category | flops | bytes accessed | tf_op | source)
XLA Modules:
  0.0 103.2 jit_solution(3964489413566074385)
XLA Ops:
  0.6 1.1 %shard_map.132 = (bf16[64,128]{1,0:T(8,128)(2,1)S(1)}, bf16[64,128]{1,0:T(8,128)(2,1)S(1)}, bf16[64,128]{1,0:T(8,128)(2,1)S(1)}, bf16[64,128]{1,0:T(8,128)(2,1)S(1)}) custom-call(bf16[64,64,128]{2,1,0:T(8,128)(2,1)} %state_ref.1), custom_call_target="tpu_custom_call" | custom-call | tf_op jit(solution)/shard_map/pallas_call | solution.py:32
  1.7 5.7 %collective-permute-start.1 = (bf16[64,128]{1,0:T(8,128)(2,1)S(1)}, bf16[64,128]{1,0:T(8,128)(2,1)S(1)}, u32[]{:S(2)}, u32[]{:S(2)}) collective-permute-start(bf16[64,128]{1,0:T(8,128)(2,1)S(1)} %get-tuple-element.28), channel_id=1, source_target_pairs={{4,0},{8,4},{12,8},{16,12},{20,16},{24,20},{28,24},{32,28},{36,32}... | collective-permute-start | bytes 49160 | tf_op jit(solution)/shard_map/ppermute | solution.py:336
  7.4 2.0 %shard_map.131 = (f32[128,128]{1,0:T(8,128)}, s32[1,1024]{1,0:T(1,128)}) custom-call(s32[1,1024]{1,0:T(1,128)} %bitcast.30, s32[1,1024]{1,0:T(1,128)} %bitcast.31, s32[1,1024]{1,0:T(1,128)} %bitcast.32, bf16[4,1024]{1,0:T(4,128)(2,1)} %bitcast.29), custom_call_target="tpu_custom_call" | custom-call | tf_op jit(solution)/shard_map/pallas_call | solution.py:32
  9.4 0.0 copy-start
  9.4 6.8 %all-to-all-start = ((f32[128,1,128]{2,1,0:T(1,128)}), f32[128,1,128]{2,1,0:T(1,128)S(1)}, u32[]{:S(2)}, u32[]{:S(2)}) async-start(f32[128,1,128]{2,1,0:T(1,128)} %bitcast.28), calls=%async_computation | async-start | bytes 131072 | tf_op jit(solution)/shard_map/all_to_all | solution.py:340
  16.2 2.0 %collective-permute-start = (bf16[64,128]{1,0:T(8,128)(2,1)S(1)}, bf16[64,128]{1,0:T(8,128)(2,1)S(1)}, u32[]{:S(2)}, u32[]{:S(2)}) collective-permute-start(bf16[64,128]{1,0:T(8,128)(2,1)S(1)} %get-tuple-element.27), channel_id=1, source_target_pairs={{0,4},{4,8},{8,12},{12,16},{16,20},{20,24},{24,28},{28,32},{32,36}... | collective-permute-start | bytes 49160 | tf_op jit(solution)/shard_map/ppermute | solution.py:336
  18.3 0.1 pad.7.clone
  18.4 0.0 collective-permute-done.1.bottom_ref
  18.4 5.1 %collective-permute-done.top_ref = bf16[64,128]{1,0:T(8,128)(2,1)S(1)} collective-permute-done((bf16[64,128]{1,0:T(8,128)(2,1)S(1)}, bf16[64,128]{1,0:T(8,128)(2,1)S(1)}, u32[]{:S(2)}, u32[]{:S(2)}) %collective-permute-start) | collective-permute-done | bytes 16416 | tf_op jit(solution)/shard_map/ppermute | solution.py:336
  23.5 0.1 maximum_maximum_fusion.1
  23.5 1.5 %collective-permute-start.2 = (bf16[80,128]{1,0:T(8,128)(2,1)S(1)}, bf16[80,128]{1,0:T(8,128)(2,1)S(1)}, u32[]{:S(2)}, u32[]{:S(2)}) collective-permute-start(bf16[80,128]{1,0:T(8,128)(2,1)S(1)} %get-tuple-element.55), channel_id=1, source_target_pairs={{0,1},{1,2},{2,3},{3,0},{4,5},{5,6},{6,7},{7,4},{8,9},{9,10},{10,1... | collective-permute-start | bytes 61448 | tf_op jit(solution)/shard_map/ppermute | solution.py:336
  25.0 1.8 %collective-permute-start.3 = (bf16[80,128]{1,0:T(8,128)(2,1)S(1)}, bf16[80,128]{1,0:T(8,128)(2,1)S(1)}, u32[]{:S(2)}, u32[]{:S(2)}) collective-permute-start(bf16[80,128]{1,0:T(8,128)(2,1)S(1)} %get-tuple-element.54), channel_id=1, source_target_pairs={{0,3},{1,0},{2,1},{3,2},{4,7},{5,4},{6,5},{7,6},{8,11},{9,8},{10,9... | collective-permute-start | bytes 61448 | tf_op jit(solution)/shard_map/ppermute | solution.py:336
  26.8 1.8 %collective-permute-done.2.left_ref = bf16[80,128]{1,0:T(8,128)(2,1)S(1)} collective-permute-done((bf16[80,128]{1,0:T(8,128)(2,1)S(1)}, bf16[80,128]{1,0:T(8,128)(2,1)S(1)}, u32[]{:S(2)}, u32[]{:S(2)}) %collective-permute-start.2) | collective-permute-done | bytes 20512 | tf_op jit(solution)/shard_map/ppermute | solution.py:336
  28.6 0.2 collective-permute-done.3.right_ref
  28.8 0.0 all-to-all-done
  28.8 8.7 %shard_map.133 = bf16[2048,128]{1,0:T(8,128)(2,1)} custom-call(f32[128,128]{1,0:T(8,128)S(1)} %bitcast.20, bf16[4096,128]{1,0:T(8,128)(2,1)} %bitcast.25, bf16[64,128]{1,0:T(8,128)(2,1)S(1)} %collective-permute-done.top_ref, bf16[64,128]{1,0:T(8,128)(2,1)S(1)} %collective-permute-done.1.bottom_ref, bf16[80,128]{1,0:T(8,128)(2,1)S(1)} %collective-permute-done.2.left_ref, ...), custom_call_target="tpu_custom_call" | custom-call | tf_op jit(solution)/shard_map/pallas_call | solution.py:32
  37.5 7.5 %all-to-all-start.1 = ((bf16[128,16,128]{2,1,0:T(8,128)(2,1)}), bf16[128,16,128]{2,1,0:T(8,128)(2,1)S(1)}, u32[]{:S(2)}, u32[]{:S(2)}) async-start(bf16[128,16,128]{2,1,0:T(8,128)(2,1)} %bitcast.26), calls=%async_computation.1 | async-start | bytes 1048576 | tf_op jit(solution)/shard_map/all_to_all | solution.py:340
  45.1 0.0 copy-done
  45.1 0.0 copy-start.1
  45.1 0.0 copy-start.2
  45.1 0.0 copy-start.3
  45.1 8.9 %shard_map.134.pcs_ref = bf16[1024,256]{1,0:T(8,128)(2,1)S(1)} custom-call(bf16[1024,8448]{1,0:T(8,128)(2,1)} %spectra_ref.1, bf16[8448,256]{1,0:T(8,128)(2,1)} %basis_ref.1, s32[1,1024]{1,0:T(1,128)S(1)} %copy-done), custom_call_target="tpu_custom_call" | custom-call | tf_op jit(solution)/shard_map/pallas_call | solution.py:32
  54.0 3.3 %all-to-all-done.1 = bf16[128,16,128]{2,1,0:T(8,128)(2,1)S(1)} async-done(((bf16[128,16,128]{2,1,0:T(8,128)(2,1)}), bf16[128,16,128]{2,1,0:T(8,128)(2,1)S(1)}, u32[]{:S(2)}, u32[]{:S(2)}) %all-to-all-start.1) | async-done | bytes 524320 | tf_op jit(solution)/shard_map/all_to_all | solution.py:340
  57.3 0.0 copy-done.1
  57.3 0.0 copy-done.2
  57.3 0.0 copy-done.3
  57.3 6.8 %shard_map.135 = (bf16[1024,256]{1,0:T(8,128)(2,1)}, bf16[2048,128]{1,0:T(8,128)(2,1)}) custom-call(bf16[2048,128]{1,0:T(8,128)(2,1)S(1)} %bitcast.19, s32[1,1024]{1,0:T(1,128)S(1)} %copy-done, bf16[1024,256]{1,0:T(8,128)(2,1)S(1)} %shard_map.134.pcs_ref, f32[1,256]{1,0:T(1,128)S(1)} %bitcast.23, bf16[128,512]{1,0:T(8,128)(2,1)} %w_in_hbm.1, ...), custom_call_target="tpu_custom_call" | custom-call | tf_op jit(solution)/shard_map/pallas_call | solution.py:32
  64.1 6.5 %all-to-all-start.2 = ((bf16[128,16,128]{2,1,0:T(8,128)(2,1)}), bf16[128,16,128]{2,1,0:T(8,128)(2,1)S(1)}, u32[]{:S(2)}, u32[]{:S(2)}) async-start(bf16[128,16,128]{2,1,0:T(8,128)(2,1)} %bitcast.27), calls=%async_computation.2 | async-start | bytes 1048576 | tf_op jit(solution)/shard_map/all_to_all | solution.py:340
  70.6 0.5 shard_map.136.fields_ref
  71.0 11.8 %all-to-all-done.2 = bf16[128,16,128]{2,1,0:T(8,128)(2,1)S(1)} async-done(((bf16[128,16,128]{2,1,0:T(8,128)(2,1)}), bf16[128,16,128]{2,1,0:T(8,128)(2,1)S(1)}, u32[]{:S(2)}, u32[]{:S(2)}) %all-to-all-start.2) | async-done | bytes 524320 | tf_op jit(solution)/shard_map/all_to_all | solution.py:340
  82.8 0.5 shard_map.137
  83.3 0.6 collective-permute-start.4
  84.0 2.7 %collective-permute-start.5 = (bf16[80,128]{1,0:T(8,128)(2,1)S(1)}, bf16[80,128]{1,0:T(8,128)(2,1)S(1)}, u32[]{:S(2)}, u32[]{:S(2)}) collective-permute-start(bf16[80,128]{1,0:T(8,128)(2,1)S(1)} %get-tuple-element.39), channel_id=1, source_target_pairs={{0,3},{1,0},{2,1},{3,2},{4,7},{5,4},{6,5},{7,6},{8,11},{9,8},{10,9... | collective-permute-start | bytes 61448 | tf_op jit(solution)/shard_map/ppermute | solution.py:336
  86.6 3.3 %shard_map.138.refs_0_ = f32[64,64,128]{2,1,0:T(8,128)} custom-call(f32[8,2048]{1,0:T(8,128)S(1)} %shard_map.136.fields_ref, bf16[2048,128]{1,0:T(8,128)(2,1)S(1)} %bitcast.17), custom_call_target="tpu_custom_call" | custom-call | tf_op jit(solution)/shard_map/pallas_call | solution.py:32
  89.9 0.0 collective-permute-done.4.left_ref
  90.0 0.0 collective-permute-done.5.right_ref
  90.0 1.9 %collective-permute-start.6 = (bf16[64,128]{1,0:T(8,128)(2,1)S(1)}, bf16[64,128]{1,0:T(8,128)(2,1)S(1)}, u32[]{:S(2)}, u32[]{:S(2)}) collective-permute-start(bf16[64,128]{1,0:T(8,128)(2,1)S(1)} %get-tuple-element.46), channel_id=1, source_target_pairs={{0,4},{4,8},{8,12},{12,16},{16,20},{20,24},{24,28},{28,32},{32,36}... | collective-permute-start | bytes 49160 | tf_op jit(solution)/shard_map/ppermute | solution.py:336
  91.9 5.8 %collective-permute-start.7 = (bf16[64,128]{1,0:T(8,128)(2,1)S(1)}, bf16[64,128]{1,0:T(8,128)(2,1)S(1)}, u32[]{:S(2)}, u32[]{:S(2)}) collective-permute-start(bf16[64,128]{1,0:T(8,128)(2,1)S(1)} %get-tuple-element.47), channel_id=1, source_target_pairs={{4,0},{8,4},{12,8},{16,12},{20,16},{24,20},{28,24},{32,28},{36,32}... | collective-permute-start | bytes 49160 | tf_op jit(solution)/shard_map/ppermute | solution.py:336
  97.7 3.3 %shard_map.140.grad_ref = f32[64,64,128]{2,1,0:T(8,128)} custom-call(f32[8,2048]{1,0:T(8,128)S(1)} %shard_map.136.fields_ref, bf16[2048,128]{1,0:T(8,128)(2,1)S(1)} %bitcast.18, f32[64,64,128]{2,1,0:T(8,128)} %shard_map.138.refs_0_), custom_call_target="tpu_custom_call", output_to_operand_aliasing={{}: (2, {})} | custom-call | tf_op jit(solution)/shard_map/pallas_call | solution.py:32
  101.0 0.0 collective-permute-done.6.above_ref
  101.0 0.0 collective-permute-done.7.below_ref
  101.0 2.0 %shard_map.141 = f32[64,64,128]{2,1,0:T(8,128)} custom-call(bf16[80,128]{1,0:T(8,128)(2,1)S(1)} %collective-permute-done.4.left_ref, bf16[80,128]{1,0:T(8,128)(2,1)S(1)} %collective-permute-done.5.right_ref, bf16[64,128]{1,0:T(8,128)(2,1)S(1)} %collective-permute-done.6.above_ref, ...), custom_call_target="tpu_custom_call", output_to_operand_aliasing={{}: (4, {})} | custom-call | tf_op jit(solution)/shard_map/pallas_call | solution.py:32
  (4 shorter events, 0.0 us)
Async XLA Ops:
  1.7 16.7 %collective-permute-start.1 = (bf16[64,128]{1,0:T(8,128)(2,1)S(1)}, bf16[64,128]{1,0:T(8,128)(2,1)S(1)}, u32[]{:S(2)}, u32[]{:S(2)}) collective-permute-start(bf16[64,128]{1,0:T(8,128)(2,1)S(1)} %get-tuple-element.28), channel_id=1, source_target_pairs={{4,0},{8,4},{12,8},{16,12},{20,16},{24,20},{28,24},{32,28},{36,32}... | collective-permute-start | bytes 49160 | tf_op jit(solution)/shard_map/ppermute | solution.py:336
  9.4 35.7 %copy-start = (s32[1,1024]{1,0:T(1,128)S(1)}, s32[1,1024]{1,0:T(1,128)}, u32[]{:S(2)}) copy-start(s32[1,1024]{1,0:T(1,128)} %get-tuple-element.33.place_ref) | copy-start | bytes 12292
  9.4 19.4 %all-to-all-start = ((f32[128,1,128]{2,1,0:T(1,128)}), f32[128,1,128]{2,1,0:T(1,128)S(1)}, u32[]{:S(2)}, u32[]{:S(2)}) async-start(f32[128,1,128]{2,1,0:T(1,128)} %bitcast.28), calls=%async_computation | async-start | bytes 131072 | tf_op jit(solution)/shard_map/all_to_all | solution.py:340
  16.2 7.2 %collective-permute-start = (bf16[64,128]{1,0:T(8,128)(2,1)S(1)}, bf16[64,128]{1,0:T(8,128)(2,1)S(1)}, u32[]{:S(2)}, u32[]{:S(2)}) collective-permute-start(bf16[64,128]{1,0:T(8,128)(2,1)S(1)} %get-tuple-element.27), channel_id=1, source_target_pairs={{0,4},{4,8},{8,12},{12,16},{16,20},{20,24},{24,28},{28,32},{32,36}... | collective-permute-start | bytes 49160 | tf_op jit(solution)/shard_map/ppermute | solution.py:336
  23.5 5.1 %collective-permute-start.2 = (bf16[80,128]{1,0:T(8,128)(2,1)S(1)}, bf16[80,128]{1,0:T(8,128)(2,1)S(1)}, u32[]{:S(2)}, u32[]{:S(2)}) collective-permute-start(bf16[80,128]{1,0:T(8,128)(2,1)S(1)} %get-tuple-element.55), channel_id=1, source_target_pairs={{0,1},{1,2},{2,3},{3,0},{4,5},{5,6},{6,7},{7,4},{8,9},{9,10},{10,1... | collective-permute-start | bytes 61448 | tf_op jit(solution)/shard_map/ppermute | solution.py:336
  25.0 3.8 %collective-permute-start.3 = (bf16[80,128]{1,0:T(8,128)(2,1)S(1)}, bf16[80,128]{1,0:T(8,128)(2,1)S(1)}, u32[]{:S(2)}, u32[]{:S(2)}) collective-permute-start(bf16[80,128]{1,0:T(8,128)(2,1)S(1)} %get-tuple-element.54), channel_id=1, source_target_pairs={{0,3},{1,0},{2,1},{3,2},{4,7},{5,4},{6,5},{7,6},{8,11},{9,8},{10,9... | collective-permute-start | bytes 61448 | tf_op jit(solution)/shard_map/ppermute | solution.py:336
  37.5 19.8 %all-to-all-start.1 = ((bf16[128,16,128]{2,1,0:T(8,128)(2,1)}), bf16[128,16,128]{2,1,0:T(8,128)(2,1)S(1)}, u32[]{:S(2)}, u32[]{:S(2)}) async-start(bf16[128,16,128]{2,1,0:T(8,128)(2,1)} %bitcast.26), calls=%async_computation.1 | async-start | bytes 1048576 | tf_op jit(solution)/shard_map/all_to_all | solution.py:340
  45.1 12.2 %copy-start.1 = (f32[512]{0:T(512)S(1)}, f32[512]{0:T(512)}, u32[]{:S(2)}) copy-start(f32[512]{0:T(512)} %param.21) | copy-start | bytes 6148
  45.1 12.2 %copy-start.2 = (f32[256]{0:T(256)S(1)}, f32[256]{0:T(256)}, u32[]{:S(2)}) copy-start(f32[256]{0:T(256)} %param.19) | copy-start | bytes 3076
  45.1 12.2 %copy-start.3 = (f32[256]{0:T(256)S(1)}, f32[256]{0:T(256)}, u32[]{:S(2)}) copy-start(f32[256]{0:T(256)} %param.23) | copy-start | bytes 3076
  64.1 18.7 %all-to-all-start.2 = ((bf16[128,16,128]{2,1,0:T(8,128)(2,1)}), bf16[128,16,128]{2,1,0:T(8,128)(2,1)S(1)}, u32[]{:S(2)}, u32[]{:S(2)}) async-start(bf16[128,16,128]{2,1,0:T(8,128)(2,1)} %bitcast.27), calls=%async_computation.2 | async-start | bytes 1048576 | tf_op jit(solution)/shard_map/all_to_all | solution.py:340
  83.3 6.6 %collective-permute-start.4 = (bf16[80,128]{1,0:T(8,128)(2,1)S(1)}, bf16[80,128]{1,0:T(8,128)(2,1)S(1)}, u32[]{:S(2)}, u32[]{:S(2)}) collective-permute-start(bf16[80,128]{1,0:T(8,128)(2,1)S(1)} %get-tuple-element.38), channel_id=1, source_target_pairs={{0,1},{1,2},{2,3},{3,0},{4,5},{5,6},{6,7},{7,4},{8,9},{9,10},{10,1... | collective-permute-start | bytes 61448 | tf_op jit(solution)/shard_map/ppermute | solution.py:336
  84.0 6.0 %collective-permute-start.5 = (bf16[80,128]{1,0:T(8,128)(2,1)S(1)}, bf16[80,128]{1,0:T(8,128)(2,1)S(1)}, u32[]{:S(2)}, u32[]{:S(2)}) collective-permute-start(bf16[80,128]{1,0:T(8,128)(2,1)S(1)} %get-tuple-element.39), channel_id=1, source_target_pairs={{0,3},{1,0},{2,1},{3,2},{4,7},{5,4},{6,5},{7,6},{8,11},{9,8},{10,9... | collective-permute-start | bytes 61448 | tf_op jit(solution)/shard_map/ppermute | solution.py:336
  90.0 11.0 %collective-permute-start.6 = (bf16[64,128]{1,0:T(8,128)(2,1)S(1)}, bf16[64,128]{1,0:T(8,128)(2,1)S(1)}, u32[]{:S(2)}, u32[]{:S(2)}) collective-permute-start(bf16[64,128]{1,0:T(8,128)(2,1)S(1)} %get-tuple-element.46), channel_id=1, source_target_pairs={{0,4},{4,8},{8,12},{12,16},{16,20},{20,24},{24,28},{28,32},{32,36}... | collective-permute-start | bytes 49160 | tf_op jit(solution)/shard_map/ppermute | solution.py:336
  91.9 9.1 %collective-permute-start.7 = (bf16[64,128]{1,0:T(8,128)(2,1)S(1)}, bf16[64,128]{1,0:T(8,128)(2,1)S(1)}, u32[]{:S(2)}, u32[]{:S(2)}) collective-permute-start(bf16[64,128]{1,0:T(8,128)(2,1)S(1)} %get-tuple-element.47), channel_id=1, source_target_pairs={{4,0},{8,4},{12,8},{16,12},{20,16},{24,20},{28,24},{32,28},{36,32}... | collective-permute-start | bytes 49160 | tf_op jit(solution)/shard_map/ppermute | solution.py:336

commit v5 on v4

--- a/solution.py
+++ b/solution.py
@@ -40,9 +40,21 @@
     )(*args)
 
 
-def route_body(dest_ref, row_ref, col_ref, weight_ref, send_ref, place_ref):
+def diagonal(rows, cols):
+    lat, lon, n_lat, n_lon = lax.axis_index("lat"), lax.axis_index("lon"), lax.axis_size("lat"), lax.axis_size("lon")
+    to = lat + rows
+    return jnp.where((to >= 0) & (to < n_lat), to * n_lon + (lon + cols + n_lon) % n_lon, -1)
+
+
+def route_body(dest_ref, row_ref, col_ref, weight_ref, state_ref, send_ref, place_ref, cells, sems):
+    spots = [(0, 0), (0, 56), (63, 0), (63, 56)]
+    copies = [
+        pltpu.make_async_copy(state_ref.at[r, pl.ds(c, 8), :], cells.at[i], sems.at[i]) for i, (r, c) in enumerate(spots)
+    ]
+    for copy in copies:
+        copy.start()
     dest = dest_ref[...]
-    tiles = send_ref.shape[0]
+    tiles = send_ref.shape[0] // 2
     obs = dest.shape[1]
     onehot = jnp.where(iota((tiles, obs), 0) == dest, 1.0, 0.0)
     before = ones_where(iota((obs, obs), 0) < iota((obs, obs), 1))
@@ -56,7 +68,17 @@
     parts = [jnp.where(here, field, 0.0) for field in fields]
     parts.append(jnp.zeros((128 - CAP * len(parts), obs), F32))
     table = jnp.concatenate(parts, 0).astype(BF16)
-    send_ref[...] = lax.dot_general(onehot.astype(BF16), table, NT, preferred_element_type=F32)
+    send_ref[pl.ds(0, tiles, stride=2), :] = lax.dot_general(
+        onehot.astype(BF16), table, NT, preferred_element_type=F32
+    )
+    for copy in copies:
+        copy.wait()
+    row = iota((tiles, 128), 0)
+    extra = jnp.zeros((tiles, 128), F32)
+    for i, (r, c) in enumerate(spots):
+        cell = cells[i].astype(F32)[7 if c else 0][None]
+        extra = jnp.where(row == diagonal(1 if r else -1, 1 if c else -1), cell, extra)
+    send_ref[pl.ds(1, tiles, stride=2), :] = extra
 
 
 def border_body(state_ref, first_ref, last_ref, head_ref, tail_ref, sides, rows, sems):
@@ -108,12 +130,16 @@
     load.start()
     rim_ref[0:64, :] = top_ref[...]
     rim_ref[64:128, :] = bottom_ref[...]
-    rim_ref[128:192, :] = left_ref[0:64, :]
-    rim_ref[192:256, :] = right_ref[0:64, :]
-    rim_ref[256:272, :] = left_ref[64:80, :]
-    rim_ref[272:288, :] = right_ref[64:80, :]
+    rim_ref[128:192, :] = left_ref[...]
+    rim_ref[192:256, :] = right_ref[...]
+    tiles = recv_ref.shape[0] // 2
+    cells = recv_ref[pl.ds(1, tiles, stride=2), :].astype(BF16)
+    row, lane = iota((16, tiles), 0), iota((16, tiles), 1)
+    for i, side in enumerate((-1, 1)):
+        source = jnp.where(row == 0, diagonal(-1, side), jnp.where(row == 1, diagonal(1, side), -1))
+        rim_ref[256 + 16 * i : 272 + 16 * i, :] = mm(ones_where(lane == source), cells).astype(BF16)
     rim_ref[288:384, :] = jnp.zeros((96, rim_ref.shape[1]), BF16)
-    recv = recv_ref[...].astype(BF16)
+    recv = recv_ref[pl.ds(0, tiles, stride=2), :].astype(BF16)
     lane = iota((chunk, 128), 1).astype(F32)
     upper = jnp.where(lane >= 64.0, 1.0, 0.0)
     in_row = (lane - 64.0 * upper).astype(BF16)
@@ -232,7 +258,7 @@
 
 
 def prepare_body(recv_ref, fields_ref):
-    fields = fields_by_lane(recv_ref[...].astype(BF16), fields_ref.shape[1])
+    fields = fields_by_lane(recv_ref[pl.ds(0, recv_ref.shape[0] // 2, stride=2), :].astype(BF16), fields_ref.shape[1])
     fields_ref[...] = jnp.concatenate(fields + [fields[5], fields[5]], 0)
 
 
@@ -365,14 +391,17 @@
     hbm = pl.BlockSpec(memory_space=pltpu.HBM)
     send_meta, place = call(
         route_body,
-        (pltpu.HBM((tiles, 128), F32), sds((1, obs), I32)),
+        (pltpu.HBM((2 * tiles, 128), F32), sds((1, obs), I32)),
         destination.reshape(1, obs),
         corner_row.reshape(1, obs),
         corner_col.reshape(1, obs),
         corner_weight.T,
+        in_hbm(state),
+        specs=[vmem] * 4 + [hbm],
+        scratch=[pltpu.VMEM((4, 8, levels), BF16), pltpu.SemaphoreType.DMA((4,))],
         grant=None,
     )
-    recv_meta = exchange(send_meta)
+    recv_meta = exchange(send_meta.reshape(tiles, 2, 128)).reshape(2 * tiles, 128)
     first, last, head, tail = call(
         border_body,
         (sds((64, levels), BF16),) * 4,
@@ -386,9 +415,8 @@
     )
     top = shift(tail, "lat", 1, False)
     bottom = shift(head, "lat", -1, False)
-    fill = jnp.zeros((14, levels), BF16)
-    left = shift(jnp.concatenate([last, top[63:], bottom[63:], fill], 0), "lon", 1, True)
-    right = shift(jnp.concatenate([first, top[:1], bottom[:1], fill], 0), "lon", -1, True)
+    left = shift(last, "lon", 1, True)
+    right = shift(first, "lon", -1, True)
 
     columns = call(
         gather_body,

time: 104 us -> 103 us (level)
  waiting for transfers between devices: 22.2 us -> 17.1 us
  starting transfers between devices: 42.8 us -> 46.5 us
    ppermute x8, waiting for transfers between devices: 7.07 us -> 1.98 us  [shift(): return lax.ppermute(x, axis, pairs)]
    all_to_all x3, starting transfers between devices: 20.9 us -> 24.5 us  [exchange(): return lax.all_to_all(x, AXES, split_axis=0, concat_axis=0, tiled=True)]
  transfers between devices with their start and end apart: 11 -> 11, of which waited for: 5 -> 4; matrix products, arithmetic and copies ran while one was open for 0% -> 0% of each run, Pallas kernels for 17% -> 17%
where the time goes in v5:
time: 103 us; the launch traced here: 102 us
  starting transfers between devices  46.5 us (45%)
  Pallas kernels  37.2 us (36%)
  waiting for transfers between devices  17.1 us (17%)
    pallas_call x11, Pallas kernels, call(): pl.pallas_call(body, in_specs=specs or [vmem] * len(args), out_specs=outs...  37.2 us
    all_to_all x3, starting transfers between devices, exchange(): return lax.all_to_all(x, AXES, split_axis=0, concat_axis=0, tiled=True)  24.5 us
    ppermute x8, starting transfers between devices, shift(): return lax.ppermute(x, axis, pairs)  22 us
    all_to_all x3, waiting for transfers between devices, exchange(): return lax.all_to_all(x, AXES, split_axis=0, concat_axis=0, tiled=True)  15.1 us
  transfers between devices with their start and end apart: 11, of which 4 were waited for; matrix products, arithmetic and copies ran while one was open for 0% of the time, Pallas kernels for 17%

profile of v5, /device:TPU:6, one launch (start us, length us, event | category | flops | bytes accessed | tf_op | source)
XLA Modules:
  0.0 101.7 jit_solution(17262995411954700301)
XLA Ops:
  0.6 2.2 %shard_map.131 = (f32[256,128]{1,0:T(8,128)}, s32[1,1024]{1,0:T(1,128)}) custom-call(s32[1,1024]{1,0:T(1,128)} %bitcast.28, s32[1,1024]{1,0:T(1,128)} %bitcast.29, s32[1,1024]{1,0:T(1,128)} %bitcast.30, bf16[4,1024]{1,0:T(4,128)(2,1)} %bitcast.27, bf16[64,64,128]{2,1,0:T(8,128)(2,1)} %state_ref.3), custom_call_target="tpu_custom_call" | custom-call | tf_op jit(solution)/shard_map/pallas_call | solution.py:32
  2.8 0.0 copy-start
  2.9 10.5 %all-to-all-start = ((f32[128,2,128]{2,1,0:T(2,128)}), f32[128,2,128]{2,1,0:T(2,128)S(1)}, u32[]{:S(2)}, u32[]{:S(2)}) async-start(f32[128,2,128]{2,1,0:T(2,128)} %bitcast.26), calls=%async_computation | async-start | bytes 262144 | tf_op jit(solution)/shard_map/all_to_all | solution.py:366
  13.3 1.1 %shard_map.132 = (bf16[64,128]{1,0:T(8,128)(2,1)S(1)}, bf16[64,128]{1,0:T(8,128)(2,1)S(1)}, bf16[64,128]{1,0:T(8,128)(2,1)S(1)}, bf16[64,128]{1,0:T(8,128)(2,1)S(1)}) custom-call(bf16[64,64,128]{2,1,0:T(8,128)(2,1)} %state_ref.3), custom_call_target="tpu_custom_call" | custom-call | tf_op jit(solution)/shard_map/pallas_call | solution.py:32
  14.4 2.0 %collective-permute-start = (bf16[64,128]{1,0:T(8,128)(2,1)S(1)}, bf16[64,128]{1,0:T(8,128)(2,1)S(1)}, u32[]{:S(2)}, u32[]{:S(2)}) collective-permute-start(bf16[64,128]{1,0:T(8,128)(2,1)S(1)} %get-tuple-element.27), channel_id=1, source_target_pairs={{0,4},{4,8},{8,12},{12,16},{16,20},{20,24},{24,28},{28,32},{32,36}... | collective-permute-start | bytes 49160 | tf_op jit(solution)/shard_map/ppermute | solution.py:362
  16.4 5.6 %collective-permute-start.1 = (bf16[64,128]{1,0:T(8,128)(2,1)S(1)}, bf16[64,128]{1,0:T(8,128)(2,1)S(1)}, u32[]{:S(2)}, u32[]{:S(2)}) collective-permute-start(bf16[64,128]{1,0:T(8,128)(2,1)S(1)} %get-tuple-element.28), channel_id=1, source_target_pairs={{4,0},{8,4},{12,8},{16,12},{20,16},{24,20},{28,24},{32,28},{36,32}... | collective-permute-start | bytes 49160 | tf_op jit(solution)/shard_map/ppermute | solution.py:362
  22.1 1.5 %collective-permute-start.2 = (bf16[64,128]{1,0:T(8,128)(2,1)S(1)}, bf16[64,128]{1,0:T(8,128)(2,1)S(1)}, u32[]{:S(2)}, u32[]{:S(2)}) collective-permute-start(bf16[64,128]{1,0:T(8,128)(2,1)S(1)} %get-tuple-element.29), channel_id=1, source_target_pairs={{0,1},{1,2},{2,3},{3,0},{4,5},{5,6},{6,7},{7,4},{8,9},{9,10},{10,1... | collective-permute-start | bytes 49160 | tf_op jit(solution)/shard_map/ppermute | solution.py:362
  23.6 1.8 %collective-permute-start.3 = (bf16[64,128]{1,0:T(8,128)(2,1)S(1)}, bf16[64,128]{1,0:T(8,128)(2,1)S(1)}, u32[]{:S(2)}, u32[]{:S(2)}) collective-permute-start(bf16[64,128]{1,0:T(8,128)(2,1)S(1)} %get-tuple-element.30), channel_id=1, source_target_pairs={{0,3},{1,0},{2,1},{3,2},{4,7},{5,4},{6,5},{7,6},{8,11},{9,8},{10,9... | collective-permute-start | bytes 49160 | tf_op jit(solution)/shard_map/ppermute | solution.py:362
  25.4 0.0 collective-permute-done.top_ref
  25.4 0.0 collective-permute-done.1.bottom_ref
  25.4 1.7 %collective-permute-done.2.left_ref = bf16[64,128]{1,0:T(8,128)(2,1)S(1)} collective-permute-done((bf16[64,128]{1,0:T(8,128)(2,1)S(1)}, bf16[64,128]{1,0:T(8,128)(2,1)S(1)}, u32[]{:S(2)}, u32[]{:S(2)}) %collective-permute-start.2) | collective-permute-done | bytes 16416 | tf_op jit(solution)/shard_map/ppermute | solution.py:362
  27.1 0.3 collective-permute-done.3.right_ref
  27.4 0.0 all-to-all-done
  27.4 8.7 %shard_map.133 = bf16[2048,128]{1,0:T(8,128)(2,1)} custom-call(f32[256,128]{1,0:T(8,128)S(1)} %bitcast.18, bf16[4096,128]{1,0:T(8,128)(2,1)} %bitcast.23, bf16[64,128]{1,0:T(8,128)(2,1)S(1)} %collective-permute-done.top_ref, bf16[64,128]{1,0:T(8,128)(2,1)S(1)} %collective-permute-done.1.bottom_ref, bf16[64,128]{1,0:T(8,128)(2,1)S(1)} %collective-permute-done.2.left_ref, ...), custom_call_target="tpu_custom_call" | custom-call | tf_op jit(solution)/shard_map/pallas_call | solution.py:32
  36.1 7.5 %all-to-all-start.1 = ((bf16[128,16,128]{2,1,0:T(8,128)(2,1)}), bf16[128,16,128]{2,1,0:T(8,128)(2,1)S(1)}, u32[]{:S(2)}, u32[]{:S(2)}) async-start(bf16[128,16,128]{2,1,0:T(8,128)(2,1)} %bitcast.24), calls=%async_computation.1 | async-start | bytes 1048576 | tf_op jit(solution)/shard_map/all_to_all | solution.py:366
  43.6 0.0 copy-done
  43.6 0.0 copy-start.1
  43.6 0.0 copy-start.2
  43.7 0.0 copy-start.3
  43.7 8.9 %shard_map.134.pcs_ref = bf16[1024,256]{1,0:T(8,128)(2,1)S(1)} custom-call(bf16[1024,8448]{1,0:T(8,128)(2,1)} %spectra_ref.1, bf16[8448,256]{1,0:T(8,128)(2,1)} %basis_ref.1, s32[1,1024]{1,0:T(1,128)S(1)} %copy-done), custom_call_target="tpu_custom_call" | custom-call | tf_op jit(solution)/shard_map/pallas_call | solution.py:32
  52.5 3.3 %all-to-all-done.1 = bf16[128,16,128]{2,1,0:T(8,128)(2,1)S(1)} async-done(((bf16[128,16,128]{2,1,0:T(8,128)(2,1)}), bf16[128,16,128]{2,1,0:T(8,128)(2,1)S(1)}, u32[]{:S(2)}, u32[]{:S(2)}) %all-to-all-start.1) | async-done | bytes 524320 | tf_op jit(solution)/shard_map/all_to_all | solution.py:366
  55.9 0.0 copy-done.1
  55.9 0.0 copy-done.2
  55.9 0.0 copy-done.3
  55.9 6.8 %shard_map.135 = (bf16[1024,256]{1,0:T(8,128)(2,1)}, bf16[2048,128]{1,0:T(8,128)(2,1)}) custom-call(bf16[2048,128]{1,0:T(8,128)(2,1)S(1)} %bitcast.17, s32[1,1024]{1,0:T(1,128)S(1)} %copy-done, bf16[1024,256]{1,0:T(8,128)(2,1)S(1)} %shard_map.134.pcs_ref, f32[1,256]{1,0:T(1,128)S(1)} %bitcast.21, bf16[128,512]{1,0:T(8,128)(2,1)} %w_in_hbm.1, ...), custom_call_target="tpu_custom_call" | custom-call | tf_op jit(solution)/shard_map/pallas_call | solution.py:32
  62.7 6.5 %all-to-all-start.2 = ((bf16[128,16,128]{2,1,0:T(8,128)(2,1)}), bf16[128,16,128]{2,1,0:T(8,128)(2,1)S(1)}, u32[]{:S(2)}, u32[]{:S(2)}) async-start(bf16[128,16,128]{2,1,0:T(8,128)(2,1)} %bitcast.25), calls=%async_computation.2 | async-start | bytes 1048576 | tf_op jit(solution)/shard_map/all_to_all | solution.py:366
  69.1 0.5 shard_map.136.fields_ref
  69.6 11.8 %all-to-all-done.2 = bf16[128,16,128]{2,1,0:T(8,128)(2,1)S(1)} async-done(((bf16[128,16,128]{2,1,0:T(8,128)(2,1)}), bf16[128,16,128]{2,1,0:T(8,128)(2,1)S(1)}, u32[]{:S(2)}, u32[]{:S(2)}) %all-to-all-start.2) | async-done | bytes 524320 | tf_op jit(solution)/shard_map/all_to_all | solution.py:366
  81.4 0.5 shard_map.137
  81.9 0.6 collective-permute-start.4
  82.5 2.7 %collective-permute-start.5 = (bf16[80,128]{1,0:T(8,128)(2,1)S(1)}, bf16[80,128]{1,0:T(8,128)(2,1)S(1)}, u32[]{:S(2)}, u32[]{:S(2)}) collective-permute-start(bf16[80,128]{1,0:T(8,128)(2,1)S(1)} %get-tuple-element.39), channel_id=1, source_target_pairs={{0,3},{1,0},{2,1},{3,2},{4,7},{5,4},{6,5},{7,6},{8,11},{9,8},{10,9... | collective-permute-start | bytes 61448 | tf_op jit(solution)/shard_map/ppermute | solution.py:362
  85.2 3.3 %shard_map.138.refs_0_ = f32[64,64,128]{2,1,0:T(8,128)} custom-call(f32[8,2048]{1,0:T(8,128)S(1)} %shard_map.136.fields_ref, bf16[2048,128]{1,0:T(8,128)(2,1)S(1)} %bitcast.15), custom_call_target="tpu_custom_call" | custom-call | tf_op jit(solution)/shard_map/pallas_call | solution.py:32
  88.5 0.0 collective-permute-done.4.left_ref
  88.5 0.0 collective-permute-done.5.right_ref
  88.5 1.9 %collective-permute-start.6 = (bf16[64,128]{1,0:T(8,128)(2,1)S(1)}, bf16[64,128]{1,0:T(8,128)(2,1)S(1)}, u32[]{:S(2)}, u32[]{:S(2)}) collective-permute-start(bf16[64,128]{1,0:T(8,128)(2,1)S(1)} %get-tuple-element.46), channel_id=1, source_target_pairs={{0,4},{4,8},{8,12},{12,16},{16,20},{20,24},{24,28},{28,32},{32,36}... | collective-permute-start | bytes 49160 | tf_op jit(solution)/shard_map/ppermute | solution.py:362
  90.5 5.8 %collective-permute-start.7 = (bf16[64,128]{1,0:T(8,128)(2,1)S(1)}, bf16[64,128]{1,0:T(8,128)(2,1)S(1)}, u32[]{:S(2)}, u32[]{:S(2)}) collective-permute-start(bf16[64,128]{1,0:T(8,128)(2,1)S(1)} %get-tuple-element.47), channel_id=1, source_target_pairs={{4,0},{8,4},{12,8},{16,12},{20,16},{24,20},{28,24},{32,28},{36,32}... | collective-permute-start | bytes 49160 | tf_op jit(solution)/shard_map/ppermute | solution.py:362
  96.2 3.3 %shard_map.140.grad_ref = f32[64,64,128]{2,1,0:T(8,128)} custom-call(f32[8,2048]{1,0:T(8,128)S(1)} %shard_map.136.fields_ref, bf16[2048,128]{1,0:T(8,128)(2,1)S(1)} %bitcast.16, f32[64,64,128]{2,1,0:T(8,128)} %shard_map.138.refs_0_), custom_call_target="tpu_custom_call", output_to_operand_aliasing={{}: (2, {})} | custom-call | tf_op jit(solution)/shard_map/pallas_call | solution.py:32
  99.5 0.0 collective-permute-done.6.above_ref
  99.6 0.0 collective-permute-done.7.below_ref
  99.6 2.0 %shard_map.141 = f32[64,64,128]{2,1,0:T(8,128)} custom-call(bf16[80,128]{1,0:T(8,128)(2,1)S(1)} %collective-permute-done.4.left_ref, bf16[80,128]{1,0:T(8,128)(2,1)S(1)} %collective-permute-done.5.right_ref, bf16[64,128]{1,0:T(8,128)(2,1)S(1)} %collective-permute-done.6.above_ref, ...), custom_call_target="tpu_custom_call", output_to_operand_aliasing={{}: (4, {})} | custom-call | tf_op jit(solution)/shard_map/pallas_call | solution.py:32
  (1 shorter events, 0.0 us)
Async XLA Ops:
  2.8 40.8 %copy-start = (s32[1,1024]{1,0:T(1,128)S(1)}, s32[1,1024]{1,0:T(1,128)}, u32[]{:S(2)}) copy-start(s32[1,1024]{1,0:T(1,128)} %get-tuple-element.33.place_ref) | copy-start | bytes 12292
  2.9 24.5 %all-to-all-start = ((f32[128,2,128]{2,1,0:T(2,128)}), f32[128,2,128]{2,1,0:T(2,128)S(1)}, u32[]{:S(2)}, u32[]{:S(2)}) async-start(f32[128,2,128]{2,1,0:T(2,128)} %bitcast.26), calls=%async_computation | async-start | bytes 262144 | tf_op jit(solution)/shard_map/all_to_all | solution.py:366
  14.4 11.0 %collective-permute-start = (bf16[64,128]{1,0:T(8,128)(2,1)S(1)}, bf16[64,128]{1,0:T(8,128)(2,1)S(1)}, u32[]{:S(2)}, u32[]{:S(2)}) collective-permute-start(bf16[64,128]{1,0:T(8,128)(2,1)S(1)} %get-tuple-element.27), channel_id=1, source_target_pairs={{0,4},{4,8},{8,12},{12,16},{16,20},{20,24},{24,28},{28,32},{32,36}... | collective-permute-start | bytes 49160 | tf_op jit(solution)/shard_map/ppermute | solution.py:362
  16.4 9.0 %collective-permute-start.1 = (bf16[64,128]{1,0:T(8,128)(2,1)S(1)}, bf16[64,128]{1,0:T(8,128)(2,1)S(1)}, u32[]{:S(2)}, u32[]{:S(2)}) collective-permute-start(bf16[64,128]{1,0:T(8,128)(2,1)S(1)} %get-tuple-element.28), channel_id=1, source_target_pairs={{4,0},{8,4},{12,8},{16,12},{20,16},{24,20},{28,24},{32,28},{36,32}... | collective-permute-start | bytes 49160 | tf_op jit(solution)/shard_map/ppermute | solution.py:362
  22.1 5.0 %collective-permute-start.2 = (bf16[64,128]{1,0:T(8,128)(2,1)S(1)}, bf16[64,128]{1,0:T(8,128)(2,1)S(1)}, u32[]{:S(2)}, u32[]{:S(2)}) collective-permute-start(bf16[64,128]{1,0:T(8,128)(2,1)S(1)} %get-tuple-element.29), channel_id=1, source_target_pairs={{0,1},{1,2},{2,3},{3,0},{4,5},{5,6},{6,7},{7,4},{8,9},{9,10},{10,1... | collective-permute-start | bytes 49160 | tf_op jit(solution)/shard_map/ppermute | solution.py:362
  23.6 3.7 %collective-permute-start.3 = (bf16[64,128]{1,0:T(8,128)(2,1)S(1)}, bf16[64,128]{1,0:T(8,128)(2,1)S(1)}, u32[]{:S(2)}, u32[]{:S(2)}) collective-permute-start(bf16[64,128]{1,0:T(8,128)(2,1)S(1)} %get-tuple-element.30), channel_id=1, source_target_pairs={{0,3},{1,0},{2,1},{3,2},{4,7},{5,4},{6,5},{7,6},{8,11},{9,8},{10,9... | collective-permute-start | bytes 49160 | tf_op jit(solution)/shard_map/ppermute | solution.py:362
  36.1 19.8 %all-to-all-start.1 = ((bf16[128,16,128]{2,1,0:T(8,128)(2,1)}), bf16[128,16,128]{2,1,0:T(8,128)(2,1)S(1)}, u32[]{:S(2)}, u32[]{:S(2)}) async-start(bf16[128,16,128]{2,1,0:T(8,128)(2,1)} %bitcast.24), calls=%async_computation.1 | async-start | bytes 1048576 | tf_op jit(solution)/shard_map/all_to_all | solution.py:366
  43.6 12.2 %copy-start.1 = (f32[512]{0:T(512)S(1)}, f32[512]{0:T(512)}, u32[]{:S(2)}) copy-start(f32[512]{0:T(512)} %param.21) | copy-start | bytes 6148
  43.6 12.2 %copy-start.2 = (f32[256]{0:T(256)S(1)}, f32[256]{0:T(256)}, u32[]{:S(2)}) copy-start(f32[256]{0:T(256)} %param.19) | copy-start | bytes 3076
  43.7 12.2 %copy-start.3 = (f32[256]{0:T(256)S(1)}, f32[256]{0:T(256)}, u32[]{:S(2)}) copy-start(f32[256]{0:T(256)} %param.23) | copy-start | bytes 3076
  62.7 18.7 %all-to-all-start.2 = ((bf16[128,16,128]{2,1,0:T(8,128)(2,1)}), bf16[128,16,128]{2,1,0:T(8,128)(2,1)S(1)}, u32[]{:S(2)}, u32[]{:S(2)}) async-start(bf16[128,16,128]{2,1,0:T(8,128)(2,1)} %bitcast.25), calls=%async_computation.2 | async-start | bytes 1048576 | tf_op jit(solution)/shard_map/all_to_all | solution.py:366
  81.9 6.6 %collective-permute-start.4 = (bf16[80,128]{1,0:T(8,128)(2,1)S(1)}, bf16[80,128]{1,0:T(8,128)(2,1)S(1)}, u32[]{:S(2)}, u32[]{:S(2)}) collective-permute-start(bf16[80,128]{1,0:T(8,128)(2,1)S(1)} %get-tuple-element.38), channel_id=1, source_target_pairs={{0,1},{1,2},{2,3},{3,0},{4,5},{5,6},{6,7},{7,4},{8,9},{9,10},{10,1... | collective-permute-start | bytes 61448 | tf_op jit(solution)/shard_map/ppermute | solution.py:362
  82.5 6.0 %collective-permute-start.5 = (bf16[80,128]{1,0:T(8,128)(2,1)S(1)}, bf16[80,128]{1,0:T(8,128)(2,1)S(1)}, u32[]{:S(2)}, u32[]{:S(2)}) collective-permute-start(bf16[80,128]{1,0:T(8,128)(2,1)S(1)} %get-tuple-element.39), channel_id=1, source_target_pairs={{0,3},{1,0},{2,1},{3,2},{4,7},{5,4},{6,5},{7,6},{8,11},{9,8},{10,9... | collective-permute-start | bytes 61448 | tf_op jit(solution)/shard_map/ppermute | solution.py:362
  88.5 11.0 %collective-permute-start.6 = (bf16[64,128]{1,0:T(8,128)(2,1)S(1)}, bf16[64,128]{1,0:T(8,128)(2,1)S(1)}, u32[]{:S(2)}, u32[]{:S(2)}) collective-permute-start(bf16[64,128]{1,0:T(8,128)(2,1)S(1)} %get-tuple-element.46), channel_id=1, source_target_pairs={{0,4},{4,8},{8,12},{12,16},{16,20},{20,24},{24,28},{28,32},{32,36}... | collective-permute-start | bytes 49160 | tf_op jit(solution)/shard_map/ppermute | solution.py:362
  90.5 9.1 %collective-permute-start.7 = (bf16[64,128]{1,0:T(8,128)(2,1)S(1)}, bf16[64,128]{1,0:T(8,128)(2,1)S(1)}, u32[]{:S(2)}, u32[]{:S(2)}) collective-permute-start(bf16[64,128]{1,0:T(8,128)(2,1)S(1)} %get-tuple-element.47), channel_id=1, source_target_pairs={{4,0},{8,4},{12,8},{16,12},{20,16},{24,20},{28,24},{32,28},{36,32}... | collective-permute-start | bytes 49160 | tf_op jit(solution)/shard_map/ppermute | solution.py:362

commit v6 on v5

--- a/solution.py
+++ b/solution.py
@@ -46,11 +46,14 @@
     return jnp.where((to >= 0) & (to < n_lat), to * n_lon + (lon + cols + n_lon) % n_lon, -1)
 
 
-def route_body(dest_ref, row_ref, col_ref, weight_ref, state_ref, send_ref, place_ref, cells, sems):
-    spots = [(0, 0), (0, 56), (63, 0), (63, 56)]
-    copies = [
-        pltpu.make_async_copy(state_ref.at[r, pl.ds(c, 8), :], cells.at[i], sems.at[i]) for i, (r, c) in enumerate(spots)
+def route_body(dest_ref, row_ref, col_ref, weight_ref, state_ref, send_ref, place_ref, first_ref, last_ref, head_ref, tail_ref, sides, rows, sems):
+    edges = [
+        (state_ref.at[:, pl.ds(0, 8), :], sides.at[0]),
+        (state_ref.at[:, pl.ds(56, 8), :], sides.at[1]),
+        (state_ref.at[0], rows.at[0]),
+        (state_ref.at[63], rows.at[1]),
     ]
+    copies = [pltpu.make_async_copy(a, b, sems.at[i]) for i, (a, b) in enumerate(edges)]
     for copy in copies:
         copy.start()
     dest = dest_ref[...]
@@ -73,30 +76,17 @@
     )
     for copy in copies:
         copy.wait()
-    row = iota((tiles, 128), 0)
-    extra = jnp.zeros((tiles, 128), F32)
-    for i, (r, c) in enumerate(spots):
-        cell = cells[i].astype(F32)[7 if c else 0][None]
-        extra = jnp.where(row == diagonal(1 if r else -1, 1 if c else -1), cell, extra)
-    send_ref[pl.ds(1, tiles, stride=2), :] = extra
-
-
-def border_body(state_ref, first_ref, last_ref, head_ref, tail_ref, sides, rows, sems):
-    edges = [
-        (state_ref.at[:, pl.ds(0, 8), :], sides.at[0]),
-        (state_ref.at[:, pl.ds(56, 8), :], sides.at[1]),
-        (state_ref.at[0], rows.at[0]),
-        (state_ref.at[63], rows.at[1]),
-    ]
-    copies = [pltpu.make_async_copy(a, b, sems.at[i]) for i, (a, b) in enumerate(edges)]
-    for copy in copies:
-        copy.start()
-    for copy in copies:
-        copy.wait()
     first_ref[...] = sides[0, :, 0, :]
     last_ref[...] = sides[1, :, 7, :]
     head_ref[...] = rows[0]
     tail_ref[...] = rows[1]
+    row = iota((tiles, 128), 0)
+    extra = jnp.zeros((tiles, 128), F32)
+    for r in range(2):
+        for c in range(2):
+            cell = sides[c, 63 * r].astype(F32)[7 * c][None]
+            extra = jnp.where(row == diagonal(2 * r - 1, 2 * c - 1), cell, extra)
+    send_ref[pl.ds(1, tiles, stride=2), :] = extra
 
 
 def fields_by_row(recv, first, count):
@@ -389,34 +379,27 @@
 
     vmem = pl.BlockSpec(memory_space=pltpu.VMEM)
     hbm = pl.BlockSpec(memory_space=pltpu.HBM)
-    send_meta, place = call(
+    send_meta, place, first, last, head, tail = call(
         route_body,
-        (pltpu.HBM((2 * tiles, 128), F32), sds((1, obs), I32)),
+        (pltpu.HBM((2 * tiles, 128), F32), sds((1, obs), I32)) + (sds((64, levels), BF16),) * 4,
         destination.reshape(1, obs),
         corner_row.reshape(1, obs),
         corner_col.reshape(1, obs),
         corner_weight.T,
         in_hbm(state),
         specs=[vmem] * 4 + [hbm],
-        scratch=[pltpu.VMEM((4, 8, levels), BF16), pltpu.SemaphoreType.DMA((4,))],
-        grant=None,
-    )
-    recv_meta = exchange(send_meta.reshape(tiles, 2, 128)).reshape(2 * tiles, 128)
-    first, last, head, tail = call(
-        border_body,
-        (sds((64, levels), BF16),) * 4,
-        in_hbm(state),
-        specs=[hbm],
         scratch=[
             pltpu.VMEM((2, 64, 8, levels), BF16),
             pltpu.VMEM((2, 64, levels), BF16),
             pltpu.SemaphoreType.DMA((4,)),
         ],
-    )
+        grant=None,
+    )
+    recv_meta = exchange(send_meta.reshape(tiles, 2, 128)).reshape(2 * tiles, 128)
+    left = shift(last, "lon", 1, True)
+    right = shift(first, "lon", -1, True)
     top = shift(tail, "lat", 1, False)
     bottom = shift(head, "lat", -1, False)
-    left = shift(last, "lon", 1, True)
-    right = shift(first, "lon", -1, True)
 
     columns = call(
         gather_body,

time: 103 us -> 102 us (level)
    pallas_call x11 -> x10, Pallas kernels: 37.2 us -> 36.4 us  [call(): pl.pallas_call(body, in_specs=specs or [vmem] * len(args), out_specs=outs...]
  transfers between devices with their start and end apart: 11 -> 11, of which waited for: 4 -> 4; matrix products, arithmetic and copies ran while one was open for 0% -> 0% of each run, Pallas kernels for 17% -> 16%
where the time goes in v6:
time: 102 us; the launch traced here: 101 us
  starting transfers between devices  46.5 us (46%)
  Pallas kernels  36.4 us (36%)
  waiting for transfers between devices  17.3 us (17%)
    pallas_call x10, Pallas kernels, call(): pl.pallas_call(body, in_specs=specs or [vmem] * len(args), out_specs=outs...  36.4 us
    all_to_all x3, starting transfers between devices, exchange(): return lax.all_to_all(x, AXES, split_axis=0, concat_axis=0, tiled=True)  24.5 us
    ppermute x8, starting transfers between devices, shift(): return lax.ppermute(x, axis, pairs)  22 us
    all_to_all x3, waiting for transfers between devices, exchange(): return lax.all_to_all(x, AXES, split_axis=0, concat_axis=0, tiled=True)  15.1 us
    ppermute x8, waiting for transfers between devices, shift(): return lax.ppermute(x, axis, pairs)  2.19 us
  transfers between devices with their start and end apart: 11, of which 4 were waited for; matrix products, arithmetic and copies ran while one was open for 0% of the time, Pallas kernels for 16%

profile of v6, /device:TPU:6, one launch (start us, length us, event | category | flops | bytes accessed | tf_op | source)
XLA Modules:
  0.0 101.2 jit_solution(10863230274593783558)
XLA Ops:
  0.6 2.5 %shard_map.131 = (f32[256,128]{1,0:T(8,128)}, s32[1,1024]{1,0:T(1,128)}, bf16[64,128]{1,0:T(8,128)(2,1)}, bf16[64,128]{1,0:T(8,128)(2,1)}, bf16[64,128]{1,0:T(8,128)(2,1)}, /*index=5*/bf16[64,128]{1,0:T(8,128)(2,1)}) custom-call(s32[1,1024]{1,0:T(1,128)} %bitcast.28, s32[1,1024]{1,0:T(1,128)} %bitcast.29, s32[1,1024]{1,0:T(1,128)} %bitcast.30, ...), custom_call_target="tpu_custom_call" | custom-call | tf_op jit(solution)/shard_map/pallas_call | solution.py:32
  3.1 0.0 copy-start
  3.1 10.5 %all-to-all-start = ((f32[128,2,128]{2,1,0:T(2,128)}), f32[128,2,128]{2,1,0:T(2,128)S(1)}, u32[]{:S(2)}, u32[]{:S(2)}) async-start(f32[128,2,128]{2,1,0:T(2,128)} %bitcast.26), calls=%async_computation | async-start | bytes 262144 | tf_op jit(solution)/shard_map/all_to_all | solution.py:356
  13.6 2.0 %collective-permute-start = (bf16[64,128]{1,0:T(8,128)(2,1)}, bf16[64,128]{1,0:T(8,128)(2,1)S(1)}, u32[]{:S(2)}, u32[]{:S(2)}) collective-permute-start(bf16[64,128]{1,0:T(8,128)(2,1)} %get-tuple-element.27), channel_id=1, source_target_pairs={{0,4},{4,8},{8,12},{12,16},{16,20},{20,24},{24,28},{28,32},{32,36}... | collective-permute-start | bytes 49160 | tf_op jit(solution)/shard_map/ppermute | solution.py:352
  15.7 5.6 %collective-permute-start.1 = (bf16[64,128]{1,0:T(8,128)(2,1)}, bf16[64,128]{1,0:T(8,128)(2,1)S(1)}, u32[]{:S(2)}, u32[]{:S(2)}) collective-permute-start(bf16[64,128]{1,0:T(8,128)(2,1)} %get-tuple-element.28), channel_id=1, source_target_pairs={{4,0},{8,4},{12,8},{16,12},{20,16},{24,20},{28,24},{32,28},{36,32}... | collective-permute-start | bytes 49160 | tf_op jit(solution)/shard_map/ppermute | solution.py:352
  21.3 1.5 %collective-permute-start.2 = (bf16[64,128]{1,0:T(8,128)(2,1)}, bf16[64,128]{1,0:T(8,128)(2,1)S(1)}, u32[]{:S(2)}, u32[]{:S(2)}) collective-permute-start(bf16[64,128]{1,0:T(8,128)(2,1)} %get-tuple-element.29), channel_id=1, source_target_pairs={{0,1},{1,2},{2,3},{3,0},{4,5},{5,6},{6,7},{7,4},{8,9},{9,10},{10,1... | collective-permute-start | bytes 49160 | tf_op jit(solution)/shard_map/ppermute | solution.py:352
  22.9 1.8 %collective-permute-start.3 = (bf16[64,128]{1,0:T(8,128)(2,1)}, bf16[64,128]{1,0:T(8,128)(2,1)S(1)}, u32[]{:S(2)}, u32[]{:S(2)}) collective-permute-start(bf16[64,128]{1,0:T(8,128)(2,1)} %get-tuple-element.30), channel_id=1, source_target_pairs={{0,3},{1,0},{2,1},{3,2},{4,7},{5,4},{6,5},{7,6},{8,11},{9,8},{10,9... | collective-permute-start | bytes 49160 | tf_op jit(solution)/shard_map/ppermute | solution.py:352
  24.6 0.0 collective-permute-done.top_ref
  24.6 0.0 collective-permute-done.1.bottom_ref
  24.6 1.9 %collective-permute-done.2.left_ref = bf16[64,128]{1,0:T(8,128)(2,1)S(1)} collective-permute-done((bf16[64,128]{1,0:T(8,128)(2,1)}, bf16[64,128]{1,0:T(8,128)(2,1)S(1)}, u32[]{:S(2)}, u32[]{:S(2)}) %collective-permute-start.2) | collective-permute-done | bytes 16416 | tf_op jit(solution)/shard_map/ppermute | solution.py:352
  26.6 0.3 collective-permute-done.3.right_ref
  26.8 0.0 all-to-all-done
  26.8 8.7 %shard_map.132 = bf16[2048,128]{1,0:T(8,128)(2,1)} custom-call(f32[256,128]{1,0:T(8,128)S(1)} %bitcast.18, bf16[4096,128]{1,0:T(8,128)(2,1)} %bitcast.23, bf16[64,128]{1,0:T(8,128)(2,1)S(1)} %collective-permute-done.top_ref, bf16[64,128]{1,0:T(8,128)(2,1)S(1)} %collective-permute-done.1.bottom_ref, bf16[64,128]{1,0:T(8,128)(2,1)S(1)} %collective-permute-done.2.left_ref, ...), custom_call_target="tpu_custom_call" | custom-call | tf_op jit(solution)/shard_map/pallas_call | solution.py:32
  35.5 7.5 %all-to-all-start.1 = ((bf16[128,16,128]{2,1,0:T(8,128)(2,1)}), bf16[128,16,128]{2,1,0:T(8,128)(2,1)S(1)}, u32[]{:S(2)}, u32[]{:S(2)}) async-start(bf16[128,16,128]{2,1,0:T(8,128)(2,1)} %bitcast.24), calls=%async_computation.1 | async-start | bytes 1048576 | tf_op jit(solution)/shard_map/all_to_all | solution.py:356
  43.1 0.0 copy-done
  43.1 0.0 copy-start.1
  43.1 0.0 copy-start.2
  43.1 0.0 copy-start.3
  43.1 8.9 %shard_map.133.pcs_ref = bf16[1024,256]{1,0:T(8,128)(2,1)S(1)} custom-call(bf16[1024,8448]{1,0:T(8,128)(2,1)} %spectra_ref.1, bf16[8448,256]{1,0:T(8,128)(2,1)} %basis_ref.1, s32[1,1024]{1,0:T(1,128)S(1)} %copy-done), custom_call_target="tpu_custom_call" | custom-call | tf_op jit(solution)/shard_map/pallas_call | solution.py:32
  52.0 3.3 %all-to-all-done.1 = bf16[128,16,128]{2,1,0:T(8,128)(2,1)S(1)} async-done(((bf16[128,16,128]{2,1,0:T(8,128)(2,1)}), bf16[128,16,128]{2,1,0:T(8,128)(2,1)S(1)}, u32[]{:S(2)}, u32[]{:S(2)}) %all-to-all-start.1) | async-done | bytes 524320 | tf_op jit(solution)/shard_map/all_to_all | solution.py:356
  55.3 0.0 copy-done.1
  55.3 0.0 copy-done.2
  55.3 0.0 copy-done.3
  55.3 6.8 %shard_map.134 = (bf16[1024,256]{1,0:T(8,128)(2,1)}, bf16[2048,128]{1,0:T(8,128)(2,1)}) custom-call(bf16[2048,128]{1,0:T(8,128)(2,1)S(1)} %bitcast.17, s32[1,1024]{1,0:T(1,128)S(1)} %copy-done, bf16[1024,256]{1,0:T(8,128)(2,1)S(1)} %shard_map.133.pcs_ref, f32[1,256]{1,0:T(1,128)S(1)} %bitcast.21, bf16[128,512]{1,0:T(8,128)(2,1)} %w_in_hbm.1, ...), custom_call_target="tpu_custom_call" | custom-call | tf_op jit(solution)/shard_map/pallas_call | solution.py:32
  62.1 6.5 %all-to-all-start.2 = ((bf16[128,16,128]{2,1,0:T(8,128)(2,1)}), bf16[128,16,128]{2,1,0:T(8,128)(2,1)S(1)}, u32[]{:S(2)}, u32[]{:S(2)}) async-start(bf16[128,16,128]{2,1,0:T(8,128)(2,1)} %bitcast.25), calls=%async_computation.2 | async-start | bytes 1048576 | tf_op jit(solution)/shard_map/all_to_all | solution.py:356
  68.6 0.5 shard_map.135.fields_ref
  69.0 11.8 %all-to-all-done.2 = bf16[128,16,128]{2,1,0:T(8,128)(2,1)S(1)} async-done(((bf16[128,16,128]{2,1,0:T(8,128)(2,1)}), bf16[128,16,128]{2,1,0:T(8,128)(2,1)S(1)}, u32[]{:S(2)}, u32[]{:S(2)}) %all-to-all-start.2) | async-done | bytes 524320 | tf_op jit(solution)/shard_map/all_to_all | solution.py:356
  80.8 0.5 shard_map.136
  81.3 0.6 collective-permute-start.4
  82.0 2.7 %collective-permute-start.5 = (bf16[80,128]{1,0:T(8,128)(2,1)S(1)}, bf16[80,128]{1,0:T(8,128)(2,1)S(1)}, u32[]{:S(2)}, u32[]{:S(2)}) collective-permute-start(bf16[80,128]{1,0:T(8,128)(2,1)S(1)} %get-tuple-element.39), channel_id=1, source_target_pairs={{0,3},{1,0},{2,1},{3,2},{4,7},{5,4},{6,5},{7,6},{8,11},{9,8},{10,9... | collective-permute-start | bytes 61448 | tf_op jit(solution)/shard_map/ppermute | solution.py:352
  84.6 3.3 %shard_map.137.refs_0_ = f32[64,64,128]{2,1,0:T(8,128)} custom-call(f32[8,2048]{1,0:T(8,128)S(1)} %shard_map.135.fields_ref, bf16[2048,128]{1,0:T(8,128)(2,1)S(1)} %bitcast.15), custom_call_target="tpu_custom_call" | custom-call | tf_op jit(solution)/shard_map/pallas_call | solution.py:32
  87.9 0.0 collective-permute-done.4.left_ref
  88.0 0.0 collective-permute-done.5.right_ref
  88.0 1.9 %collective-permute-start.6 = (bf16[64,128]{1,0:T(8,128)(2,1)S(1)}, bf16[64,128]{1,0:T(8,128)(2,1)S(1)}, u32[]{:S(2)}, u32[]{:S(2)}) collective-permute-start(bf16[64,128]{1,0:T(8,128)(2,1)S(1)} %get-tuple-element.46), channel_id=1, source_target_pairs={{0,4},{4,8},{8,12},{12,16},{16,20},{20,24},{24,28},{28,32},{32,36}... | collective-permute-start | bytes 49160 | tf_op jit(solution)/shard_map/ppermute | solution.py:352
  89.9 5.8 %collective-permute-start.7 = (bf16[64,128]{1,0:T(8,128)(2,1)S(1)}, bf16[64,128]{1,0:T(8,128)(2,1)S(1)}, u32[]{:S(2)}, u32[]{:S(2)}) collective-permute-start(bf16[64,128]{1,0:T(8,128)(2,1)S(1)} %get-tuple-element.47), channel_id=1, source_target_pairs={{4,0},{8,4},{12,8},{16,12},{20,16},{24,20},{28,24},{32,28},{36,32}... | collective-permute-start | bytes 49160 | tf_op jit(solution)/shard_map/ppermute | solution.py:352
  95.7 3.3 %shard_map.139.grad_ref = f32[64,64,128]{2,1,0:T(8,128)} custom-call(f32[8,2048]{1,0:T(8,128)S(1)} %shard_map.135.fields_ref, bf16[2048,128]{1,0:T(8,128)(2,1)S(1)} %bitcast.16, f32[64,64,128]{2,1,0:T(8,128)} %shard_map.137.refs_0_), custom_call_target="tpu_custom_call", output_to_operand_aliasing={{}: (2, {})} | custom-call | tf_op jit(solution)/shard_map/pallas_call | solution.py:32
  99.0 0.0 collective-permute-done.6.above_ref
  99.0 0.0 collective-permute-done.7.below_ref
  99.0 2.0 %shard_map.140 = f32[64,64,128]{2,1,0:T(8,128)} custom-call(bf16[80,128]{1,0:T(8,128)(2,1)S(1)} %collective-permute-done.4.left_ref, bf16[80,128]{1,0:T(8,128)(2,1)S(1)} %collective-permute-done.5.right_ref, bf16[64,128]{1,0:T(8,128)(2,1)S(1)} %collective-permute-done.6.above_ref, ...), custom_call_target="tpu_custom_call", output_to_operand_aliasing={{}: (4, {})} | custom-call | tf_op jit(solution)/shard_map/pallas_call | solution.py:32
  (1 shorter events, 0.0 us)
Async XLA Ops:
  3.1 39.9 %copy-start = (s32[1,1024]{1,0:T(1,128)S(1)}, s32[1,1024]{1,0:T(1,128)}, u32[]{:S(2)}) copy-start(s32[1,1024]{1,0:T(1,128)} %get-tuple-element.33.place_ref) | copy-start | bytes 12292
  3.1 23.7 %all-to-all-start = ((f32[128,2,128]{2,1,0:T(2,128)}), f32[128,2,128]{2,1,0:T(2,128)S(1)}, u32[]{:S(2)}, u32[]{:S(2)}) async-start(f32[128,2,128]{2,1,0:T(2,128)} %bitcast.26), calls=%async_computation | async-start | bytes 262144 | tf_op jit(solution)/shard_map/all_to_all | solution.py:356
  13.6 11.0 %collective-permute-start = (bf16[64,128]{1,0:T(8,128)(2,1)}, bf16[64,128]{1,0:T(8,128)(2,1)S(1)}, u32[]{:S(2)}, u32[]{:S(2)}) collective-permute-start(bf16[64,128]{1,0:T(8,128)(2,1)} %get-tuple-element.27), channel_id=1, source_target_pairs={{0,4},{4,8},{8,12},{12,16},{16,20},{20,24},{24,28},{28,32},{32,36}... | collective-permute-start | bytes 49160 | tf_op jit(solution)/shard_map/ppermute | solution.py:352
  15.7 9.0 %collective-permute-start.1 = (bf16[64,128]{1,0:T(8,128)(2,1)}, bf16[64,128]{1,0:T(8,128)(2,1)S(1)}, u32[]{:S(2)}, u32[]{:S(2)}) collective-permute-start(bf16[64,128]{1,0:T(8,128)(2,1)} %get-tuple-element.28), channel_id=1, source_target_pairs={{4,0},{8,4},{12,8},{16,12},{20,16},{24,20},{28,24},{32,28},{36,32}... | collective-permute-start | bytes 49160 | tf_op jit(solution)/shard_map/ppermute | solution.py:352
  21.3 5.2 %collective-permute-start.2 = (bf16[64,128]{1,0:T(8,128)(2,1)}, bf16[64,128]{1,0:T(8,128)(2,1)S(1)}, u32[]{:S(2)}, u32[]{:S(2)}) collective-permute-start(bf16[64,128]{1,0:T(8,128)(2,1)} %get-tuple-element.29), channel_id=1, source_target_pairs={{0,1},{1,2},{2,3},{3,0},{4,5},{5,6},{6,7},{7,4},{8,9},{9,10},{10,1... | collective-permute-start | bytes 49160 | tf_op jit(solution)/shard_map/ppermute | solution.py:352
  22.9 3.9 %collective-permute-start.3 = (bf16[64,128]{1,0:T(8,128)(2,1)}, bf16[64,128]{1,0:T(8,128)(2,1)S(1)}, u32[]{:S(2)}, u32[]{:S(2)}) collective-permute-start(bf16[64,128]{1,0:T(8,128)(2,1)} %get-tuple-element.30), channel_id=1, source_target_pairs={{0,3},{1,0},{2,1},{3,2},{4,7},{5,4},{6,5},{7,6},{8,11},{9,8},{10,9... | collective-permute-start | bytes 49160 | tf_op jit(solution)/shard_map/ppermute | solution.py:352
  35.5 19.8 %all-to-all-start.1 = ((bf16[128,16,128]{2,1,0:T(8,128)(2,1)}), bf16[128,16,128]{2,1,0:T(8,128)(2,1)S(1)}, u32[]{:S(2)}, u32[]{:S(2)}) async-start(bf16[128,16,128]{2,1,0:T(8,128)(2,1)} %bitcast.24), calls=%async_computation.1 | async-start | bytes 1048576 | tf_op jit(solution)/shard_map/all_to_all | solution.py:356
  43.1 12.2 %copy-start.1 = (f32[512]{0:T(512)S(1)}, f32[512]{0:T(512)}, u32[]{:S(2)}) copy-start(f32[512]{0:T(512)} %param.21) | copy-start | bytes 6148
  43.1 12.2 %copy-start.2 = (f32[256]{0:T(256)S(1)}, f32[256]{0:T(256)}, u32[]{:S(2)}) copy-start(f32[256]{0:T(256)} %param.19) | copy-start | bytes 3076
  43.1 12.2 %copy-start.3 = (f32[256]{0:T(256)S(1)}, f32[256]{0:T(256)}, u32[]{:S(2)}) copy-start(f32[256]{0:T(256)} %param.23) | copy-start | bytes 3076
  62.1 18.7 %all-to-all-start.2 = ((bf16[128,16,128]{2,1,0:T(8,128)(2,1)}), bf16[128,16,128]{2,1,0:T(8,128)(2,1)S(1)}, u32[]{:S(2)}, u32[]{:S(2)}) async-start(bf16[128,16,128]{2,1,0:T(8,128)(2,1)} %bitcast.25), calls=%async_computation.2 | async-start | bytes 1048576 | tf_op jit(solution)/shard_map/all_to_all | solution.py:356
  81.3 6.6 %collective-permute-start.4 = (bf16[80,128]{1,0:T(8,128)(2,1)S(1)}, bf16[80,128]{1,0:T(8,128)(2,1)S(1)}, u32[]{:S(2)}, u32[]{:S(2)}) collective-permute-start(bf16[80,128]{1,0:T(8,128)(2,1)S(1)} %get-tuple-element.38), channel_id=1, source_target_pairs={{0,1},{1,2},{2,3},{3,0},{4,5},{5,6},{6,7},{7,4},{8,9},{9,10},{10,1... | collective-permute-start | bytes 61448 | tf_op jit(solution)/shard_map/ppermute | solution.py:352
  82.0 6.0 %collective-permute-start.5 = (bf16[80,128]{1,0:T(8,128)(2,1)S(1)}, bf16[80,128]{1,0:T(8,128)(2,1)S(1)}, u32[]{:S(2)}, u32[]{:S(2)}) collective-permute-start(bf16[80,128]{1,0:T(8,128)(2,1)S(1)} %get-tuple-element.39), channel_id=1, source_target_pairs={{0,3},{1,0},{2,1},{3,2},{4,7},{5,4},{6,5},{7,6},{8,11},{9,8},{10,9... | collective-permute-start | bytes 61448 | tf_op jit(solution)/shard_map/ppermute | solution.py:352
  88.0 11.0 %collective-permute-start.6 = (bf16[64,128]{1,0:T(8,128)(2,1)S(1)}, bf16[64,128]{1,0:T(8,128)(2,1)S(1)}, u32[]{:S(2)}, u32[]{:S(2)}) collective-permute-start(bf16[64,128]{1,0:T(8,128)(2,1)S(1)} %get-tuple-element.46), channel_id=1, source_target_pairs={{0,4},{4,8},{8,12},{12,16},{16,20},{20,24},{24,28},{28,32},{32,36}... | collective-permute-start | bytes 49160 | tf_op jit(solution)/shard_map/ppermute | solution.py:352
  89.9 9.1 %collective-permute-start.7 = (bf16[64,128]{1,0:T(8,128)(2,1)S(1)}, bf16[64,128]{1,0:T(8,128)(2,1)S(1)}, u32[]{:S(2)}, u32[]{:S(2)}) collective-permute-start(bf16[64,128]{1,0:T(8,128)(2,1)S(1)} %get-tuple-element.47), channel_id=1, source_target_pairs={{4,0},{8,4},{12,8},{16,12},{20,16},{24,20},{28,24},{32,28},{36,32}... | collective-permute-start | bytes 49160 | tf_op jit(solution)/shard_map/ppermute | solution.py:352

commit v7 on v6

--- a/solution.py
+++ b/solution.py
@@ -114,8 +114,8 @@
 
 
 def gather_body(recv_ref, own_hbm, top_ref, bottom_ref, left_ref, right_ref, out_ref, own_ref, buffer, own_sem, out_sems, rim_ref, *matrices):
-    slots = out_ref.shape[0]
-    chunk = matrices[0].shape[0]
+    sizes = [m.shape[0] for m in matrices]
+    firsts = [sum(sizes[:i]) for i in range(len(sizes))]
     load = pltpu.make_async_copy(own_hbm, own_ref, own_sem)
     load.start()
     rim_ref[0:64, :] = top_ref[...]
@@ -130,13 +130,15 @@
         rim_ref[256 + 16 * i : 272 + 16 * i, :] = mm(ones_where(lane == source), cells).astype(BF16)
     rim_ref[288:384, :] = jnp.zeros((96, rim_ref.shape[1]), BF16)
     recv = recv_ref[pl.ds(0, tiles, stride=2), :].astype(BF16)
-    lane = iota((chunk, 128), 1).astype(F32)
-    upper = jnp.where(lane >= 64.0, 1.0, 0.0)
-    in_row = (lane - 64.0 * upper).astype(BF16)
-    upper = upper.astype(BF16)
-    lane = lane.astype(BF16)
+    lanes = iota((max(sizes), 128), 1).astype(F32)
+    upper = jnp.where(lanes >= 64.0, 1.0, 0.0)
+    in_rows = (lanes - 64.0 * upper).astype(BF16)
+    uppers = upper.astype(BF16)
+    lanes = lanes.astype(BF16)
 
     def build(first, matrix_ref):
+        chunk = matrix_ref.shape[0]
+        lane, in_row, upper = lanes[:chunk], in_rows[:chunk], uppers[:chunk]
         w0, w1, w2, w3, row, col = [f.astype(BF16) for f in fields_by_row(recv, first, chunk)]
         at0, at1 = in_row == col - 1.0, in_row == col
         p0 = pair_of(at0, w0, at1, w2)
@@ -157,19 +159,19 @@
 
     def use(first, matrix_ref):
         out = mm(matrix_ref[:, :4096], own_ref[...]) + mm(matrix_ref[:, 4096:], rim_ref[...])
-        at = slice(first, first + chunk)
+        at = slice(first, first + matrix_ref.shape[0])
         buffer[at, :] = out.astype(BF16)
         copies.append(pltpu.make_async_copy(buffer.at[at, :], out_ref.at[at, :], out_sems.at[len(copies)]))
         copies[-1].start()
 
     copies = []
-    count = slots // chunk
+    count = len(sizes)
     build(0, matrices[0])
     load.wait()
     for i in range(count):
         if i + 1 < count:
-            build((i + 1) * chunk, matrices[i + 1])
-        use(i * chunk, matrices[i])
+            build(firsts[i + 1], matrices[i + 1])
+        use(firsts[i], matrices[i])
     for copy in copies:
         copy.wait()
 
@@ -416,10 +418,10 @@
             pltpu.VMEM((4096, levels), BF16),
             pltpu.VMEM((slots, levels), BF16),
             pltpu.SemaphoreType.DMA,
-            pltpu.SemaphoreType.DMA((4,)),
+            pltpu.SemaphoreType.DMA((5,)),
             pltpu.VMEM((384, levels), BF16),
         ]
-        + [pltpu.VMEM((slots // 4, 4480), BF16)] * 4,
+        + [pltpu.VMEM((slots // n, 4480), BF16) for n in (8, 4, 4, 4, 8)],
         grant=28,
     )
     columns, place = lax.optimization_barrier((columns, place))

time: 102 us -> 102 us (level)
  no operation moved by 1% of the time
where the time goes in v7:
time: 102 us; the launch traced here: 101 us
  starting transfers between devices  46.5 us (46%)
  Pallas kernels  36.2 us (35%)
  waiting for transfers between devices  17.3 us (17%)
    pallas_call x10, Pallas kernels, call(): pl.pallas_call(body, in_specs=specs or [vmem] * len(args), out_specs=outs...  36.2 us
    all_to_all x3, starting transfers between devices, exchange(): return lax.all_to_all(x, AXES, split_axis=0, concat_axis=0, tiled=True)  24.5 us
    ppermute x8, starting transfers between devices, shift(): return lax.ppermute(x, axis, pairs)  22 us
    all_to_all x3, waiting for transfers between devices, exchange(): return lax.all_to_all(x, AXES, split_axis=0, concat_axis=0, tiled=True)  15.1 us
    ppermute x8, waiting for transfers between devices, shift(): return lax.ppermute(x, axis, pairs)  2.19 us
  transfers between devices with their start and end apart: 11, of which 4 were waited for; matrix products, arithmetic and copies ran while one was open for 0% of the time, Pallas kernels for 16%

profile of v7, /device:TPU:6, one launch (start us, length us, event | category | flops | bytes accessed | tf_op | source)
XLA Modules:
  0.0 101.0 jit_solution(12041801985546885681)
XLA Ops:
  0.6 2.5 %shard_map.131 = (f32[256,128]{1,0:T(8,128)}, s32[1,1024]{1,0:T(1,128)}, bf16[64,128]{1,0:T(8,128)(2,1)}, bf16[64,128]{1,0:T(8,128)(2,1)}, bf16[64,128]{1,0:T(8,128)(2,1)}, /*index=5*/bf16[64,128]{1,0:T(8,128)(2,1)}) custom-call(s32[1,1024]{1,0:T(1,128)} %bitcast.28, s32[1,1024]{1,0:T(1,128)} %bitcast.29, s32[1,1024]{1,0:T(1,128)} %bitcast.30, ...), custom_call_target="tpu_custom_call" | custom-call | tf_op jit(solution)/shard_map/pallas_call | solution.py:32
  3.1 0.0 copy-start
  3.1 10.5 %all-to-all-start = ((f32[128,2,128]{2,1,0:T(2,128)}), f32[128,2,128]{2,1,0:T(2,128)S(1)}, u32[]{:S(2)}, u32[]{:S(2)}) async-start(f32[128,2,128]{2,1,0:T(2,128)} %bitcast.26), calls=%async_computation | async-start | bytes 262144 | tf_op jit(solution)/shard_map/all_to_all | solution.py:358
  13.6 2.0 %collective-permute-start = (bf16[64,128]{1,0:T(8,128)(2,1)}, bf16[64,128]{1,0:T(8,128)(2,1)S(1)}, u32[]{:S(2)}, u32[]{:S(2)}) collective-permute-start(bf16[64,128]{1,0:T(8,128)(2,1)} %get-tuple-element.27), channel_id=1, source_target_pairs={{0,4},{4,8},{8,12},{12,16},{16,20},{20,24},{24,28},{28,32},{32,36}... | collective-permute-start | bytes 49160 | tf_op jit(solution)/shard_map/ppermute | solution.py:354
  15.7 5.6 %collective-permute-start.1 = (bf16[64,128]{1,0:T(8,128)(2,1)}, bf16[64,128]{1,0:T(8,128)(2,1)S(1)}, u32[]{:S(2)}, u32[]{:S(2)}) collective-permute-start(bf16[64,128]{1,0:T(8,128)(2,1)} %get-tuple-element.28), channel_id=1, source_target_pairs={{4,0},{8,4},{12,8},{16,12},{20,16},{24,20},{28,24},{32,28},{36,32}... | collective-permute-start | bytes 49160 | tf_op jit(solution)/shard_map/ppermute | solution.py:354
  21.3 1.5 %collective-permute-start.2 = (bf16[64,128]{1,0:T(8,128)(2,1)}, bf16[64,128]{1,0:T(8,128)(2,1)S(1)}, u32[]{:S(2)}, u32[]{:S(2)}) collective-permute-start(bf16[64,128]{1,0:T(8,128)(2,1)} %get-tuple-element.29), channel_id=1, source_target_pairs={{0,1},{1,2},{2,3},{3,0},{4,5},{5,6},{6,7},{7,4},{8,9},{9,10},{10,1... | collective-permute-start | bytes 49160 | tf_op jit(solution)/shard_map/ppermute | solution.py:354
  22.9 1.8 %collective-permute-start.3 = (bf16[64,128]{1,0:T(8,128)(2,1)}, bf16[64,128]{1,0:T(8,128)(2,1)S(1)}, u32[]{:S(2)}, u32[]{:S(2)}) collective-permute-start(bf16[64,128]{1,0:T(8,128)(2,1)} %get-tuple-element.30), channel_id=1, source_target_pairs={{0,3},{1,0},{2,1},{3,2},{4,7},{5,4},{6,5},{7,6},{8,11},{9,8},{10,9... | collective-permute-start | bytes 49160 | tf_op jit(solution)/shard_map/ppermute | solution.py:354
  24.6 0.0 collective-permute-done.top_ref
  24.6 0.0 collective-permute-done.1.bottom_ref
  24.6 1.9 %collective-permute-done.2.left_ref = bf16[64,128]{1,0:T(8,128)(2,1)S(1)} collective-permute-done((bf16[64,128]{1,0:T(8,128)(2,1)}, bf16[64,128]{1,0:T(8,128)(2,1)S(1)}, u32[]{:S(2)}, u32[]{:S(2)}) %collective-permute-start.2) | collective-permute-done | bytes 16416 | tf_op jit(solution)/shard_map/ppermute | solution.py:354
  26.6 0.3 collective-permute-done.3.right_ref
  26.8 0.0 all-to-all-done
  26.8 8.5 %shard_map.132 = bf16[2048,128]{1,0:T(8,128)(2,1)} custom-call(f32[256,128]{1,0:T(8,128)S(1)} %bitcast.18, bf16[4096,128]{1,0:T(8,128)(2,1)} %bitcast.23, bf16[64,128]{1,0:T(8,128)(2,1)S(1)} %collective-permute-done.top_ref, bf16[64,128]{1,0:T(8,128)(2,1)S(1)} %collective-permute-done.1.bottom_ref, bf16[64,128]{1,0:T(8,128)(2,1)S(1)} %collective-permute-done.2.left_ref, ...), custom_call_target="tpu_custom_call" | custom-call | tf_op jit(solution)/shard_map/pallas_call | solution.py:32
  35.4 7.5 %all-to-all-start.1 = ((bf16[128,16,128]{2,1,0:T(8,128)(2,1)}), bf16[128,16,128]{2,1,0:T(8,128)(2,1)S(1)}, u32[]{:S(2)}, u32[]{:S(2)}) async-start(bf16[128,16,128]{2,1,0:T(8,128)(2,1)} %bitcast.24), calls=%async_computation.1 | async-start | bytes 1048576 | tf_op jit(solution)/shard_map/all_to_all | solution.py:358
  42.9 0.0 copy-done
  42.9 0.0 copy-start.1
  42.9 0.0 copy-start.2
  43.0 0.0 copy-start.3
  43.0 8.9 %shard_map.133.pcs_ref = bf16[1024,256]{1,0:T(8,128)(2,1)S(1)} custom-call(bf16[1024,8448]{1,0:T(8,128)(2,1)} %spectra_ref.1, bf16[8448,256]{1,0:T(8,128)(2,1)} %basis_ref.1, s32[1,1024]{1,0:T(1,128)S(1)} %copy-done), custom_call_target="tpu_custom_call" | custom-call | tf_op jit(solution)/shard_map/pallas_call | solution.py:32
  51.8 3.3 %all-to-all-done.1 = bf16[128,16,128]{2,1,0:T(8,128)(2,1)S(1)} async-done(((bf16[128,16,128]{2,1,0:T(8,128)(2,1)}), bf16[128,16,128]{2,1,0:T(8,128)(2,1)S(1)}, u32[]{:S(2)}, u32[]{:S(2)}) %all-to-all-start.1) | async-done | bytes 524320 | tf_op jit(solution)/shard_map/all_to_all | solution.py:358
  55.2 0.0 copy-done.1
  55.2 0.0 copy-done.2
  55.2 0.0 copy-done.3
  55.2 6.8 %shard_map.134 = (bf16[1024,256]{1,0:T(8,128)(2,1)}, bf16[2048,128]{1,0:T(8,128)(2,1)}) custom-call(bf16[2048,128]{1,0:T(8,128)(2,1)S(1)} %bitcast.17, s32[1,1024]{1,0:T(1,128)S(1)} %copy-done, bf16[1024,256]{1,0:T(8,128)(2,1)S(1)} %shard_map.133.pcs_ref, f32[1,256]{1,0:T(1,128)S(1)} %bitcast.21, bf16[128,512]{1,0:T(8,128)(2,1)} %w_in_hbm.1, ...), custom_call_target="tpu_custom_call" | custom-call | tf_op jit(solution)/shard_map/pallas_call | solution.py:32
  61.9 6.5 %all-to-all-start.2 = ((bf16[128,16,128]{2,1,0:T(8,128)(2,1)}), bf16[128,16,128]{2,1,0:T(8,128)(2,1)S(1)}, u32[]{:S(2)}, u32[]{:S(2)}) async-start(bf16[128,16,128]{2,1,0:T(8,128)(2,1)} %bitcast.25), calls=%async_computation.2 | async-start | bytes 1048576 | tf_op jit(solution)/shard_map/all_to_all | solution.py:358
  68.4 0.4 shard_map.135.fields_ref
  68.9 11.8 %all-to-all-done.2 = bf16[128,16,128]{2,1,0:T(8,128)(2,1)S(1)} async-done(((bf16[128,16,128]{2,1,0:T(8,128)(2,1)}), bf16[128,16,128]{2,1,0:T(8,128)(2,1)S(1)}, u32[]{:S(2)}, u32[]{:S(2)}) %all-to-all-start.2) | async-done | bytes 524320 | tf_op jit(solution)/shard_map/all_to_all | solution.py:358
  80.7 0.5 shard_map.136
  81.2 0.6 collective-permute-start.4
  81.8 2.7 %collective-permute-start.5 = (bf16[80,128]{1,0:T(8,128)(2,1)S(1)}, bf16[80,128]{1,0:T(8,128)(2,1)S(1)}, u32[]{:S(2)}, u32[]{:S(2)}) collective-permute-start(bf16[80,128]{1,0:T(8,128)(2,1)S(1)} %get-tuple-element.39), channel_id=1, source_target_pairs={{0,3},{1,0},{2,1},{3,2},{4,7},{5,4},{6,5},{7,6},{8,11},{9,8},{10,9... | collective-permute-start | bytes 61448 | tf_op jit(solution)/shard_map/ppermute | solution.py:354
  84.5 3.3 %shard_map.137.refs_0_ = f32[64,64,128]{2,1,0:T(8,128)} custom-call(f32[8,2048]{1,0:T(8,128)S(1)} %shard_map.135.fields_ref, bf16[2048,128]{1,0:T(8,128)(2,1)S(1)} %bitcast.15), custom_call_target="tpu_custom_call" | custom-call | tf_op jit(solution)/shard_map/pallas_call | solution.py:32
  87.8 0.0 collective-permute-done.4.left_ref
  87.8 0.0 collective-permute-done.5.right_ref
  87.8 1.9 %collective-permute-start.6 = (bf16[64,128]{1,0:T(8,128)(2,1)S(1)}, bf16[64,128]{1,0:T(8,128)(2,1)S(1)}, u32[]{:S(2)}, u32[]{:S(2)}) collective-permute-start(bf16[64,128]{1,0:T(8,128)(2,1)S(1)} %get-tuple-element.46), channel_id=1, source_target_pairs={{0,4},{4,8},{8,12},{12,16},{16,20},{20,24},{24,28},{28,32},{32,36}... | collective-permute-start | bytes 49160 | tf_op jit(solution)/shard_map/ppermute | solution.py:354
  89.8 5.8 %collective-permute-start.7 = (bf16[64,128]{1,0:T(8,128)(2,1)S(1)}, bf16[64,128]{1,0:T(8,128)(2,1)S(1)}, u32[]{:S(2)}, u32[]{:S(2)}) collective-permute-start(bf16[64,128]{1,0:T(8,128)(2,1)S(1)} %get-tuple-element.47), channel_id=1, source_target_pairs={{4,0},{8,4},{12,8},{16,12},{20,16},{24,20},{28,24},{32,28},{36,32}... | collective-permute-start | bytes 49160 | tf_op jit(solution)/shard_map/ppermute | solution.py:354
  95.5 3.3 %shard_map.139.grad_ref = f32[64,64,128]{2,1,0:T(8,128)} custom-call(f32[8,2048]{1,0:T(8,128)S(1)} %shard_map.135.fields_ref, bf16[2048,128]{1,0:T(8,128)(2,1)S(1)} %bitcast.16, f32[64,64,128]{2,1,0:T(8,128)} %shard_map.137.refs_0_), custom_call_target="tpu_custom_call", output_to_operand_aliasing={{}: (2, {})} | custom-call | tf_op jit(solution)/shard_map/pallas_call | solution.py:32
  98.8 0.0 collective-permute-done.6.above_ref
  98.9 0.0 collective-permute-done.7.below_ref
  98.9 2.0 %shard_map.140 = f32[64,64,128]{2,1,0:T(8,128)} custom-call(bf16[80,128]{1,0:T(8,128)(2,1)S(1)} %collective-permute-done.4.left_ref, bf16[80,128]{1,0:T(8,128)(2,1)S(1)} %collective-permute-done.5.right_ref, bf16[64,128]{1,0:T(8,128)(2,1)S(1)} %collective-permute-done.6.above_ref, ...), custom_call_target="tpu_custom_call", output_to_operand_aliasing={{}: (4, {})} | custom-call | tf_op jit(solution)/shard_map/pallas_call | solution.py:32
  (1 shorter events, 0.0 us)
Async XLA Ops:
  3.1 39.8 %copy-start = (s32[1,1024]{1,0:T(1,128)S(1)}, s32[1,1024]{1,0:T(1,128)}, u32[]{:S(2)}) copy-start(s32[1,1024]{1,0:T(1,128)} %get-tuple-element.33.place_ref) | copy-start | bytes 12292
  3.1 23.7 %all-to-all-start = ((f32[128,2,128]{2,1,0:T(2,128)}), f32[128,2,128]{2,1,0:T(2,128)S(1)}, u32[]{:S(2)}, u32[]{:S(2)}) async-start(f32[128,2,128]{2,1,0:T(2,128)} %bitcast.26), calls=%async_computation | async-start | bytes 262144 | tf_op jit(solution)/shard_map/all_to_all | solution.py:358
  13.6 11.0 %collective-permute-start = (bf16[64,128]{1,0:T(8,128)(2,1)}, bf16[64,128]{1,0:T(8,128)(2,1)S(1)}, u32[]{:S(2)}, u32[]{:S(2)}) collective-permute-start(bf16[64,128]{1,0:T(8,128)(2,1)} %get-tuple-element.27), channel_id=1, source_target_pairs={{0,4},{4,8},{8,12},{12,16},{16,20},{20,24},{24,28},{28,32},{32,36}... | collective-permute-start | bytes 49160 | tf_op jit(solution)/shard_map/ppermute | solution.py:354
  15.7 9.0 %collective-permute-start.1 = (bf16[64,128]{1,0:T(8,128)(2,1)}, bf16[64,128]{1,0:T(8,128)(2,1)S(1)}, u32[]{:S(2)}, u32[]{:S(2)}) collective-permute-start(bf16[64,128]{1,0:T(8,128)(2,1)} %get-tuple-element.28), channel_id=1, source_target_pairs={{4,0},{8,4},{12,8},{16,12},{20,16},{24,20},{28,24},{32,28},{36,32}... | collective-permute-start | bytes 49160 | tf_op jit(solution)/shard_map/ppermute | solution.py:354
  21.3 5.2 %collective-permute-start.2 = (bf16[64,128]{1,0:T(8,128)(2,1)}, bf16[64,128]{1,0:T(8,128)(2,1)S(1)}, u32[]{:S(2)}, u32[]{:S(2)}) collective-permute-start(bf16[64,128]{1,0:T(8,128)(2,1)} %get-tuple-element.29), channel_id=1, source_target_pairs={{0,1},{1,2},{2,3},{3,0},{4,5},{5,6},{6,7},{7,4},{8,9},{9,10},{10,1... | collective-permute-start | bytes 49160 | tf_op jit(solution)/shard_map/ppermute | solution.py:354
  22.9 3.9 %collective-permute-start.3 = (bf16[64,128]{1,0:T(8,128)(2,1)}, bf16[64,128]{1,0:T(8,128)(2,1)S(1)}, u32[]{:S(2)}, u32[]{:S(2)}) collective-permute-start(bf16[64,128]{1,0:T(8,128)(2,1)} %get-tuple-element.30), channel_id=1, source_target_pairs={{0,3},{1,0},{2,1},{3,2},{4,7},{5,4},{6,5},{7,6},{8,11},{9,8},{10,9... | collective-permute-start | bytes 49160 | tf_op jit(solution)/shard_map/ppermute | solution.py:354
  35.4 19.8 %all-to-all-start.1 = ((bf16[128,16,128]{2,1,0:T(8,128)(2,1)}), bf16[128,16,128]{2,1,0:T(8,128)(2,1)S(1)}, u32[]{:S(2)}, u32[]{:S(2)}) async-start(bf16[128,16,128]{2,1,0:T(8,128)(2,1)} %bitcast.24), calls=%async_computation.1 | async-start | bytes 1048576 | tf_op jit(solution)/shard_map/all_to_all | solution.py:358
  42.9 12.2 %copy-start.1 = (f32[512]{0:T(512)S(1)}, f32[512]{0:T(512)}, u32[]{:S(2)}) copy-start(f32[512]{0:T(512)} %param.21) | copy-start | bytes 6148
  42.9 12.2 %copy-start.2 = (f32[256]{0:T(256)S(1)}, f32[256]{0:T(256)}, u32[]{:S(2)}) copy-start(f32[256]{0:T(256)} %param.19) | copy-start | bytes 3076
  43.0 12.2 %copy-start.3 = (f32[256]{0:T(256)S(1)}, f32[256]{0:T(256)}, u32[]{:S(2)}) copy-start(f32[256]{0:T(256)} %param.23) | copy-start | bytes 3076
  61.9 18.7 %all-to-all-start.2 = ((bf16[128,16,128]{2,1,0:T(8,128)(2,1)}), bf16[128,16,128]{2,1,0:T(8,128)(2,1)S(1)}, u32[]{:S(2)}, u32[]{:S(2)}) async-start(bf16[128,16,128]{2,1,0:T(8,128)(2,1)} %bitcast.25), calls=%async_computation.2 | async-start | bytes 1048576 | tf_op jit(solution)/shard_map/all_to_all | solution.py:358
  81.2 6.6 %collective-permute-start.4 = (bf16[80,128]{1,0:T(8,128)(2,1)S(1)}, bf16[80,128]{1,0:T(8,128)(2,1)S(1)}, u32[]{:S(2)}, u32[]{:S(2)}) collective-permute-start(bf16[80,128]{1,0:T(8,128)(2,1)S(1)} %get-tuple-element.38), channel_id=1, source_target_pairs={{0,1},{1,2},{2,3},{3,0},{4,5},{5,6},{6,7},{7,4},{8,9},{9,10},{10,1... | collective-permute-start | bytes 61448 | tf_op jit(solution)/shard_map/ppermute | solution.py:354
  81.8 6.0 %collective-permute-start.5 = (bf16[80,128]{1,0:T(8,128)(2,1)S(1)}, bf16[80,128]{1,0:T(8,128)(2,1)S(1)}, u32[]{:S(2)}, u32[]{:S(2)}) collective-permute-start(bf16[80,128]{1,0:T(8,128)(2,1)S(1)} %get-tuple-element.39), channel_id=1, source_target_pairs={{0,3},{1,0},{2,1},{3,2},{4,7},{5,4},{6,5},{7,6},{8,11},{9,8},{10,9... | collective-permute-start | bytes 61448 | tf_op jit(solution)/shard_map/ppermute | solution.py:354
  87.8 11.0 %collective-permute-start.6 = (bf16[64,128]{1,0:T(8,128)(2,1)S(1)}, bf16[64,128]{1,0:T(8,128)(2,1)S(1)}, u32[]{:S(2)}, u32[]{:S(2)}) collective-permute-start(bf16[64,128]{1,0:T(8,128)(2,1)S(1)} %get-tuple-element.46), channel_id=1, source_target_pairs={{0,4},{4,8},{8,12},{12,16},{16,20},{20,24},{24,28},{28,32},{32,36}... | collective-permute-start | bytes 49160 | tf_op jit(solution)/shard_map/ppermute | solution.py:354
  89.8 9.1 %collective-permute-start.7 = (bf16[64,128]{1,0:T(8,128)(2,1)S(1)}, bf16[64,128]{1,0:T(8,128)(2,1)S(1)}, u32[]{:S(2)}, u32[]{:S(2)}) collective-permute-start(bf16[64,128]{1,0:T(8,128)(2,1)S(1)} %get-tuple-element.47), channel_id=1, source_target_pairs={{4,0},{8,4},{12,8},{16,12},{20,16},{24,20},{28,24},{32,28},{36,32}... | collective-permute-start | bytes 49160 | tf_op jit(solution)/shard_map/ppermute | solution.py:354
